TPU v7x, 32 devices: a whole 2x2x4 slice. The times are simulated.
32 devices in a mesh: dom: 16 (over z, y, x), blk: 2 (over core).
Axes of the slice: x: 2, y: 2, z: 4, core: 2. Of those that a mesh axis runs over, the one named last changes fastest.
Arguments:
- pd_disp: float32 [64, 2, 128], P(('dom', 'blk')), may hold values from -4 to 4
- pd_vel: float32 [64, 2, 128], P(('dom', 'blk')), may hold values from -4 to 4
- pd_coord: float32 [64, 2, 128], P(('dom', 'blk')), may hold values from -4 to 4
- pd_modulus: float32 [64, 128], P(('dom', 'blk')), may hold values from 2 to 20
- pd_step: float32 [64, 128], P(('dom', 'blk')), may hold values from 0.03 to 0.3
- family_tile_lists: int32 [64, 3], P(('dom', 'blk')), may hold values from 0 to 11, as said below
- live_tiles: int32 [16], P('dom'), may hold values from 3 to 4, as said below
- patch_tile: int32 [32], P('dom'), may hold values from 0 to 3, as said below
- patch_blend: float32 [32, 128], P('dom'), may hold values from 0.1 to 0.9
- patch_nodes: int32 [32, 128], P(('dom', 'blk')), may hold values from 0 to 12799, as said below
- patch_matrix: float32 [32, 128, 128], P(('dom', 'blk')), may hold values from -0.5 to 0.5
- fe_disp: float32 [2, 204800], P(None, ('dom', 'blk')), may hold values from -4 to 4
- fe_vel: float32 [2, 204800], P(None, ('dom', 'blk')), may hold values from -4 to 4
- fe_step: float32 [204800], P(('dom', 'blk')), may hold values from 0.03 to 0.3
- fe_modulus: float32 [4096], P(('dom', 'blk')), may hold values from 0.5 to 2
- element_nodes: int32 [64, 4096], P(None, ('dom', 'blk')), may hold values from 0 to 12799, as said below
- shape_grad: float32 [2, 64, 64], replicated, may hold values from -0.75 to 0.75
- quad_weight: float32 [64], replicated, may hold values from 0.5 to 2
- shared_left: int32 [16, 113], P('dom'), may hold values from 0 to 12799, as said below
- shared_right: int32 [16, 113], P('dom'), may hold values from 0 to 12799, as said below
Outputs:
- pd_disp_out: float32 [64, 2, 128], P(('dom', 'blk'))
- pd_vel_out: float32 [64, 2, 128], P(('dom', 'blk'))
- fe_disp_out: float32 [2, 204800], P(None, ('dom', 'blk'))
- fe_vel_out: float32 [2, 204800], P(None, ('dom', 'blk'))
Inputs may be any that keep to these rules, and one draw needn't show every extreme that they name: Local tiles at index live_tiles[d] or above in subdomain d are padding: their inputs are ignored and their outputs are zero. `family_tile_lists`: each entry names a live tile by extended index; the first subdomain names no entry below 4, the last none at 8 or above. `patch_tile`: within a subdomain the 2 patch tiles are distinct live tiles. `patch_nodes`: node ids of a subdomain's patches are distinct and belong to its elements. `element_nodes`: local node ids of each element's subdomain. `shared_left`: row d lists distinct nodes; entry r is the same physical node as shared_right[d - 1, r]. `shared_right`: row d lists distinct nodes, none in shared_left[d].
All inputs are finite; a program needn't handle non-finite values.
Results may differ from a plain program's by a relative error of at most 0.0003.
Values sent between devices are 32-bit elements; how exact they have to be, the bound alone decides.
No kernel may reach another device: no remote copies, remote signals or barrier semaphores. Data moves between devices by JAX's collectives and lax.ppermute only.
A program may use at most 64 MiB of HBM per device.

v0:
```python
import jax
import jax.numpy as jnp
from jax import lax
from jax.sharding import PartitionSpec as P

time_step = 0.5
horizon_sq = 2.0
core_sq = 0.01
stretch_scale = 0.3


def with_halo(cells, sides, width):
    for axis, dim in sides:
        count = lax.axis_size(axis)
        ends = count - 1
        head = lax.slice_in_dim(cells, 0, width, axis=dim)
        tail = lax.slice_in_dim(cells, cells.shape[dim] - width, cells.shape[dim], axis=dim)
        cells = jnp.concatenate(
            [
                lax.ppermute(tail, axis, [(i, (i + 1) % count) for i in range(ends)]),
                cells,
                lax.ppermute(head, axis, [((i + 1) % count, i) for i in range(ends)]),
            ],
            axis=dim,
        )
    return cells


def bond_terms(x_own, u_own, x_far, u_far):
    offset = x_far[:, :, None, :] - x_own[None, :, :, None]
    deformed = offset + u_far[:, :, None, :] - u_own[None, :, :, None]
    rest_sq = jnp.sum(offset * offset, axis=1)
    rest_len = jnp.sqrt(rest_sq + core_sq)
    length = jnp.sqrt(jnp.sum(deformed * deformed, axis=1) + core_sq)
    stretch = length - rest_len
    ratio = stretch / stretch_scale
    influence = jnp.exp(-rest_sq / horizon_sq) / (1.0 + ratio * ratio)
    return (deformed, length, rest_len, stretch, influence)


def dilatation(x_own, u_own, x_far, u_far):
    deformed, length, rest_len, stretch, influence = bond_terms(x_own, u_own, x_far, u_far)
    point_volume = jnp.sum(influence * rest_len * rest_len, axis=(0, 2))
    volumetric_dilatation = (
        2.0 * jnp.sum(influence * rest_len * stretch, axis=(0, 2)) / point_volume
    )
    return (volumetric_dilatation, point_volume)


def bond_force(x_own, u_own, x_far, u_far, k_own, th_own, m_own, k_far, th_far, m_far):
    deformed, length, rest_len, stretch, influence = bond_terms(x_own, u_own, x_far, u_far)
    ko, to, mo = (k_own[None, :, None], th_own[None, :, None], m_own[None, :, None])
    kf, tf, mf = (k_far[:, None, :], th_far[:, None, :], m_far[:, None, :])
    t_own = influence * (
        2.0 * ko * to * rest_len / mo + 4.0 * ko * (stretch - 0.5 * to * rest_len) / mo
    )
    t_far = influence * (
        2.0 * kf * tf * rest_len / mf + 4.0 * kf * (stretch - 0.5 * tf * rest_len) / mf
    )
    scalar = (t_own + t_far) / length
    return jnp.sum(scalar[:, None] * deformed, axis=(0, 3))


def element_force(disp_el, modulus, shape_grad, quad_weight):
    precise = lax.Precision.HIGHEST
    grad = jnp.einsum("aqn,cne->caqe", shape_grad, disp_el, precision=precise)
    strain_xx = grad[0, 0]
    strain_yy = grad[1, 1]
    strain_xy = 0.5 * (grad[0, 1] + grad[1, 0])
    stiffen = 1.0 + strain_xx * strain_xx + strain_yy * strain_yy + 2.0 * strain_xy * strain_xy
    scaled = modulus[None, :] * quad_weight[:, None] * stiffen
    trace_sum = strain_xx + strain_yy
    s_xx = scaled * (trace_sum + 2.0 * strain_xx)
    s_yy = scaled * (trace_sum + 2.0 * strain_yy)
    s_xy = scaled * 2.0 * strain_xy
    stress = jnp.stack([jnp.stack([s_xx, s_xy]), jnp.stack([s_xy, s_yy])])
    return jnp.einsum("aqn,caqe->cne", shape_grad, stress, precision=precise)


def select_rows(wanted, first, count):
    slots = first + jnp.arange(count, dtype=jnp.int32)
    return (wanted[:, None] == slots[None, :]).astype(jnp.float32)


def blend_tiles(table, first, targets, patch_tile, patch_blend):
    precise = lax.Precision.HIGHEST
    choose = select_rows(patch_tile, first, table.shape[0])
    current = jnp.einsum("pk,kcn->pcn", choose, table, precision=precise)
    delta = patch_blend[:, None, :] * (targets - current)
    return table + jnp.einsum("pk,pcn->kcn", choose, delta, precision=precise)


def shards(
    pd_disp,
    pd_vel,
    pd_coord,
    pd_modulus,
    pd_step,
    family_tile_lists,
    live_tiles,
    patch_tile,
    patch_blend,
    patch_nodes,
    patch_matrix,
    fe_disp,
    fe_vel,
    fe_step,
    fe_modulus,
    element_nodes,
    shape_grad,
    quad_weight,
    shared_left,
    shared_right,
):
    precise = lax.Precision.HIGHEST
    blocks = lax.axis_size("blk")
    rank = lax.axis_index("blk")
    tiles_dev = pd_disp.shape[0]
    tiles_dom = tiles_dev * blocks
    patches_dev = patch_matrix.shape[0]
    active_flags = live_tiles[0]
    counter = jnp.arange(tiles_dev, dtype=jnp.int32)
    static_own = jnp.concatenate([pd_coord, pd_modulus[:, None, :]], axis=1)
    static_dom = lax.all_gather(static_own, "blk", axis=0, tiled=True)
    static_ext = with_halo(static_dom, (("dom", 0),), tiles_dom)
    coord_ext = static_ext[:, :2]
    modulus_ext = static_ext[:, 2]
    sorting_permutation = rank * tiles_dev + counter
    my_tiles = lax.dynamic_slice_in_dim(patch_tile, rank * patches_dev, patches_dev)
    my_blend = lax.dynamic_slice_in_dim(patch_blend, rank * patches_dev, patches_dev)
    alive = (rank * tiles_dev + counter < active_flags).astype(jnp.float32)[:, None, None]
    left_ids = shared_left[0]
    right_ids = shared_right[0]
    for section in range(2):
        fe_table = lax.all_gather(fe_disp, "blk", axis=1, tiled=True)
        picked = fe_table[:, patch_nodes]
        target = jnp.einsum("qpn,cqn->qcp", patch_matrix, picked, precision=precise)
        targets = lax.all_gather(target, "blk", axis=0, tiled=True)
        table = lax.all_gather(pd_disp, "blk", axis=0, tiled=True)
        blended = blend_tiles(table, 0, targets, patch_tile, patch_blend)
        disp_ext = with_halo(blended, (("dom", 0),), tiles_dom)
        own_blended = lax.dynamic_slice_in_dim(blended, rank * tiles_dev, tiles_dev)

        def dilatation_single_tile(packed_rows):
            tile_number, rows = packed_rows
            own = tiles_dom + tile_number

            def dilatation_run(discarded_output):
                volumetric_dilatation, point_volume = dilatation(
                    coord_ext[own], disp_ext[own], coord_ext[rows], disp_ext[rows]
                )
                return jnp.stack([volumetric_dilatation, point_volume])

            def dilatation_skip(discarded_output):
                return jnp.stack([jnp.zeros_like(modulus_ext[0]), jnp.ones_like(modulus_ext[0])])

            return lax.cond(tile_number < active_flags, dilatation_run, dilatation_skip, None)

        bond_state = lax.map(dilatation_single_tile, (sorting_permutation, family_tile_lists))
        state_dom = lax.all_gather(bond_state, "blk", axis=0, tiled=True)
        state_ext = with_halo(state_dom, (("dom", 0),), tiles_dom)

        def force_one(packed_rows):
            tile_number, rows = packed_rows
            own = tiles_dom + tile_number

            def force_run(discarded_output):
                return bond_force(
                    coord_ext[own],
                    disp_ext[own],
                    coord_ext[rows],
                    disp_ext[rows],
                    modulus_ext[own],
                    state_ext[own, 0],
                    state_ext[own, 1],
                    modulus_ext[rows],
                    state_ext[rows, 0],
                    state_ext[rows, 1],
                )

            def force_skip(discarded_output):
                return jnp.zeros_like(coord_ext[0])

            return lax.cond(tile_number < active_flags, force_run, force_skip, None)

        forces = lax.map(force_one, (sorting_permutation, family_tile_lists))
        forces_dom = lax.all_gather(forces, "blk", axis=0, tiled=True)
        own_force = lax.dynamic_slice_in_dim(forces_dom, rank * tiles_dev, tiles_dev)
        pd_vel = (pd_vel + pd_step[:, None, :] * own_force) * alive
        pd_disp = (own_blended + time_step * pd_vel) * alive
        choose = select_rows(my_tiles, 0, tiles_dom)
        patch_force = jnp.einsum("qk,kcn->qcn", choose, forces_dom, precision=precise)
        weighted = patch_force * my_blend[:, None, :]
        reaction = jnp.einsum("qpn,qcp->cqn", patch_matrix, weighted, precision=precise)
        disp_el = fe_table[:, element_nodes]
        forces_el = element_force(disp_el, fe_modulus, shape_grad, quad_weight)
        nodal = (
            jnp.zeros(fe_table.shape, jnp.float32)
            .at[:, element_nodes.reshape(-1)]
            .add(forces_el.reshape(2, -1))
        )
        nodal = -nodal
        nodal = nodal.at[:, patch_nodes.reshape(-1)].add(reaction.reshape(2, -1))
        sides = jnp.stack([nodal[:, left_ids], nodal[:, right_ids]])
        border = with_halo(sides, (("dom", 0),), 1)
        nodal = nodal.at[:, left_ids].add(border[0]).at[:, right_ids].add(border[3])
        total = lax.psum_scatter(nodal, "blk", scatter_dimension=1, tiled=True)
        fe_vel = fe_vel + fe_step[None, :] * total
        fe_disp = fe_disp + time_step * fe_vel
    return (pd_disp, pd_vel, fe_disp, fe_vel)


def solution(mesh):
    return jax.shard_map(
        shards,
        mesh=mesh,
        in_specs=(
            P(("dom", "blk"), None, None),
            P(("dom", "blk"), None, None),
            P(("dom", "blk"), None, None),
            P(("dom", "blk"), None),
            P(("dom", "blk"), None),
            P(("dom", "blk"), None),
            P("dom"),
            P("dom"),
            P("dom", None),
            P(("dom", "blk"), None),
            P(("dom", "blk"), None, None),
            P(None, ("dom", "blk")),
            P(None, ("dom", "blk")),
            P(("dom", "blk")),
            P(("dom", "blk")),
            P(None, ("dom", "blk")),
            P(),
            P(),
            P("dom", None),
            P("dom", None),
        ),
        out_specs=(
            P(("dom", "blk"), None, None),
            P(("dom", "blk"), None, None),
            P(None, ("dom", "blk")),
            P(None, ("dom", "blk")),
        ),
        check_vma=False,
    )
```

profile of v0, /device:TPU:0, one launch (start us, length us, event | category | flops | bytes accessed | tf_op | source)
XLA Modules:
  0.0 422.8 jit_solution(17404575114632485086)
XLA Ops:
  9.9 4.7 %collective-permute-start = (f32[4,3,128]{2,1,0:T(4,128)S(1)}, f32[4,3,128]{2,1,0:T(4,128)S(1)}, u32[]{:S(2)}, u32[]{:S(2)}) collective-permute-start(f32[4,3,128]{2,1,0:T(4,128)S(1)} %all_gather.36), channel_id=1, source_target_pairs={{0,2},{2,4},{4,6},{6,8},{8,10},{10,12},{12,14},{14,16},{16,18},{18... | collective-permute-start | bytes 18440 | tf_op jit(solution)/shard_map/ppermute | solution.py:20
  19.9 6.8 %all_gather.34 = f32[2,12800]{0,1:T(8,128)} all-gather(f32[2,6400]{0,1:T(8,128)S(1)} %copy.148), channel_id=1, replica_groups=mesh['dom'=16,'blk'=2] {'blk'}, dimensions={1}, use_global_device_ids=true | all-gather | bytes 153600 | tf_op jit(solution)/shard_map/all_gather | solution.py:135
  26.6 3.5 gather_fusion.14
  33.9 5.2 %collective-permute-start.2 = (f32[4,2,128]{2,0,1:T(4,128)S(1)}, f32[4,2,128]{2,0,1:T(4,128)S(1)}, u32[]{:S(2)}, u32[]{:S(2)}) collective-permute-start(f32[4,2,128]{2,0,1:T(4,128)S(1)} %convolution_add_fusion.1), channel_id=1, source_target_pairs={{0,2},{2,4},{4,6},{6,8},{8,10},{10,12},{12,14},{14,16},{16,18},{18... | collective-permute-start | bytes 12296 | tf_op jit(solution)/shard_map/ppermute | solution.py:20
  39.2 30.6 %gather_fusion.15 = f32[8192,2]{1,0:T(8,128)} fusion(f32[2,12800]{0,1:T(8,128)} %all_gather.34, s32[8192]{0:T(1024)S(1)} %fusion.75), kind=kCustom, calls=%fused_computation.15 | custom fusion | bytes 163840 | tf_op jit(solution)/shard_map/gather | solution.py:195
  73.6 9.8 %while.40 = (s32[]{:T(128)}, f32[2,2,128]{2,1,0:T(2,128)S(1)}, s32[2]{0:T(128)S(1)}, s32[]{:T(128)}, s32[2,3]{1,0:T(2,128)S(1)}, /*index=5*/f32[12,2,128]{2,1,0:T(2,128)S(1)}, f32[12,2,128]{2,1,0:T(2,128)S(1)}, s32[]{:T(128)}) while((s32[]{:T(128)}, f32[2,2,128]{2,1,0:T(2,128)S(1)}, s32[2]{0:T(128)S(1)}, s32[]{:T(128)}, s32[2,3]{1,0:T(2,128)S(1)}, ...), condition=%wide.region_7.8_spmd, body=%wide.region_0.7_spmd.sunk | while | flops 1279249 | bytes 822045 | solution.py:159
  86.5 5.5 %collective-permute-start.4 = (f32[4,2,128]{2,1,0:T(2,128)S(1)}, f32[4,2,128]{2,1,0:T(2,128)S(1)}, u32[]{:S(2)}, u32[]{:S(2)}) collective-permute-start(f32[4,2,128]{2,1,0:T(2,128)S(1)} %all_gather.37), channel_id=1, source_target_pairs={{0,2},{2,4},{4,6},{6,8},{8,10},{10,12},{12,14},{14,16},{16,18},{18... | collective-permute-start | bytes 12296 | tf_op jit(solution)/shard_map/ppermute | solution.py:20
  95.8 47.4 %scatter_custom_fusion = f32[2,12800]{0,1:T(8,128)} fusion(s32[8192]{0:T(1024)S(1)} %bitcast.304, f32[8192,2]{1,0:T(8,128)} %bitcast.295, f32[]{:T(128)} %constant.284.clone.1), kind=kCustom, calls=%fused_computation.146 | custom fusion | flops 16384 | bytes 102912 | tf_op jit(solution)/shard_map/scatter-add | solution.py:200
  143.2 4.9 %neg.34 = f32[2,12800]{0,1:T(8,128)} negate(f32[2,12800]{0,1:T(8,128)} %scatter_custom_fusion) | non-fusion elementwise | flops 25600 | bytes 204800 | tf_op jit(solution)/shard_map/neg | solution.py:202
  148.1 14.0 %while.41 = (s32[]{:T(128)}, f32[2,2,128]{2,1,0:T(2,128)S(1)}, s32[2]{0:T(128)S(1)}, s32[]{:T(128)}, s32[2,3]{1,0:T(2,128)S(1)}, /*index=5*/f32[12,2,128]{2,1,0:...) while((s32[]{:T(128)}, f32[2,2,128]{2,1,0:T(2,128)S(1)}, ...), condition=%wide.region_14.15_spmd, body=%wide.region_8.14_spmd.sunk | while | flops 2362144 | bytes 1249193 | solution.py:186
  150.0 5.1 %conditional.9 = (f32[1,2,128]{2,1,0:T(2,128)S(1)}) conditional(s32[]{:T(128)} %convert_element_type.30, () %tuple.177, (s32[2,3]{1,0:T(2,128)S(1)}, s32[]{:T(128)}, f32[12,2,128]{2,1,0:T(2,128)S(1)}, s32[]{:T(128)}, f32[12,2,128]{2,1,0:T(2,128)S(1)}, /*index=5*/f32[12,128]{1,0:T(8,128)S(1)}, f32[12,2,128]{2,1,0:T(2,128)S(1)}) %tuple.178), branch_computations={%region_9.9_spmd, %region_10.13_spmd} | conditional | flops 2362140 | bytes 1246950 | solution.py:184
  157.0 5.1 %conditional.9 = (f32[1,2,128]{2,1,0:T(2,128)S(1)}) conditional(s32[]{:T(128)} %convert_element_type.30, () %tuple.177, (s32[2,3]{1,0:T(2,128)S(1)}, s32[]{:T(128)}, f32[12,2,128]{2,1,0:T(2,128)S(1)}, s32[]{:T(128)}, f32[12,2,128]{2,1,0:T(2,128)S(1)}, /*index=5*/f32[12,128]{1,0:T(8,128)S(1)}, f32[12,2,128]{2,1,0:T(2,128)S(1)}) %tuple.178), branch_computations={%region_9.9_spmd, %region_10.13_spmd} | conditional | flops 2362140 | bytes 1246950 | solution.py:184
  165.0 6.7 %scatter_fusion = f32[2,12800]{0,1:T(8,128)} fusion(f32[2,12800]{0,1:T(8,128)} %neg.34, s32[128]{0:T(128)S(1)} %fusion.97, f32[128,2]{1,0:T(8,128)S(1)} %copy.160), kind=kCustom, calls=%fused_computation.23 | custom fusion | flops 256 | bytes 3584 | tf_op jit(solution)/shard_map/scatter-add | solution.py:203
  178.8 4.8 %collective-permute-start.6 = (f32[1,2,113]{1,2,0:T(8,128)S(1)}, f32[1,2,113]{1,2,0:T(8,128)S(1)}, u32[]{:S(2)}, u32[]{:S(2)}) collective-permute-start(f32[1,2,113]{1,2,0:T(8,128)S(1)} %bitcast.313), channel_id=1, source_target_pairs={{0,2},{2,4},{4,6},{6,8},{8,10},{10,12},{12,14},{14,16},{16,18},{18... | collective-permute-start | bytes 2720 | tf_op jit(solution)/shard_map/ppermute | solution.py:20
  185.4 6.7 %scatter_custom_fusion.2 = f32[2,12800]{0,1:T(8,128)} fusion(f32[2,12800]{0,1:T(8,128)} %scatter_fusion, s32[113]{0:T(128)S(1)} %fusion.98, f32[1,2,113]{1,2,0:T(8,128)S(1)} %collective-permute-done.6), kind=kCustom, calls=%fused_computation.190 | custom fusion | flops 226 | bytes 163840 | tf_op jit(solution)/shard_map/scatter-add | solution.py:206
  192.1 6.7 %scatter_custom_fusion.3 = f32[2,12800]{0,1:T(8,128)} fusion(f32[2,12800]{0,1:T(8,128)} %scatter_custom_fusion.2, s32[113]{0:T(128)S(1)} %fusion.99, f32[1,2,113]{1,2,0:T(8,128)S(1)} %collective-permute-done.7), kind=kCustom, calls=%fused_computation.188 | custom fusion | flops 226 | bytes 163840 | tf_op jit(solution)/shard_map/scatter-add | solution.py:206
  200.8 15.4 %reduce-scatter.7.cloned.1.call-done = f32[6400,2]{1,0:T(8,128)} async-done(((f32[12800,2]{1,0:T(8,128)}), f32[6400,2]{1,0:T(8,128)}) %reduce-scatter.7.cloned.1.call-update) | async-done | bytes 51216
  221.4 4.2 copy.162
  232.9 4.5 %collective-permute-start.8 = (f32[4,2,128]{2,0,1:T(4,128)S(1)}, f32[4,2,128]{2,0,1:T(4,128)S(1)}, u32[]{:S(2)}, u32[]{:S(2)}) collective-permute-start(f32[4,2,128]{2,0,1:T(4,128)S(1)} %convolution_add_fusion), channel_id=1, source_target_pairs={{0,2},{2,4},{4,6},{6,8},{8,10},{10,12},{12,14},{14,16},{16,18},{18... | collective-permute-start | bytes 12296 | tf_op jit(solution)/shard_map/ppermute | solution.py:20
  237.5 30.6 %gather_fusion.19 = f32[8192,2]{1,0:T(8,128)} fusion(f32[2,12800]{0,1:T(8,128)} %copy.162, s32[8192]{0:T(1024)S(1)} %fusion.75), kind=kCustom, calls=%fused_computation.19 | custom fusion | bytes 163840 | tf_op jit(solution)/shard_map/gather | solution.py:195
  271.4 9.7 %while.42 = (s32[]{:T(128)}, f32[2,2,128]{2,1,0:T(2,128)S(1)}, s32[2]{0:T(128)S(1)}, s32[]{:T(128)}, s32[2,3]{1,0:T(2,128)S(1)}, /*index=5*/f32[12,2,128]{2,1,0:T(2,128)S(1)}, f32[12,2,128]{2,1,0:T(2,128)S(1)}, s32[]{:T(128)}) while((s32[]{:T(128)}, f32[2,2,128]{2,1,0:T(2,128)S(1)}, s32[2]{0:T(128)S(1)}, s32[]{:T(128)}, ...), condition=%wide.region_27.28_spmd, body=%wide.region_20.27_spmd.sunk | while | flops 1279249 | bytes 822045 | solution.py:159
  284.4 5.3 %collective-permute-start.10 = (f32[4,2,128]{2,1,0:T(2,128)S(1)}, f32[4,2,128]{2,1,0:T(2,128)S(1)}, u32[]{:S(2)}, u32[]{:S(2)}) collective-permute-start(f32[4,2,128]{2,1,0:T(2,128)S(1)} %all_gather.42), channel_id=1, source_target_pairs={{0,2},{2,4},{4,6},{6,8},{8,10},{10,12},{12,14},{14,16},{16,18},{18... | collective-permute-start | bytes 12296 | tf_op jit(solution)/shard_map/ppermute | solution.py:20
  292.6 47.4 %scatter_custom_fusion.4 = f32[2,12800]{0,1:T(8,128)} fusion(s32[8192]{0:T(1024)S(1)} %bitcast.305, f32[8192,2]{1,0:T(8,128)} %bitcast.294, f32[]{:T(128)} %constant.284.clone.1), kind=kCustom, calls=%fused_computation.144 | custom fusion | flops 16384 | bytes 102912 | tf_op jit(solution)/shard_map/scatter-add | solution.py:200
  340.0 4.9 %neg.35 = f32[2,12800]{0,1:T(8,128)} negate(f32[2,12800]{0,1:T(8,128)} %scatter_custom_fusion.4) | non-fusion elementwise | flops 25600 | bytes 204800 | tf_op jit(solution)/shard_map/neg | solution.py:202
  344.9 14.0 %while.43 = (s32[]{:T(128)}, f32[2,2,128]{2,1,0:T(2,128)S(1)}, s32[2]{0:T(128)S(1)}, s32[]{:T(128)}, s32[2,3]{1,0:T(2,128)S(1)}, /*index=5*/f32[12,2,128]{2,1,0:...) while((s32[]{:T(128)}, f32[2,2,128]{2,1,0:T(2,128)S(1)}, ...), condition=%wide.region_34.35_spmd, body=%wide.region_28.34_spmd.sunk | while | flops 2362144 | bytes 1249193 | solution.py:186
  346.8 5.1 %conditional.11 = (f32[1,2,128]{2,1,0:T(2,128)S(1)}) conditional(s32[]{:T(128)} %convert_element_type.32, () %tuple.183, (s32[2,3]{1,0:T(2,128)S(1)}, s32[]{:T(128)}, f32[12,2,128]{2,1,0:T(2,128)S(1)}, s32[]{:T(128)}, f32[12,2,128]{2,1,0:T(2,128)S(1)}, /*index=5*/f32[12,128]{1,0:T(8,128)S(1)}, f32[12,2,128]{2,1,0:T(2,128)S(1)}) %tuple.184), branch_computations={%region_29.29_spmd, %region_30.33_spmd} | conditional | flops 2362140 | bytes 1246950 | solution.py:184
  353.8 5.1 %conditional.11 = (f32[1,2,128]{2,1,0:T(2,128)S(1)}) conditional(s32[]{:T(128)} %convert_element_type.32, () %tuple.183, (s32[2,3]{1,0:T(2,128)S(1)}, s32[]{:T(128)}, f32[12,2,128]{2,1,0:T(2,128)S(1)}, s32[]{:T(128)}, f32[12,2,128]{2,1,0:T(2,128)S(1)}, /*index=5*/f32[12,128]{1,0:T(8,128)S(1)}, f32[12,2,128]{2,1,0:T(2,128)S(1)}) %tuple.184), branch_computations={%region_29.29_spmd, %region_30.33_spmd} | conditional | flops 2362140 | bytes 1246950 | solution.py:184
  361.8 6.7 %scatter_fusion.1 = f32[2,12800]{0,1:T(8,128)} fusion(f32[2,12800]{0,1:T(8,128)} %neg.35, s32[128]{0:T(128)S(1)} %fusion.97, f32[128,2]{1,0:T(8,128)S(1)} %copy.173), kind=kCustom, calls=%fused_computation.27 | custom fusion | flops 256 | bytes 3584 | tf_op jit(solution)/shard_map/scatter-add | solution.py:203
  375.6 4.8 %collective-permute-start.12 = (f32[1,2,113]{1,2,0:T(8,128)S(1)}, f32[1,2,113]{1,2,0:T(8,128)S(1)}, u32[]{:S(2)}, u32[]{:S(2)}) collective-permute-start(f32[1,2,113]{1,2,0:T(8,128)S(1)} %bitcast.314), channel_id=1, source_target_pairs={{0,2},{2,4},{4,6},{6,8},{8,10},{10,12},{12,14},{14,16},{16,18},{18... | collective-permute-start | bytes 2720 | tf_op jit(solution)/shard_map/ppermute | solution.py:20
  382.3 6.7 %scatter_custom_fusion.6 = f32[2,12800]{0,1:T(8,128)} fusion(f32[2,12800]{0,1:T(8,128)} %scatter_fusion.1, s32[113]{0:T(128)S(1)} %fusion.98, f32[1,2,113]{1,2,0:T(8,128)S(1)} %collective-permute-done.12), kind=kCustom, calls=%fused_computation.186 | custom fusion | flops 226 | bytes 163840 | tf_op jit(solution)/shard_map/scatter-add | solution.py:206
  388.9 6.7 %scatter_custom_fusion.7 = f32[2,12800]{0,1:T(8,128)} fusion(f32[2,12800]{0,1:T(8,128)} %scatter_custom_fusion.6, s32[113]{0:T(128)S(1)} %fusion.99, f32[1,2,113]{1,2,0:T(8,128)S(1)} %collective-permute-done.13), kind=kCustom, calls=%fused_computation.184 | custom fusion | flops 226 | bytes 163840 | tf_op jit(solution)/shard_map/scatter-add | solution.py:206
  396.9 15.9 %reduce-scatter.9.cloned.1.call-done = f32[6400,2]{1,0:T(8,128)} async-done(((f32[12800,2]{1,0:T(8,128)}), f32[6400,2]{1,0:T(8,128)}) %reduce-scatter.9.cloned.1.call-update) | async-done | bytes 51216
  (259 shorter events, 111.3 us)
Async XLA Ops:
  7.2 65.5 %copy-start = (f32[2,64,64]{2,1,0:T(8,128)S(1)}, f32[2,64,64]{2,1,0:T(8,128)}, u32[]{:S(2)}) copy-start(f32[2,64,64]{2,1,0:T(8,128)} %param.52) | copy-start | bytes 98308
  7.2 209.0 %reduce-scatter.7.cloned.1.call-start = ((), (), s32[]{:S(2)}) async-start(), calls=%async_computation.2 | async-start | bytes 9830400
  9.9 63.6 %collective-permute-start = (f32[4,3,128]{2,1,0:T(4,128)S(1)}, f32[4,3,128]{2,1,0:T(4,128)S(1)}, u32[]{:S(2)}, u32[]{:S(2)}) collective-permute-start(f32[4,3,128]{2,1,0:T(4,128)S(1)} %all_gather.36), channel_id=1, source_target_pairs={{0,2},{2,4},{4,6},{6,8},{8,10},{10,12},{12,14},{14,16},{16,18},{18... | collective-permute-start | bytes 18440 | tf_op jit(solution)/shard_map/ppermute | solution.py:20
  14.6 58.9 %collective-permute-start.1 = (f32[4,3,128]{2,1,0:T(4,128)S(1)}, f32[4,3,128]{2,1,0:T(4,128)S(1)}, u32[]{:S(2)}, u32[]{:S(2)}) collective-permute-start(f32[4,3,128]{2,1,0:T(4,128)S(1)} %all_gather.36), channel_id=1, source_target_pairs={{2,0},{4,2},{6,4},{8,6},{10,8},{12,10},{14,12},{16,14},{18,16},{20... | collective-permute-start | bytes 18440 | tf_op jit(solution)/shard_map/ppermute | solution.py:22
  17.9 8.7 %copy-start.12 = (s32[1,128]{1,0:T(1,128)S(1)}, s32[1,128]{1,0:T(1,128)}, u32[]{:S(2)}) copy-start(s32[1,128]{1,0:T(1,128)} %param.45) | copy-start | bytes 1540
  17.9 12.2 %copy-start.1 = (f32[1,128,128]{2,1,0:T(8,128)S(1)}, f32[1,128,128]{2,1,0:T(8,128)}, u32[]{:S(2)}) copy-start(f32[1,128,128]{2,1,0:T(8,128)} %param.46) | copy-start | bytes 196612
  17.9 14.3 %copy-start.11 = (f32[2,128]{1,0:T(2,128)S(1)}, f32[2,128]{1,0:T(2,128)}, u32[]{:S(2)}) copy-start(f32[2,128]{1,0:T(2,128)} %param.44) | copy-start | bytes 3076
  17.9 14.3 %copy-start.15 = (s32[2]{0:T(128)S(1)}, s32[2]{0:T(128)}, u32[]{:S(2)}) copy-start(s32[2]{0:T(128)} %param.43) | copy-start | bytes 28
  17.9 21.2 %copy-start.4 = (s32[64,128]{1,0:T(8,128)S(1)}, s32[64,128]{1,0:T(8,128)}, u32[]{:S(2)}) copy-start(s32[64,128]{1,0:T(8,128)} %param.51) | copy-start | bytes 98308
  19.8 53.1 %copy-start.9 = (f32[64]{0:T(128)S(1)}, f32[64]{0:T(128)}, u32[]{:S(2)}) copy-start(f32[64]{0:T(128)} %param.53) | copy-start | bytes 772
  19.8 53.1 %copy-start.10 = (f32[128]{0:T(128)S(1)}, f32[128]{0:T(128)}, u32[]{:S(2)}) copy-start(f32[128]{0:T(128)} %param.50) | copy-start | bytes 1540
  19.8 53.2 %copy-start.13 = (s32[1,113]{1,0:T(1,128)S(1)}, s32[1,113]{1,0:T(1,128)}, u32[]{:S(2)}) copy-start(s32[1,113]{1,0:T(1,128)} %param.54) | copy-start | bytes 1360
  19.8 53.3 %copy-start.14 = (s32[1,113]{1,0:T(1,128)S(1)}, s32[1,113]{1,0:T(1,128)}, u32[]{:S(2)}) copy-start(s32[1,113]{1,0:T(1,128)} %param.55) | copy-start | bytes 1360
  19.8 53.7 %copy-start.6 = (s32[2,3]{1,0:T(2,128)S(1)}, s32[2,3]{1,0:T(2,128)}, u32[]{:S(2)}) copy-start(s32[2,3]{1,0:T(2,128)} %param.41) | copy-start | bytes 76
  32.6 40.8 %collective-permute-start.3 = (f32[4,2,128]{2,0,1:T(4,128)S(1)}, f32[4,2,128]{2,0,1:T(4,128)S(1)}, u32[]{:S(2)}, u32[]{:S(2)}) collective-permute-start(f32[4,2,128]{2,0,1:T(4,128)S(1)} %convolution_add_fusion.1), channel_id=1, source_target_pairs={{2,0},{4,2},{6,4},{8,6},{10,8},{12,10},{14,12},{16,14},{18,16},{20... | collective-permute-start | bytes 12296 | tf_op jit(solution)/shard_map/ppermute | solution.py:22
  33.9 39.5 %collective-permute-start.2 = (f32[4,2,128]{2,0,1:T(4,128)S(1)}, f32[4,2,128]{2,0,1:T(4,128)S(1)}, u32[]{:S(2)}, u32[]{:S(2)}) collective-permute-start(f32[4,2,128]{2,0,1:T(4,128)S(1)} %convolution_add_fusion.1), channel_id=1, source_target_pairs={{0,2},{2,4},{4,6},{6,8},{8,10},{10,12},{12,14},{14,16},{16,18},{18... | collective-permute-start | bytes 12296 | tf_op jit(solution)/shard_map/ppermute | solution.py:20
  85.2 62.9 %collective-permute-start.5 = (f32[4,2,128]{2,1,0:T(2,128)S(1)}, f32[4,2,128]{2,1,0:T(2,128)S(1)}, u32[]{:S(2)}, u32[]{:S(2)}) collective-permute-start(f32[4,2,128]{2,1,0:T(2,128)S(1)} %all_gather.37), channel_id=1, source_target_pairs={{2,0},{4,2},{6,4},{8,6},{10,8},{12,10},{14,12},{16,14},{18,16},{20... | collective-permute-start | bytes 12296 | tf_op jit(solution)/shard_map/ppermute | solution.py:22
  86.5 61.6 %collective-permute-start.4 = (f32[4,2,128]{2,1,0:T(2,128)S(1)}, f32[4,2,128]{2,1,0:T(2,128)S(1)}, u32[]{:S(2)}, u32[]{:S(2)}) collective-permute-start(f32[4,2,128]{2,1,0:T(2,128)S(1)} %all_gather.37), channel_id=1, source_target_pairs={{0,2},{2,4},{4,6},{6,8},{8,10},{10,12},{12,14},{14,16},{16,18},{18... | collective-permute-start | bytes 12296 | tf_op jit(solution)/shard_map/ppermute | solution.py:20
  178.8 6.7 %collective-permute-start.6 = (f32[1,2,113]{1,2,0:T(8,128)S(1)}, f32[1,2,113]{1,2,0:T(8,128)S(1)}, u32[]{:S(2)}, u32[]{:S(2)}) collective-permute-start(f32[1,2,113]{1,2,0:T(8,128)S(1)} %bitcast.313), channel_id=1, source_target_pairs={{0,2},{2,4},{4,6},{6,8},{8,10},{10,12},{12,14},{14,16},{16,18},{18... | collective-permute-start | bytes 2720 | tf_op jit(solution)/shard_map/ppermute | solution.py:20
  183.6 8.5 %collective-permute-start.7 = (f32[1,2,113]{1,2,0:T(8,128)S(1)}, f32[1,2,113]{1,2,0:T(8,128)S(1)}, u32[]{:S(2)}, u32[]{:S(2)}) collective-permute-start(f32[1,2,113]{1,2,0:T(8,128)S(1)} %bitcast.311), channel_id=1, source_target_pairs={{2,0},{4,2},{6,4},{8,6},{10,8},{12,10},{14,12},{16,14},{18,16},{20... | collective-permute-start | bytes 2720 | tf_op jit(solution)/shard_map/ppermute | solution.py:22
  192.1 6.8 %copy-start.7 = (f32[2,2,128]{2,1,0:T(2,128)S(1)}, f32[2,2,128]{2,1,0:T(2,128)}, u32[]{:S(2)}) copy-start(f32[2,2,128]{2,1,0:T(2,128)} %param.37) | copy-start | bytes 6148
  192.1 6.8 %copy-start.8 = (f32[2,128]{1,0:T(2,128)S(1)}, f32[2,128]{1,0:T(2,128)}, u32[]{:S(2)}) copy-start(f32[2,128]{1,0:T(2,128)} %param.40) | copy-start | bytes 3076
  198.8 19.8 %copy-start.2 = (f32[2,6400]{1,0:T(2,128)S(1)}, f32[2,6400]{1,0:T(2,128)}, u32[]{:S(2)}) copy-start(f32[2,6400]{1,0:T(2,128)} %param.48) | copy-start | bytes 153604
  198.8 19.8 %copy-start.3 = (f32[2,6400]{1,0:T(2,128)S(1)}, f32[2,6400]{1,0:T(2,128)}, u32[]{:S(2)}) copy-start(f32[2,6400]{1,0:T(2,128)} %param.47) | copy-start | bytes 153604
  198.8 19.8 %copy-start.5 = (f32[6400]{0:T(1024)S(1)}, f32[6400]{0:T(1024)}, u32[]{:S(2)}) copy-start(f32[6400]{0:T(1024)} %param.49) | copy-start | bytes 76804
  198.8 213.9 %reduce-scatter.9.cloned.1.call-start = ((), (), s32[]{:S(2)}) async-start(), calls=%async_computation.3 | async-start | bytes 9830400
  231.6 39.7 %collective-permute-start.9 = (f32[4,2,128]{2,0,1:T(4,128)S(1)}, f32[4,2,128]{2,0,1:T(4,128)S(1)}, u32[]{:S(2)}, u32[]{:S(2)}) collective-permute-start(f32[4,2,128]{2,0,1:T(4,128)S(1)} %convolution_add_fusion), channel_id=1, source_target_pairs={{2,0},{4,2},{6,4},{8,6},{10,8},{12,10},{14,12},{16,14},{18,16},{20... | collective-permute-start | bytes 12296 | tf_op jit(solution)/shard_map/ppermute | solution.py:22
  232.9 38.4 %collective-permute-start.8 = (f32[4,2,128]{2,0,1:T(4,128)S(1)}, f32[4,2,128]{2,0,1:T(4,128)S(1)}, u32[]{:S(2)}, u32[]{:S(2)}) collective-permute-start(f32[4,2,128]{2,0,1:T(4,128)S(1)} %convolution_add_fusion), channel_id=1, source_target_pairs={{0,2},{2,4},{4,6},{6,8},{8,10},{10,12},{12,14},{14,16},{16,18},{18... | collective-permute-start | bytes 12296 | tf_op jit(solution)/shard_map/ppermute | solution.py:20
  283.0 62.0 %collective-permute-start.11 = (f32[4,2,128]{2,1,0:T(2,128)S(1)}, f32[4,2,128]{2,1,0:T(2,128)S(1)}, u32[]{:S(2)}, u32[]{:S(2)}) collective-permute-start(f32[4,2,128]{2,1,0:T(2,128)S(1)} %all_gather.42), channel_id=1, source_target_pairs={{2,0},{4,2},{6,4},{8,6},{10,8},{12,10},{14,12},{16,14},{18,16},{20... | collective-permute-start | bytes 12296 | tf_op jit(solution)/shard_map/ppermute | solution.py:22
  284.4 60.5 %collective-permute-start.10 = (f32[4,2,128]{2,1,0:T(2,128)S(1)}, f32[4,2,128]{2,1,0:T(2,128)S(1)}, u32[]{:S(2)}, u32[]{:S(2)}) collective-permute-start(f32[4,2,128]{2,1,0:T(2,128)S(1)} %all_gather.42), channel_id=1, source_target_pairs={{0,2},{2,4},{4,6},{6,8},{8,10},{10,12},{12,14},{14,16},{16,18},{18... | collective-permute-start | bytes 12296 | tf_op jit(solution)/shard_map/ppermute | solution.py:20
  375.6 6.7 %collective-permute-start.12 = (f32[1,2,113]{1,2,0:T(8,128)S(1)}, f32[1,2,113]{1,2,0:T(8,128)S(1)}, u32[]{:S(2)}, u32[]{:S(2)}) collective-permute-start(f32[1,2,113]{1,2,0:T(8,128)S(1)} %bitcast.314), channel_id=1, source_target_pairs={{0,2},{2,4},{4,6},{6,8},{8,10},{10,12},{12,14},{14,16},{16,18},{18... | collective-permute-start | bytes 2720 | tf_op jit(solution)/shard_map/ppermute | solution.py:20
  380.4 8.5 %collective-permute-start.13 = (f32[1,2,113]{1,2,0:T(8,128)S(1)}, f32[1,2,113]{1,2,0:T(8,128)S(1)}, u32[]{:S(2)}, u32[]{:S(2)}) collective-permute-start(f32[1,2,113]{1,2,0:T(8,128)S(1)} %bitcast.312), channel_id=1, source_target_pairs={{2,0},{4,2},{6,4},{8,6},{10,8},{12,10},{14,12},{16,14},{18,16},{20... | collective-permute-start | bytes 2720 | tf_op jit(solution)/shard_map/ppermute | solution.py:22
Sparse Core Ops, SparseCore 0:
  199.0 17.1 reduce-scatter.6
  395.8 16.9 reduce-scatter.8
where the time goes:
time: 425 us; the launch traced here: 423 us
  other arithmetic  152 us (36%)
  local copies, waits for them, and re-layouts  127 us (30%)
  starting transfers between devices  44.1 us (10%)
  waiting for transfers between devices  32.4 us (8%)
  blocking collectives  26.3 us (6%)
  loops' own time  21.4 us (5%)
  between operations  15.4 us (4%)
    scatter-add x2, other arithmetic, shards(): nodal = jnp.zeros(fe_table.shape, jnp.float32).at[:, element_nodes.reshap...  94.8 us
    gather x4, local copies, waits for them, and re-layouts, shards(): disp_el = fe_table[:, element_nodes]  66.9 us
    ppermute x7, starting transfers between devices, with_halo(): lax.ppermute(tail, axis, [(i, (i + 1) % count) for i in range(ends)])  34.8 us
    unnamed x4, waiting for transfers between devices  31.3 us
    scatter-add x4, other arithmetic, shards(): nodal = nodal.at[:, left_ids].add(border[0]).at[:, right_ids].add(border[3])  26.7 us
    gather x4, local copies, waits for them, and re-layouts, shards(): sides = jnp.stack([nodal[:, left_ids], nodal[:, right_ids]])  14 us
    scatter-add x2, other arithmetic, shards(): nodal = nodal.at[:, patch_nodes.reshape(-1)].add(reaction.reshape(2, -1))  13.5 us
    neg x2, other arithmetic, shards(): nodal = -nodal  9.76 us
  transfers between devices with their start and end apart: 16, of which 4 were waited for; matrix products, arithmetic and copies ran while one was open for 47% of the time, Pallas kernels for 0%

commit v1 on v0

v1 whole, which is shorter than its diff:
```python
import functools

import jax
import jax.numpy as jnp
from jax import lax
from jax.experimental import pallas as pl
from jax.experimental.pallas import tpu as pltpu
from jax.sharding import PartitionSpec as P

time_step = 0.5
horizon_sq = 2.0
core_sq = 0.01
stretch_scale = 0.3

f32 = jnp.float32
bf16 = jnp.bfloat16
LANES = 128
NT = (((1,), (1,)), ((), ()))
NN = (((1,), (0,)), ((), ()))
VM = pl.BlockSpec(memory_space=pltpu.VMEM)
SM = pl.BlockSpec(memory_space=pltpu.SMEM)
HIGHEST = lax.Precision.HIGHEST


def dot(a, b, dims, precision=None):
    return lax.dot_general(a, b, dims, precision=precision, preferred_element_type=f32)


def split(x, parts):
    out = []
    for _ in range(parts):
        piece = x.astype(bf16)
        out.append(piece)
        x = x - piece.astype(f32)
    return out


class Nodes:
    def __init__(self, nodes_dev):
        self.rows_dev = nodes_dev // LANES
        self.half = -(-self.rows_dev // 8) * 8
        self.rows = 2 * self.half

    def rows_of(self, ids):
        row = ids >> 7
        return row + jnp.where(row >= self.rows_dev, self.half - self.rows_dev, 0)

    def row_mask(self, row):
        return lax.broadcasted_iota(jnp.int32, (self.rows, row.shape[1]), 0) == row

    def lane_onehot(self, ids):
        lane = ids & (LANES - 1)
        hit = lax.broadcasted_iota(jnp.int32, (LANES, ids.shape[1]), 0) == lane
        return jnp.where(hit, 1.0, 0.0).astype(bf16)

    def pick(self, table, ids, parts=3):
        pieces = jnp.concatenate(split(table, parts), axis=1)
        onehot = self.lane_onehot(ids)
        rows = dot(pieces, jnp.concatenate([onehot] * parts, axis=0), NN)
        mask = self.row_mask(self.rows_of(ids))
        n = self.rows
        return [
            jnp.sum(jnp.where(mask, rows[c * n : (c + 1) * n], 0.0), axis=0, keepdims=True)
            for c in range(2)
        ]

    def spread(self, values, ids, parts=3):
        mask = self.row_mask(self.rows_of(ids))
        placed = jnp.concatenate([jnp.where(mask, v, 0.0) for v in values], axis=0)
        onehot = self.lane_onehot(ids)
        return dot(
            jnp.concatenate(split(placed, parts), axis=1),
            jnp.concatenate([onehot] * parts, axis=1),
            NT,
        )


def blend_tiles(rank, picked, blend, patch_tile, matrices, pack):
    patches = len(matrices) // 2
    for k, matrix in enumerate(matrices):
        side, index = divmod(k, patches)
        patch = jnp.where(side == 0, rank, 1 - rank) * patches + index
        cut = slice(k * LANES, (k + 1) * LANES)
        rows = jnp.concatenate(
            [picked[0][:, cut], picked[1][:, cut], jnp.zeros((6, LANES), f32)], axis=0
        )
        target = dot(rows, matrix, NT, HIGHEST)[:2]
        tile = patch_tile[patch]
        u = pack[tile, 2:4, :]
        weight = blend[pl.ds(patch, 1), :]
        pack[tile, 2:4, :] = u + weight * (target - u)


def table_halves(nodes, rank, own, partner, table):
    r = nodes.rows_dev
    pad = jnp.zeros((nodes.half - r, LANES), f32)
    for c in range(2):
        for ref, side in ((own, rank), (partner, 1 - rank)):
            at = pl.multiple_of(c * nodes.rows + side * nodes.half, 8)
            rows = ref[pl.ds(c, r, stride=2), :]
            table[pl.ds(at, nodes.half), :] = jnp.concatenate([rows, pad], axis=0)


def start_kernel(nodes, patch_tile, f_own, f_par, s_own, s_par, ids, blend, m_own, m_par, table, pack):
    rank = lax.axis_index("blk")
    table_halves(nodes, rank, f_own, f_par, table)
    tiles = s_own.shape[0]
    for t in range(tiles):
        pack[rank * tiles + t] = s_own[t]
        pack[(1 - rank) * tiles + t] = s_par[t]
    picked = nodes.pick(table[...], ids[...])
    matrices = [m_own[p] for p in range(m_own.shape[0])] + [m_par[p] for p in range(m_par.shape[0])]
    blend_tiles(rank, picked, blend, patch_tile, matrices, pack)


def element_kernel(nodes, table, ids, modulus, quad, grad, out, cat, lanes, disp, force):
    local, elems = ids.shape
    n = nodes.rows
    block = 4
    width = block * elems
    pieces = split(table[...], 2)
    cat[:, :LANES] = pieces[0]
    cat[:, LANES:] = pieces[1]

    def block_ids(step):
        rows = [ids[pl.ds(step * block + k, 1), :] for k in range(block)]
        return jnp.concatenate(rows, axis=1)

    def gather(step, carry):
        nid = block_ids(step)
        onehot = nodes.lane_onehot(nid)
        lanes[step] = onehot
        rows = dot(cat[...], jnp.concatenate([onehot, onehot], axis=0), NN)
        mask = nodes.row_mask(nodes.rows_of(nid))
        for c in range(2):
            got = jnp.sum(jnp.where(mask, rows[c * n : (c + 1) * n], 0.0), axis=0, keepdims=True)
            for k in range(block):
                disp[pl.ds(c * local + step * block + k, 1), :] = got[:, k * elems : (k + 1) * elems]
        return carry

    lax.fori_loop(0, local // block, gather, 0)
    g = grad[...]
    half = g.shape[0] // 2
    gx = dot(g, disp[:local], NN, HIGHEST)
    gy = dot(g, disp[local:], NN, HIGHEST)
    exx = gx[:half]
    eyy = gy[half:]
    exy = 0.5 * (gx[half:] + gy[:half])
    stiffen = 1.0 + exx * exx + eyy * eyy + 2.0 * exy * exy
    scaled = modulus[...] * quad[...] * stiffen
    trace = exx + eyy
    s_xx = scaled * (trace + 2.0 * exx)
    s_yy = scaled * (trace + 2.0 * eyy)
    s_xy = scaled * 2.0 * exy
    gt = g.T
    fx = dot(gt, jnp.concatenate([s_xx, s_xy], axis=0), NN, HIGHEST)
    fy = dot(gt, jnp.concatenate([s_xy, s_yy], axis=0), NN, HIGHEST)
    both = jnp.concatenate([fx, fy], axis=0)
    high = both.astype(bf16).astype(f32)
    force[0] = high
    force[1] = both - high
    out[...] = jnp.zeros_like(out)

    def scatter(step, carry):
        nid = block_ids(step)
        mask = nodes.row_mask(nodes.rows_of(nid))
        onehot = lanes[step]
        parts = []
        for part in range(2):
            comps = []
            for c in range(2):
                rows = [
                    force[part, pl.ds(c * local + step * block + k, 1), :] for k in range(block)
                ]
                comps.append(jnp.where(mask, jnp.concatenate(rows, axis=1), 0.0))
            parts.append(jnp.concatenate(comps, axis=0).astype(bf16))
        out[...] += dot(
            jnp.concatenate(parts, axis=1), jnp.concatenate([onehot, onehot], axis=1), NT
        )
        return carry

    lax.fori_loop(0, local // block, scatter, 0)


def gather_tiles(own, left, right, ext):
    tiles = own.shape[0]
    for k, ref in enumerate((left, own, right)):
        for t in range(tiles):
            ext[k * tiles + t] = ref[t]


CHUNK = 16


def pair_terms(x0, x1, u0, u1, far):
    o0 = far[0:1] - x0
    o1 = far[1:2] - x1
    d0 = o0 + (far[2:3] - u0)
    d1 = o1 + (far[3:4] - u1)
    rest_sq = o0 * o0 + o1 * o1
    rest_len = jnp.sqrt(rest_sq + core_sq)
    length = jnp.sqrt((d0 * d0 + d1 * d1) + core_sq)
    stretch = length - rest_len
    ratio = stretch * (1.0 / stretch_scale)
    bell = jnp.exp(rest_sq * (-1.0 / horizon_sq))
    return d0, d1, rest_sq, rest_len, length, stretch, bell, 1.0 + ratio * ratio


def family(fam_own, ints_par, rank, tile, slot, tiles_dev):
    side, index = divmod(tile, tiles_dev)
    if side == 0:
        return fam_own[index, slot]
    return ints_par[index, slot]


def dilatation_kernel(fam_own, fam_par, live, own, left, right, out, ext, cols, sums):
    rank = lax.axis_index("blk")
    tiles = own.shape[0]
    dev, slots = fam_own.shape
    gather_tiles(own, left, right, ext)
    ones = jnp.ones((8, LANES), f32)
    out[...] = jnp.zeros_like(out)
    for t in range(tiles):
        side, index = divmod(t, dev)
        tile = (rank if side == 0 else 1 - rank) * dev + index
        fam = fam_own if side == 0 else fam_par

        @pl.when(tile < live[0])
        def _():
            me = ext[tiles + tile]
            turned = me.T
            for q in range(4):
                cols[q] = jnp.broadcast_to(turned[:, q : q + 1], (LANES, LANES))
            fars = [ext[fam[index, s]] for s in range(slots)]

            def chunk(i, carry):
                at = pl.multiple_of(i * CHUNK, CHUNK)
                x0, x1, u0, u1 = [cols[q, pl.ds(at, CHUNK), :] for q in range(4)]
                vol = jnp.zeros((CHUNK, LANES), f32)
                dil = jnp.zeros((CHUNK, LANES), f32)
                for far in fars:
                    _, _, rest_sq, rest_len, _, stretch, bell, soft = pair_terms(x0, x1, u0, u1, far)
                    influence = bell / soft
                    vol = vol + influence * (rest_sq + core_sq)
                    dil = dil + influence * rest_len * stretch
                sums[pl.ds(at, CHUNK), :] = vol
                sums[pl.ds(LANES + at, CHUNK), :] = dil
                return carry

            lax.fori_loop(0, LANES // CHUNK, chunk, 0)
            total = dot(ones, sums[...], NT, HIGHEST)
            volume = total[:1, :LANES]
            theta = 2.0 * total[:1, LANES:] / volume
            k = me[6:7]
            scale = 4.0 * k / volume
            out[pl.ds(tile, 1), :] = 2.0 * k * theta / volume - scale * (0.5 * theta)
            out[pl.ds(tiles + tile, 1), :] = scale


def force_kernel(
    nodes, last, fam_own, fam_par, live, patch_tile, own, left, right, ac, ac_left, ac_right,
    el_own, el_par, ids, blend, m_own, m_par, shared, *refs,
):
    if last:
        nodal, low, high, disp_out, vel_out, ext, ext2, cols, sums, held = refs
    else:
        nodal, low, high, state, ext, ext2, cols, sums, held = refs
    rank = lax.axis_index("blk")
    tiles = own.shape[0]
    dev, slots = fam_own.shape
    gather_tiles(own, left, right, ext)
    for k, ref in enumerate((ac_left, ac, ac_right)):
        for t in range(tiles):
            ext2[k * tiles + t, 0:1, :] = ref[t : t + 1, :]
            ext2[k * tiles + t, 1:2, :] = ref[tiles + t : tiles + t + 1, :]
    ones = jnp.ones((8, LANES), f32)
    held[...] = jnp.zeros_like(held)
    for t in range(tiles):
        side, index = divmod(t, dev)
        tile = (rank if side == 0 else 1 - rank) * dev + index
        fam = fam_own if side == 0 else fam_par

        @pl.when(tile < live[0])
        def _():
            me = ext[tiles + tile]
            turned = me.T
            turned2 = ext2[tiles + tile].T
            for q in range(4):
                cols[q] = jnp.broadcast_to(turned[:, q : q + 1], (LANES, LANES))
            for q in range(2):
                cols[4 + q] = jnp.broadcast_to(turned2[:, q : q + 1], (LANES, LANES))
            fars = [(ext[fam[index, s]], ext2[fam[index, s]]) for s in range(slots)]

            def chunk(i, carry):
                at = pl.multiple_of(i * CHUNK, CHUNK)
                x0, x1, u0, u1, a_own, c_own = [cols[q, pl.ds(at, CHUNK), :] for q in range(6)]
                f0 = jnp.zeros((CHUNK, LANES), f32)
                f1 = jnp.zeros((CHUNK, LANES), f32)
                for far, far2 in fars:
                    d0, d1, _, rest_len, length, stretch, bell, soft = pair_terms(x0, x1, u0, u1, far)
                    scalar = (bell / (soft * length)) * (
                        rest_len * (a_own + far2[0:1]) + stretch * (c_own + far2[1:2])
                    )
                    f0 = f0 + scalar * d0
                    f1 = f1 + scalar * d1
                sums[pl.ds(at, CHUNK), :] = f0
                sums[pl.ds(LANES + at, CHUNK), :] = f1
                return carry

            lax.fori_loop(0, LANES // CHUNK, chunk, 0)
            total = dot(ones, sums[...], NT, HIGHEST)
            force = jnp.concatenate([total[:1, :LANES], total[:1, LANES:]], axis=0)
            vel = me[4:6] + me[7:8] * force
            disp = me[2:4] + time_step * vel
            held[tile, 0:2, :] = force
            held[tile, 2:4, :] = disp
            held[tile, 4:6, :] = vel

    if last:
        for t in range(dev):
            disp_out[t] = held[rank * dev + t, 2:4, :]
            vel_out[t] = held[rank * dev + t, 4:6, :]
    else:
        for t in range(tiles):
            mine = own[t]
            now = held[t]
            state[t] = jnp.concatenate([mine[0:2], now[2:6], mine[6:8]], axis=0)
    matrices = [m_own[p] for p in range(m_own.shape[0])] + [m_par[p] for p in range(m_par.shape[0])]
    patches = m_own.shape[0]
    reactions = []
    for k, matrix in enumerate(matrices):
        side, index = divmod(k, patches)
        patch = (rank if side == 0 else 1 - rank) * patches + index
        weighted = held[patch_tile[patch], 0:2, :] * blend[pl.ds(patch, 1), :]
        rows = jnp.concatenate([weighted, jnp.zeros((6, LANES), f32)], axis=0)
        reactions.append(dot(rows, matrix, NN, HIGHEST))
    react = jnp.concatenate(reactions, axis=1)
    total = nodes.spread([react[0:1], react[1:2]], ids[...]) - (el_own[...] + el_par[...])
    nodal[...] = total
    picked = nodes.pick(total, shared[...])
    for ref, at in ((low, 0), (high, LANES)):
        ref[...] = jnp.concatenate(
            [picked[0][:, at : at + LANES], picked[1][:, at : at + LANES], jnp.zeros((6, LANES), f32)],
            axis=0,
        )


def add_border(nodes, total, shared, from_low, from_high):
    dom = lax.axis_index("dom")
    ends = lax.axis_size("dom") - 1
    low = jnp.where(dom > 0, from_low[...], 0.0)
    high = jnp.where(dom < ends, from_high[...], 0.0)
    rows = jnp.concatenate([low, high], axis=1)
    return total + nodes.spread([rows[0:1], rows[1:2]], shared)


def update_kernel(
    nodes, patch_tile, nodal, table, v_own, v_par, t_own, t_par, from_low, from_high, shared, ids,
    blend, m_own, m_par, state, table_out, vel_out, step_out, pack,
):
    rank = lax.axis_index("blk")
    r = nodes.rows_dev
    force = add_border(nodes, nodal[...], shared[...], from_low, from_high)
    table_halves(nodes, rank, v_own, v_par, vel_out)
    pad = jnp.zeros((nodes.half - r, LANES), f32)
    for ref, side in ((t_own, rank), (t_par, 1 - rank)):
        at = pl.multiple_of(side * nodes.half, 8)
        step_out[pl.ds(at, nodes.half), :] = jnp.concatenate([ref[...], pad], axis=0)
    step = step_out[...]
    vel = vel_out[...] + jnp.concatenate([step, step], axis=0) * force
    vel_out[...] = vel
    disp = table[...] + time_step * vel
    table_out[...] = disp
    pack[...] = state[...]
    picked = nodes.pick(disp, ids[...])
    matrices = [m_own[p] for p in range(m_own.shape[0])] + [m_par[p] for p in range(m_par.shape[0])]
    blend_tiles(rank, picked, blend, patch_tile, matrices, pack)


def final_kernel(nodes, nodal, table, vel, step, from_low, from_high, shared, disp_out, vel_out, f_s, v_s):
    rank = lax.axis_index("blk")
    force = add_border(nodes, nodal[...], shared[...], from_low, from_high)
    steps = step[...]
    now = vel[...] + jnp.concatenate([steps, steps], axis=0) * force
    v_s[...] = now
    f_s[...] = table[...] + time_step * now
    r = nodes.rows_dev
    for c in range(2):
        at = pl.multiple_of(c * nodes.rows + rank * nodes.half, 8)
        disp_out[pl.ds(c, r, stride=2), :] = f_s[pl.ds(at, nodes.half), :][:r]
        vel_out[pl.ds(c, r, stride=2), :] = v_s[pl.ds(at, nodes.half), :][:r]


def call(kernel, name, outs, scalars, arrays, scratch=(), flops=0):
    size = sum(a.size * 4 for a in arrays) + sum(o.size * 4 for o in outs)
    return pl.pallas_call(
        kernel,
        name=name,
        out_shape=list(outs),
        in_specs=[SM] * len(scalars) + [VM] * len(arrays),
        out_specs=[VM] * len(outs),
        scratch_shapes=list(scratch),
        cost_estimate=pl.CostEstimate(flops=flops, bytes_accessed=size, transcendentals=0),
    )(*scalars, *arrays)


def shape(*dims, dtype=f32):
    return jax.ShapeDtypeStruct(dims, dtype)


def interleaved(x):
    comps, n = x.shape
    return x.reshape(comps, n // LANES, LANES).transpose(1, 0, 2).reshape(-1, LANES)


def shards(
    pd_disp, pd_vel, pd_coord, pd_modulus, pd_step, family_tile_lists, live_tiles, patch_tile,
    patch_blend, patch_nodes, patch_matrix, fe_disp, fe_vel, fe_step, fe_modulus, element_nodes,
    shape_grad, quad_weight, shared_left, shared_right,
):
    doms = lax.axis_size("dom")
    dev = pd_disp.shape[0]
    tiles = 2 * dev
    nodes = Nodes(fe_disp.shape[1])
    n2 = 2 * nodes.rows
    local, elems = element_nodes.shape

    def swap(x):
        return lax.ppermute(x, "blk", [(0, 1), (1, 0)])

    def up(x):
        return lax.ppermute(x, "dom", [(i, (i + 1) % doms) for i in range(doms)])

    def down(x):
        return lax.ppermute(x, "dom", [((i + 1) % doms, i) for i in range(doms)])

    f_own = interleaved(fe_disp)
    v_own = interleaved(fe_vel)
    t_own = fe_step.reshape(-1, LANES)
    s_own = jnp.concatenate(
        [pd_coord, pd_disp, pd_vel, pd_modulus[:, None], pd_step[:, None]], axis=1
    )
    f_par, s_par, m_par, ids_par = swap(f_own), swap(s_own), swap(patch_matrix), swap(patch_nodes)
    fam_par = swap(family_tile_lists)
    v_par, t_par = swap(v_own), swap(t_own)
    ids = jnp.concatenate([patch_nodes, ids_par], axis=0).reshape(1, -1)
    gap = ((0, 0), (0, LANES - shared_left.shape[1]))
    shared = jnp.concatenate(
        [jnp.pad(x, gap, constant_values=-1) for x in (shared_left, shared_right)], axis=1
    )
    grad = shape_grad.reshape(-1, local)
    quad = quad_weight[:, None]
    modulus = fe_modulus[None, :]

    table, pack = call(
        functools.partial(start_kernel, nodes), "start",
        [shape(n2, LANES), shape(tiles, 8, LANES)],
        [patch_tile],
        [f_own, f_par, s_own, s_par, ids, patch_blend, patch_matrix, m_par],
    )
    for section in range(2):
        last = section == 1
        pack_left, pack_right = up(pack), down(pack)
        (el_own,) = call(
            functools.partial(element_kernel, nodes), "elements",
            [shape(n2, LANES)],
            [],
            [table, element_nodes, modulus, quad, grad],
            [
                pltpu.VMEM((n2, 2 * LANES), bf16),
                pltpu.VMEM((local // 4, LANES, 4 * elems), bf16),
                pltpu.VMEM((2 * local, elems), f32),
                pltpu.VMEM((2, 2 * local, elems), f32),
            ],
            flops=4 * 10**9,
        )
        el_par = swap(el_own)
        (ac,) = call(
            dilatation_kernel, "dilatation",
            [shape(2 * tiles, LANES)],
            [family_tile_lists, fam_par, live_tiles],
            [pack, pack_left, pack_right],
            [
                pltpu.VMEM((3 * tiles, 8, LANES), f32),
                pltpu.VMEM((4, LANES, LANES), f32),
                pltpu.VMEM((2 * LANES, LANES), f32),
            ],
        )
        ac_left, ac_right = up(ac), down(ac)
        outs = [shape(n2, LANES), shape(8, LANES), shape(8, LANES)]
        if last:
            outs += [shape(dev, 2, LANES)] * 2
        else:
            outs += [shape(tiles, 8, LANES)]
        nodal, low, high, *rest = call(
            functools.partial(force_kernel, nodes, last), "force",
            outs,
            [family_tile_lists, fam_par, live_tiles, patch_tile],
            [
                pack, pack_left, pack_right, ac, ac_left, ac_right, el_own, el_par, ids,
                patch_blend, patch_matrix, m_par, shared,
            ],
            [
                pltpu.VMEM((3 * tiles, 8, LANES), f32),
                pltpu.VMEM((3 * tiles, 8, LANES), f32),
                pltpu.VMEM((6, LANES, LANES), f32),
                pltpu.VMEM((2 * LANES, LANES), f32),
                pltpu.VMEM((tiles, 8, LANES), f32),
            ],
        )
        from_low, from_high = up(high), down(low)
        if not last:
            table, vel, step, pack = call(
                functools.partial(update_kernel, nodes), "update",
                [shape(n2, LANES), shape(n2, LANES), shape(nodes.rows, LANES), shape(tiles, 8, LANES)],
                [patch_tile],
                [
                    nodal, table, v_own, v_par, t_own, t_par, from_low, from_high, shared, ids,
                    patch_blend, patch_matrix, m_par, rest[0],
                ],
            )
        else:
            pd_disp, pd_vel = rest
            fe_disp, fe_vel = call(
                functools.partial(final_kernel, nodes), "final",
                [shape(2 * nodes.rows_dev, LANES)] * 2,
                [],
                [nodal, table, vel, step, from_low, from_high, shared],
                [pltpu.VMEM((n2, LANES), f32)] * 2,
            )

    def flat(x):
        return x.reshape(-1, 2, LANES).transpose(1, 0, 2).reshape(2, -1)

    return (pd_disp, pd_vel, flat(fe_disp), flat(fe_vel))


def solution(mesh):
    return jax.shard_map(
        shards,
        mesh=mesh,
        in_specs=(
            P(("dom", "blk"), None, None),
            P(("dom", "blk"), None, None),
            P(("dom", "blk"), None, None),
            P(("dom", "blk"), None),
            P(("dom", "blk"), None),
            P(("dom", "blk"), None),
            P("dom"),
            P("dom"),
            P("dom", None),
            P(("dom", "blk"), None),
            P(("dom", "blk"), None, None),
            P(None, ("dom", "blk")),
            P(None, ("dom", "blk")),
            P(("dom", "blk")),
            P(("dom", "blk")),
            P(None, ("dom", "blk")),
            P(),
            P(),
            P("dom", None),
            P("dom", None),
        ),
        out_specs=(
            P(("dom", "blk"), None, None),
            P(("dom", "blk"), None, None),
            P(None, ("dom", "blk")),
            P(None, ("dom", "blk")),
        ),
        check_vma=False,
    )
```

time: 425 us -> 123 us (0.29)
  other arithmetic: 152 us -> 1.2 us
  local copies, waits for them, and re-layouts: 127 us -> 11.8 us
  Pallas kernels: 0 us -> 51.2 us
  blocking collectives: 26.3 us -> 0 us
  loops' own time: 21.4 us -> 0 us
  between operations: 15.4 us -> 1.59 us
  starting transfers between devices: 44.1 us -> 32.9 us
  waiting for transfers between devices: 32.4 us -> 23.1 us
    scatter-add x8 -> x0, other arithmetic: 135 us -> none  [the longest x2 94.8 us: shards(): nodal = jnp.zeros(fe_table.shape, jnp.float32).at[:, element_nodes.reshap...]
    gather x38 -> x0, local copies, waits for them, and re-layouts: 104 us -> none  [the longest x4 66.9 us: shards(): disp_el = fe_table[:, element_nodes]]
    pallas_call x0 -> x9, Pallas kernels: none -> 51.2 us  [call(): pl.pallas_call(kernel, name=name, out_shape=list(outs), in_specs=[SM] * l...]
    unnamed x4 -> x0, waiting for transfers between devices: 31.3 us -> none
    all_gather x11 -> x0, blocking collectives: 26.3 us -> none  [the longest x2 9.45 us: shards(): fe_table = lax.all_gather(fe_disp, 'blk', axis=1, tiled=True)]
    ppermute x14 -> x21, waiting for transfers between devices: 1.09 us -> 23.1 us  [the longest x6 18.9 us: up(): return lax.ppermute(x, 'dom', [(i, (i + 1) % doms) for i in range(doms)])]
    another operation x12 -> x0, loops' own time: 21.4 us -> none  [the longest x4 5.53 us: force_one(): return lax.cond(tile_number < active_flags, force_run, force_skip, None)]
    ppermute x14 -> x21, starting transfers between devices: 44 us -> 32.9 us  [the longest x6 28 us: down(): return lax.ppermute(x, 'dom', [((i + 1) % doms, i) for i in range(doms)])]
  transfers between devices with their start and end apart: 16 -> 21, of which waited for: 4 -> 8; matrix products, arithmetic and copies ran while one was open for 47% -> 3% of each run, Pallas kernels for 0% -> 22%
where the time goes in v1:
time: 123 us; the launch traced here: 122 us
  Pallas kernels  51.2 us (42%)
  starting transfers between devices  32.9 us (27%)
  waiting for transfers between devices  23.1 us (19%)
  local copies, waits for them, and re-layouts  11.8 us (10%)
  between operations  1.59 us (1%)
    pallas_call x9, Pallas kernels, call(): pl.pallas_call(kernel, name=name, out_shape=list(outs), in_specs=[SM] * l...  51.2 us
    ppermute x6, starting transfers between devices, down(): return lax.ppermute(x, 'dom', [((i + 1) % doms, i) for i in range(doms)])  28 us
    ppermute x6, waiting for transfers between devices, up(): return lax.ppermute(x, 'dom', [(i, (i + 1) % doms) for i in range(doms)])  18.9 us
    unnamed x70, local copies, waits for them, and re-layouts  7.77 us
    ppermute x6, waiting for transfers between devices, down(): return lax.ppermute(x, 'dom', [((i + 1) % doms, i) for i in range(doms)])  4.17 us
    ppermute x9, starting transfers between devices, swap(): return lax.ppermute(x, 'blk', [(0, 1), (1, 0)])  2.78 us
  transfers between devices with their start and end apart: 21, of which 8 were waited for; matrix products, arithmetic and copies ran while one was open for 3% of the time, Pallas kernels for 22%

profile of v1, /device:TPU:0, one launch (start us, length us, event | category | flops | bytes accessed | tf_op | source)
XLA Modules:
  0.0 121.8 jit_solution(7330351670415519233)
XLA Ops:
  1.9 0.7 concatenate.9.s_own
  2.7 0.8 reshape.41
  4.9 0.7 copy.31.quad
  6.9 2.1 %start.1 = (f32[224,128]{1,0:T(8,128)}, f32[4,8,128]{2,1,0:T(8,128)}) custom-call(s32[2]{0:T(128)} %patch_tile.7, f32[100,128]{1,0:T(8,128)} %copy-done.3, f32[100,128]{1,0:T(8,128)} %copy-done.13, f32[2,8,128]{2,1,0:T(8,128)} %copy-done.15, f32[2,8,128]{2,1,0:T(8,128)} %copy-done.20, s32[1,256]{1,0:T(1,128)} %bitcast.27, f32[2,128]{1,0:T(2,128)} %blend.7, ...), custom_call_target="tpu_custom_call" | custom-call | bytes 382976 | tf_op jit(solution)/shard_map/start/pallas_call | solution.py:396
  9.0 6.5 %collective-permute-start.6 = (f32[4,8,128]{2,1,0:T(8,128)}, f32[4,8,128]{2,1,0:T(8,128)S(1)}, u32[]{:S(2)}, u32[]{:S(2)}) collective-permute-start(f32[4,8,128]{2,1,0:T(8,128)} %get-tuple-element.21.own), channel_id=1, source_target_pairs={{2,0},{4,2},{6,4},{8,6},{10,8},{12,10},{14,12},{16,14},{18,16},{20... | collective-permute-start | bytes 49160 | tf_op jit(solution)/shard_map/ppermute | solution.py:435
  15.5 11.0 %elements.2.el_own = f32[224,128]{1,0:T(8,128)} custom-call(f32[224,128]{1,0:T(8,128)} %get-tuple-element.22.table, s32[64,128]{1,0:T(8,128)} %ids.3, f32[1,128]{1,0:T(1,128)} %bitcast.36, f32[64,1]{1,0:T(8,128)} %copy.31.quad, f32[128,64]{1,0:T(8,128)} %bitcast.34), custom_call_target="tpu_custom_call" | custom-call | flops 4000000000 | bytes 295680 | tf_op jit(solution)/shard_map/elements/pallas_call | solution.py:396
  29.6 4.9 %dilatation.2.ac = f32[8,128]{1,0:T(8,128)} custom-call(s32[2,3]{1,0:T(2,128)} %fam_own.7, s32[2,3]{1,0:T(2,128)} %copy-done.19, s32[1]{0:T(128)S(6)} %copy.44.live, f32[4,8,128]{2,1,0:T(8,128)} %get-tuple-element.21.own, f32[4,8,128]{2,1,0:T(8,128)} %copy-done.8, f32[4,8,128]{2,1,0:T(8,128)} %copy-done.6), custom_call_target="tpu_custom_call" | custom-call | bytes 53248 | tf_op jit(solution)/shard_map/dilatation/pallas_call | solution.py:396
  34.6 4.7 %collective-permute-start.8 = (f32[8,128]{1,0:T(8,128)}, f32[8,128]{1,0:T(8,128)S(1)}, u32[]{:S(2)}, u32[]{:S(2)}) collective-permute-start(f32[8,128]{1,0:T(8,128)} %dilatation.2.ac), channel_id=1, source_target_pairs={{2,0},{4,2},{6,4},{8,6},{10,8},{12,10},{14,12},{16,14},{18,16},{20... | collective-permute-start | bytes 12296 | tf_op jit(solution)/shard_map/ppermute | solution.py:435
  39.9 0.9 collective-permute-done.8.ac_right
  40.8 5.9 %collective-permute-done.7.ac_left = f32[8,128]{1,0:T(8,128)S(1)} collective-permute-done((f32[8,128]{1,0:T(8,128)}, f32[8,128]{1,0:T(8,128)S(1)}, u32[]{:S(2)}, u32[]{:S(2)}) %collective-permute-start.7) | collective-permute-done | bytes 4128 | tf_op jit(solution)/shard_map/ppermute | solution.py:432
  47.3 0.6 copy-done.4
  47.9 6.4 %force.2 = (f32[224,128]{1,0:T(8,128)}, f32[8,128]{1,0:T(8,128)}, f32[8,128]{1,0:T(8,128)}, f32[4,8,128]{2,1,0:T(8,128)}) custom-call(s32[2,3]{1,0:T(2,128)} %fam_own.7, s32[2,3]{1,0:T(2,128)} %copy-done.19, s32[1]{0:T(128)S(6)} %copy.44.live, s32[2]{0:T(128)} %patch_tile.7, f32[4,8,128]{2,1,0:T(8,128)} %get-tuple-element.21.own, f32[4,8,128]{2,1,0:T(8,128)} %copy-done.8, ...), custom_call_target="tpu_custom_call" | custom-call | bytes 564224 | tf_op jit(solution)/shard_map/force/pallas_call | solution.py:396
  54.4 5.6 %collective-permute-start.13 = (f32[8,128]{1,0:T(8,128)}, f32[8,128]{1,0:T(8,128)S(1)}, u32[]{:S(2)}, u32[]{:S(2)}) collective-permute-start(f32[8,128]{1,0:T(8,128)} %get-tuple-element.25), channel_id=1, source_target_pairs={{2,0},{4,2},{6,4},{8,6},{10,8},{12,10},{14,12},{16,14},{18,16},{20... | collective-permute-start | bytes 12296 | tf_op jit(solution)/shard_map/ppermute | solution.py:435
  60.0 1.8 %collective-permute-done.12.from_low = f32[8,128]{1,0:T(8,128)S(1)} collective-permute-done((f32[8,128]{1,0:T(8,128)}, f32[8,128]{1,0:T(8,128)S(1)}, u32[]{:S(2)}, u32[]{:S(2)}) %collective-permute-start.12) | collective-permute-done | bytes 4128 | tf_op jit(solution)/shard_map/ppermute | solution.py:432
  62.4 2.5 %update.1 = (f32[224,128]{1,0:T(8,128)}, f32[224,128]{1,0:T(8,128)}, f32[112,128]{1,0:T(8,128)}, f32[4,8,128]{2,1,0:T(8,128)}) custom-call(s32[2]{0:T(128)} %patch_tile.7, f32[224,128]{1,0:T(8,128)} %get-tuple-element.23.nodal, f32[224,128]{1,0:T(8,128)} %get-tuple-element.22.table, f32[100,128]{1,0:T(8,128)} %copy-done.2, f32[100,128]{1,0:T(8,128)} %copy-done.11, ...), custom_call_target="tpu_custom_call" | custom-call | bytes 844800 | tf_op jit(solution)/shard_map/update/pallas_call | solution.py:396
  64.9 10.9 %elements.3.el_own = f32[224,128]{1,0:T(8,128)} custom-call(f32[224,128]{1,0:T(8,128)} %get-tuple-element.28.table, s32[64,128]{1,0:T(8,128)} %ids.3, f32[1,128]{1,0:T(1,128)} %bitcast.37, f32[64,1]{1,0:T(8,128)} %copy.31.quad, f32[128,64]{1,0:T(8,128)} %bitcast.35), custom_call_target="tpu_custom_call" | custom-call | flops 4000000000 | bytes 295680 | tf_op jit(solution)/shard_map/elements/pallas_call | solution.py:396
  75.9 5.6 %collective-permute-start.15 = (f32[4,8,128]{2,1,0:T(8,128)S(1)}, f32[4,8,128]{2,1,0:T(8,128)S(1)}, u32[]{:S(2)}, u32[]{:S(2)}) collective-permute-start(f32[4,8,128]{2,1,0:T(8,128)S(1)} %copy-done.7), channel_id=1, source_target_pairs={{2,0},{4,2},{6,4},{8,6},{10,8},{12,10},{14,12},{16,14},{18,16},{20... | collective-permute-start | bytes 49160 | tf_op jit(solution)/shard_map/ppermute | solution.py:435
  81.5 1.4 %collective-permute-done.15.right = f32[4,8,128]{2,1,0:T(8,128)S(1)} collective-permute-done((f32[4,8,128]{2,1,0:T(8,128)S(1)}, f32[4,8,128]{2,1,0:T(8,128)S(1)}, u32[]{:S(2)}, u32[]{:S(2)}) %collective-permute-start.15) | collective-permute-done | bytes 16416 | tf_op jit(solution)/shard_map/ppermute | solution.py:435
  82.9 5.9 %collective-permute-done.14.left = f32[4,8,128]{2,1,0:T(8,128)S(1)} collective-permute-done((f32[4,8,128]{2,1,0:T(8,128)S(1)}, f32[4,8,128]{2,1,0:T(8,128)S(1)}, u32[]{:S(2)}, u32[]{:S(2)}) %collective-permute-start.14) | collective-permute-done | bytes 16416 | tf_op jit(solution)/shard_map/ppermute | solution.py:432
  88.8 0.6 copy-done.10
  89.4 4.9 %dilatation.3.ac = f32[8,128]{1,0:T(8,128)} custom-call(s32[2,3]{1,0:T(2,128)} %fam_own.7, s32[2,3]{1,0:T(2,128)} %copy-done.19, s32[1]{0:T(128)S(6)} %copy.44.live, f32[4,8,128]{2,1,0:T(8,128)} %get-tuple-element.27.own, f32[4,8,128]{2,1,0:T(8,128)} %copy-done.10, f32[4,8,128]{2,1,0:T(8,128)} %copy-done.9), custom_call_target="tpu_custom_call" | custom-call | bytes 53248 | tf_op jit(solution)/shard_map/dilatation/pallas_call | solution.py:396
  94.3 2.0 %collective-permute-start.16 = (f32[8,128]{1,0:T(8,128)}, f32[8,128]{1,0:T(8,128)S(1)}, u32[]{:S(2)}, u32[]{:S(2)}) collective-permute-start(f32[8,128]{1,0:T(8,128)} %dilatation.3.ac), channel_id=1, source_target_pairs={{0,2},{2,4},{4,6},{6,8},{8,10},{10,12},{12,14},{14,16},{16,18},{18... | collective-permute-start | bytes 12296 | tf_op jit(solution)/shard_map/ppermute | solution.py:432
  96.3 1.8 %collective-permute-done.17.ac_right = f32[8,128]{1,0:T(8,128)S(1)} collective-permute-done((f32[8,128]{1,0:T(8,128)}, f32[8,128]{1,0:T(8,128)S(1)}, u32[]{:S(2)}, u32[]{:S(2)}) %collective-permute-start.17) | collective-permute-done | bytes 4128 | tf_op jit(solution)/shard_map/ppermute | solution.py:435
  98.1 3.6 %collective-permute-done.16.ac_left = f32[8,128]{1,0:T(8,128)S(1)} collective-permute-done((f32[8,128]{1,0:T(8,128)}, f32[8,128]{1,0:T(8,128)S(1)}, u32[]{:S(2)}, u32[]{:S(2)}) %collective-permute-start.16) | collective-permute-done | bytes 4128 | tf_op jit(solution)/shard_map/ppermute | solution.py:432
  102.3 0.6 copy-done.5
  103.0 6.4 %force.3 = (f32[224,128]{1,0:T(8,128)}, f32[8,128]{1,0:T(8,128)}, f32[8,128]{1,0:T(8,128)}, f32[2,2,128]{2,1,0:T(2,128)}, f32[2,2,128]{2,1,0:T(2,128)}) custom-call(s32[2,3]{1,0:T(2,128)} %fam_own.7, s32[2,3]{1,0:T(2,128)} %copy-done.19, s32[1]{0:T(128)S(6)} %copy.44.live, s32[2]{0:T(128)} %patch_tile.7, f32[4,8,128]{2,1,0:T(8,128)} %get-tuple-element.27.own, ...), custom_call_target="tpu_custom_call" | custom-call | bytes 551936 | tf_op jit(solution)/shard_map/force/pallas_call | solution.py:396
  109.4 5.6 %collective-permute-start.20 = (f32[8,128]{1,0:T(8,128)}, f32[8,128]{1,0:T(8,128)S(1)}, u32[]{:S(2)}, u32[]{:S(2)}) collective-permute-start(f32[8,128]{1,0:T(8,128)} %get-tuple-element.35), channel_id=1, source_target_pairs={{2,0},{4,2},{6,4},{8,6},{10,8},{12,10},{14,12},{16,14},{18,16},{20... | collective-permute-start | bytes 12296 | tf_op jit(solution)/shard_map/ppermute | solution.py:435
  115.0 1.8 %collective-permute-done.19.from_low = f32[8,128]{1,0:T(8,128)S(1)} collective-permute-done((f32[8,128]{1,0:T(8,128)}, f32[8,128]{1,0:T(8,128)S(1)}, u32[]{:S(2)}, u32[]{:S(2)}) %collective-permute-start.19) | collective-permute-done | bytes 4128 | tf_op jit(solution)/shard_map/ppermute | solution.py:432
  117.4 2.0 %final.1 = (f32[100,128]{1,0:T(8,128)}, f32[100,128]{1,0:T(8,128)}) custom-call(f32[224,128]{1,0:T(8,128)} %get-tuple-element.31.nodal, f32[224,128]{1,0:T(8,128)} %get-tuple-element.28.table, f32[224,128]{1,0:T(8,128)} %get-tuple-element.32.vel, f32[112,128]{1,0:T(8,128)} %get-tuple-element.33.step, f32[8,128]{1,0:T(8,128)} %copy-done.23, ...), custom_call_target="tpu_custom_call" | custom-call | bytes 513024 | tf_op jit(solution)/shard_map/final/pallas_call | solution.py:396
  119.4 0.8 reshape.48
  120.2 0.8 copy-done.12
  121.1 0.7 copy_bitcast_fusion.2
  (104 shorter events, 9.4 us)
Async XLA Ops:
  0.6 5.0 %collective-permute-start.3 = (s32[1,128]{1,0:T(1,128)}, s32[1,128]{1,0:T(1,128)S(1)}, u32[]{:S(2)}, u32[]{:S(2)}) collective-permute-start(s32[1,128]{1,0:T(1,128)} %param.29), channel_id=1, source_target_pairs={{0,1},{1,0},{2,3},{3,2},{4,5},{5,4},{6,7},{7,6},{8,9},{9,8},{10,11... | collective-permute-start | bytes 1544 | tf_op jit(solution)/shard_map/ppermute | solution.py:429
  2.6 3.6 %collective-permute-start.2 = (f32[2,8,128]{2,1,0:T(8,128)S(1)}, f32[2,8,128]{2,1,0:T(8,128)S(1)}, u32[]{:S(2)}, u32[]{:S(2)}) collective-permute-start(f32[2,8,128]{2,1,0:T(8,128)S(1)} %concatenate.9.s_own), channel_id=1, source_target_pairs={{0,1},{1,0},{2,3},{3,2},{4,5},{5,4},{6,7},{7,6},{8,9},{9,8},{10,11... | collective-permute-start | bytes 24584 | tf_op jit(solution)/shard_map/ppermute | solution.py:429
  3.6 2.6 %copy-start.3 = (f32[100,128]{1,0:T(8,128)}, f32[100,128]{1,0:T(8,128)S(1)}, u32[]{:S(2)}) copy-start(f32[100,128]{1,0:T(8,128)S(1)} %reshape.42.f_own) | copy-start | bytes 153604
  3.7 2.6 %collective-permute-start.1 = (f32[100,128]{1,0:T(8,128)S(1)}, f32[100,128]{1,0:T(8,128)S(1)}, u32[]{:S(2)}, u32[]{:S(2)}) collective-permute-start(f32[100,128]{1,0:T(8,128)S(1)} %reshape.42.f_own), channel_id=1, source_target_pairs={{0,1},{1,0},{2,3},{3,2},{4,5},{5,4},{6,7},{7,6},{8,9},{9,8},{10,11... | collective-permute-start | bytes 153608 | tf_op jit(solution)/shard_map/ppermute | solution.py:429
  4.4 1.8 %collective-permute-start.4 = (f32[1,128,128]{2,1,0:T(8,128)S(1)}, f32[1,128,128]{2,1,0:T(8,128)S(1)}, u32[]{:S(2)}, u32[]{:S(2)}) collective-permute-start(f32[1,128,128]{2,1,0:T(8,128)S(1)} %copy-done), channel_id=1, source_target_pairs={{0,1},{1,0},{2,3},{3,2},{4,5},{5,4},{6,7},{7,6},{8,9},{9,8},{10,11... | collective-permute-start | bytes 196616 | tf_op jit(solution)/shard_map/ppermute | solution.py:429
  9.0 19.4 %collective-permute-start.6 = (f32[4,8,128]{2,1,0:T(8,128)}, f32[4,8,128]{2,1,0:T(8,128)S(1)}, u32[]{:S(2)}, u32[]{:S(2)}) collective-permute-start(f32[4,8,128]{2,1,0:T(8,128)} %get-tuple-element.21.own), channel_id=1, source_target_pairs={{2,0},{4,2},{6,4},{8,6},{10,8},{12,10},{14,12},{16,14},{18,16},{20... | collective-permute-start | bytes 49160 | tf_op jit(solution)/shard_map/ppermute | solution.py:435
  15.5 12.9 %collective-permute-start.5 = (f32[4,8,128]{2,1,0:T(8,128)}, f32[4,8,128]{2,1,0:T(8,128)S(1)}, u32[]{:S(2)}, u32[]{:S(2)}) collective-permute-start(f32[4,8,128]{2,1,0:T(8,128)} %get-tuple-element.21.own), channel_id=1, source_target_pairs={{0,2},{2,4},{4,6},{6,8},{8,10},{10,12},{12,14},{14,16},{16,18},{18... | collective-permute-start | bytes 49160 | tf_op jit(solution)/shard_map/ppermute | solution.py:432
  15.5 11.2 %copy-start.18 = (s32[2,3]{1,0:T(2,128)S(1)}, s32[2,3]{1,0:T(2,128)}, u32[]{:S(2)}) copy-start(s32[2,3]{1,0:T(2,128)} %fam_own.7) | copy-start | bytes 76
  15.5 11.5 %copy-start.16 = (f32[6400]{0:T(1024)S(1)}, f32[6400]{0:T(1024)}, u32[]{:S(2)}) copy-start(f32[6400]{0:T(1024)} %param.33) | copy-start | bytes 76804
  15.5 12.3 %copy-start.14 = (f32[2,6400]{1,0:T(2,128)S(1)}, f32[2,6400]{1,0:T(2,128)}, u32[]{:S(2)}) copy-start(f32[2,6400]{1,0:T(2,128)} %param.32) | copy-start | bytes 153604
  26.5 20.2 %collective-permute-start.9 = (f32[224,128]{1,0:T(8,128)}, f32[224,128]{1,0:T(8,128)S(1)}, u32[]{:S(2)}, u32[]{:S(2)}) collective-permute-start(f32[224,128]{1,0:T(8,128)} %elements.2.el_own), channel_id=1, source_target_pairs={{0,1},{1,0},{2,3},{3,2},{4,5},{5,4},{6,7},{7,6},{8,9},{9,8},{10,11... | collective-permute-start | bytes 344072 | tf_op jit(solution)/shard_map/ppermute | solution.py:429
  26.7 1.3 %collective-permute-start = (s32[2,3]{1,0:T(2,128)S(1)}, s32[2,3]{1,0:T(2,128)S(1)}, u32[]{:S(2)}, u32[]{:S(2)}) collective-permute-start(s32[2,3]{1,0:T(2,128)S(1)} %copy-done.18), channel_id=1, source_target_pairs={{0,1},{1,0},{2,3},{3,2},{4,5},{5,4},{6,7},{7,6},{8,9},{9,8},{10,11... | collective-permute-start | bytes 80 | tf_op jit(solution)/shard_map/ppermute | solution.py:429
  27.0 33.0 %collective-permute-start.11 = (f32[50,128]{1,0:T(8,128)S(1)}, f32[50,128]{1,0:T(8,128)S(1)}, u32[]{:S(2)}, u32[]{:S(2)}) collective-permute-start(f32[50,128]{1,0:T(8,128)S(1)} %bitcast.26), channel_id=1, source_target_pairs={{0,1},{1,0},{2,3},{3,2},{4,5},{5,4},{6,7},{7,6},{8,9},{9,8},{10,11... | collective-permute-start | bytes 76808 | tf_op jit(solution)/shard_map/ppermute | solution.py:429
  28.0 26.3 %copy-start.2 = (f32[100,128]{1,0:T(8,128)}, f32[100,128]{1,0:T(8,128)S(1)}, u32[]{:S(2)}) copy-start(f32[100,128]{1,0:T(8,128)S(1)} %reshape.46.v_own) | copy-start | bytes 153604
  28.0 11.3 %copy-start.33 = (s32[1,113]{1,0:T(1,128)S(1)}, s32[1,113]{1,0:T(1,128)}, u32[]{:S(2)}) copy-start(s32[1,113]{1,0:T(1,128)} %param.39) | copy-start | bytes 1360
  28.0 11.3 %copy-start.34 = (s32[1,113]{1,0:T(1,128)S(1)}, s32[1,113]{1,0:T(1,128)}, u32[]{:S(2)}) copy-start(s32[1,113]{1,0:T(1,128)} %param.38) | copy-start | bytes 1360
  28.1 31.9 %collective-permute-start.10 = (f32[100,128]{1,0:T(8,128)S(1)}, f32[100,128]{1,0:T(8,128)S(1)}, u32[]{:S(2)}, u32[]{:S(2)}) collective-permute-start(f32[100,128]{1,0:T(8,128)S(1)} %reshape.46.v_own), channel_id=1, source_target_pairs={{0,1},{1,0},{2,3},{3,2},{4,5},{5,4},{6,7},{7,6},{8,9},{9,8},{10,11... | collective-permute-start | bytes 153608 | tf_op jit(solution)/shard_map/ppermute | solution.py:429
  34.6 6.3 %collective-permute-start.8 = (f32[8,128]{1,0:T(8,128)}, f32[8,128]{1,0:T(8,128)S(1)}, u32[]{:S(2)}, u32[]{:S(2)}) collective-permute-start(f32[8,128]{1,0:T(8,128)} %dilatation.2.ac), channel_id=1, source_target_pairs={{2,0},{4,2},{6,4},{8,6},{10,8},{12,10},{14,12},{16,14},{18,16},{20... | collective-permute-start | bytes 12296 | tf_op jit(solution)/shard_map/ppermute | solution.py:435
  39.3 7.4 %collective-permute-start.7 = (f32[8,128]{1,0:T(8,128)}, f32[8,128]{1,0:T(8,128)S(1)}, u32[]{:S(2)}, u32[]{:S(2)}) collective-permute-start(f32[8,128]{1,0:T(8,128)} %dilatation.2.ac), channel_id=1, source_target_pairs={{0,2},{2,4},{4,6},{6,8},{8,10},{10,12},{12,14},{14,16},{16,18},{18... | collective-permute-start | bytes 12296 | tf_op jit(solution)/shard_map/ppermute | solution.py:432
  40.8 5.9 %copy-start.27 = (f32[8,128]{1,0:T(8,128)}, f32[8,128]{1,0:T(8,128)S(1)}, u32[]{:S(2)}) copy-start(f32[8,128]{1,0:T(8,128)S(1)} %collective-permute-done.8.ac_right) | copy-start | bytes 12292
  54.3 7.5 %collective-permute-start.12 = (f32[8,128]{1,0:T(8,128)}, f32[8,128]{1,0:T(8,128)S(1)}, u32[]{:S(2)}, u32[]{:S(2)}) collective-permute-start(f32[8,128]{1,0:T(8,128)} %get-tuple-element.24), channel_id=1, source_target_pairs={{0,2},{2,4},{4,6},{6,8},{8,10},{10,12},{12,14},{14,16},{16,18},{18... | collective-permute-start | bytes 12296 | tf_op jit(solution)/shard_map/ppermute | solution.py:432
  54.4 7.4 %collective-permute-start.13 = (f32[8,128]{1,0:T(8,128)}, f32[8,128]{1,0:T(8,128)S(1)}, u32[]{:S(2)}, u32[]{:S(2)}) collective-permute-start(f32[8,128]{1,0:T(8,128)} %get-tuple-element.25), channel_id=1, source_target_pairs={{2,0},{4,2},{6,4},{8,6},{10,8},{12,10},{14,12},{16,14},{18,16},{20... | collective-permute-start | bytes 12296 | tf_op jit(solution)/shard_map/ppermute | solution.py:435
  64.9 10.9 %copy-start.7 = (f32[4,8,128]{2,1,0:T(8,128)S(1)}, f32[4,8,128]{2,1,0:T(8,128)}, u32[]{:S(2)}) copy-start(f32[4,8,128]{2,1,0:T(8,128)} %get-tuple-element.27.own) | copy-start | bytes 49156
  75.8 25.9 %collective-permute-start.18 = (f32[224,128]{1,0:T(8,128)}, f32[224,128]{1,0:T(8,128)S(1)}, u32[]{:S(2)}, u32[]{:S(2)}) collective-permute-start(f32[224,128]{1,0:T(8,128)} %elements.3.el_own), channel_id=1, source_target_pairs={{0,1},{1,0},{2,3},{3,2},{4,5},{5,4},{6,7},{7,6},{8,9},{9,8},{10,11... | collective-permute-start | bytes 344072 | tf_op jit(solution)/shard_map/ppermute | solution.py:429
  75.9 7.1 %collective-permute-start.15 = (f32[4,8,128]{2,1,0:T(8,128)S(1)}, f32[4,8,128]{2,1,0:T(8,128)S(1)}, u32[]{:S(2)}, u32[]{:S(2)}) collective-permute-start(f32[4,8,128]{2,1,0:T(8,128)S(1)} %copy-done.7), channel_id=1, source_target_pairs={{2,0},{4,2},{6,4},{8,6},{10,8},{12,10},{14,12},{16,14},{18,16},{20... | collective-permute-start | bytes 49160 | tf_op jit(solution)/shard_map/ppermute | solution.py:435
  81.5 7.3 %collective-permute-start.14 = (f32[4,8,128]{2,1,0:T(8,128)S(1)}, f32[4,8,128]{2,1,0:T(8,128)S(1)}, u32[]{:S(2)}, u32[]{:S(2)}) collective-permute-start(f32[4,8,128]{2,1,0:T(8,128)S(1)} %copy-done.7), channel_id=1, source_target_pairs={{0,2},{2,4},{4,6},{6,8},{8,10},{10,12},{12,14},{14,16},{16,18},{18... | collective-permute-start | bytes 49160 | tf_op jit(solution)/shard_map/ppermute | solution.py:432
  82.9 5.9 %copy-start.9 = (f32[4,8,128]{2,1,0:T(8,128)}, f32[4,8,128]{2,1,0:T(8,128)S(1)}, u32[]{:S(2)}) copy-start(f32[4,8,128]{2,1,0:T(8,128)S(1)} %collective-permute-done.15.right) | copy-start | bytes 49156
  94.3 3.8 %collective-permute-start.17 = (f32[8,128]{1,0:T(8,128)}, f32[8,128]{1,0:T(8,128)S(1)}, u32[]{:S(2)}, u32[]{:S(2)}) collective-permute-start(f32[8,128]{1,0:T(8,128)} %dilatation.3.ac), channel_id=1, source_target_pairs={{2,0},{4,2},{6,4},{8,6},{10,8},{12,10},{14,12},{16,14},{18,16},{20... | collective-permute-start | bytes 12296 | tf_op jit(solution)/shard_map/ppermute | solution.py:435
  94.3 7.4 %collective-permute-start.16 = (f32[8,128]{1,0:T(8,128)}, f32[8,128]{1,0:T(8,128)S(1)}, u32[]{:S(2)}, u32[]{:S(2)}) collective-permute-start(f32[8,128]{1,0:T(8,128)} %dilatation.3.ac), channel_id=1, source_target_pairs={{0,2},{2,4},{4,6},{6,8},{8,10},{10,12},{12,14},{14,16},{16,18},{18... | collective-permute-start | bytes 12296 | tf_op jit(solution)/shard_map/ppermute | solution.py:432
  98.1 3.6 %copy-start.25 = (f32[8,128]{1,0:T(8,128)}, f32[8,128]{1,0:T(8,128)S(1)}, u32[]{:S(2)}) copy-start(f32[8,128]{1,0:T(8,128)S(1)} %collective-permute-done.17.ac_right) | copy-start | bytes 12292
  109.4 7.4 %collective-permute-start.19 = (f32[8,128]{1,0:T(8,128)}, f32[8,128]{1,0:T(8,128)S(1)}, u32[]{:S(2)}, u32[]{:S(2)}) collective-permute-start(f32[8,128]{1,0:T(8,128)} %get-tuple-element.34), channel_id=1, source_target_pairs={{0,2},{2,4},{4,6},{6,8},{8,10},{10,12},{12,14},{14,16},{16,18},{18... | collective-permute-start | bytes 12296 | tf_op jit(solution)/shard_map/ppermute | solution.py:432
  109.4 7.4 %collective-permute-start.20 = (f32[8,128]{1,0:T(8,128)}, f32[8,128]{1,0:T(8,128)S(1)}, u32[]{:S(2)}, u32[]{:S(2)}) collective-permute-start(f32[8,128]{1,0:T(8,128)} %get-tuple-element.35), channel_id=1, source_target_pairs={{2,0},{4,2},{6,4},{8,6},{10,8},{12,10},{14,12},{16,14},{18,16},{20... | collective-permute-start | bytes 12296 | tf_op jit(solution)/shard_map/ppermute | solution.py:435
  (24 other events, 18.6 us)

commit v2 on v1

v2 whole, which is shorter than its diff:
```python
import functools

import jax
import jax.numpy as jnp
from jax import lax
from jax.experimental import pallas as pl
from jax.experimental.pallas import tpu as pltpu
from jax.sharding import PartitionSpec as P


time_step = 0.5
horizon_sq = 2.0
core_sq = 0.01
stretch_scale = 0.3

f32 = jnp.float32
bf16 = jnp.bfloat16
LANES = 128
NT = (((1,), (1,)), ((), ()))
NN = (((1,), (0,)), ((), ()))
VM = pl.BlockSpec(memory_space=pltpu.VMEM)
SM = pl.BlockSpec(memory_space=pltpu.SMEM)
HBM = pl.BlockSpec(memory_space=pltpu.HBM)
HIGHEST = lax.Precision.HIGHEST


def dot(a, b, dims, precision=None):
    return lax.dot_general(a, b, dims, precision=precision, preferred_element_type=f32)


def split(x, parts):
    out = []
    for _ in range(parts):
        piece = x.astype(bf16)
        out.append(piece)
        x = x - piece.astype(f32)
    return out


class Nodes:
    def __init__(self, nodes_dev):
        self.rows_dev = nodes_dev // LANES
        self.half = -(-self.rows_dev // 8) * 8
        self.rows = 2 * self.half

    def rows_of(self, ids):
        row = ids >> 7
        return row + jnp.where(row >= self.rows_dev, self.half - self.rows_dev, 0)

    def row_mask(self, row):
        return lax.broadcasted_iota(jnp.int32, (self.rows, row.shape[1]), 0) == row

    def lane_onehot(self, ids):
        lane = ids & (LANES - 1)
        hit = lax.broadcasted_iota(jnp.int32, (LANES, ids.shape[1]), 0) == lane
        return jnp.where(hit, 1.0, 0.0).astype(bf16)

    def pick(self, table, ids, parts=3):
        pieces = jnp.concatenate(split(table, parts), axis=1)
        onehot = self.lane_onehot(ids)
        rows = dot(pieces, jnp.concatenate([onehot] * parts, axis=0), NN)
        mask = self.row_mask(self.rows_of(ids))
        n = self.rows
        return [
            jnp.sum(jnp.where(mask, rows[c * n : (c + 1) * n], 0.0), axis=0, keepdims=True)
            for c in range(2)
        ]

    def spread(self, values, ids, parts=3):
        mask = self.row_mask(self.rows_of(ids))
        placed = jnp.concatenate([jnp.where(mask, v, 0.0) for v in values], axis=0)
        onehot = self.lane_onehot(ids)
        return dot(
            jnp.concatenate(split(placed, parts), axis=1),
            jnp.concatenate([onehot] * parts, axis=1),
            NT,
        )


def blend_tiles(picked, patch_rows, matrices, pack):
    patches = matrices.shape[0]
    for k in range(patches):
        cut = slice(k * LANES, (k + 1) * LANES)
        rows = jnp.concatenate(
            [picked[0][:, cut], picked[1][:, cut], jnp.zeros((6, LANES), f32)], axis=0
        )
        target = dot(rows, matrices[k], NT, HIGHEST)[:2]
        weight = patch_rows[k : k + 1, :]
        chosen = patch_rows[patches + k : patches + k + 1, :]
        for t in range(pack.shape[0]):
            u = pack[t, 2:4, :]
            pack[t, 2:4, :] = u + jnp.where(chosen == float(t), weight * (target - u), 0.0)


class Parcel:
    def __init__(self, nodes, tiles, patches, local):
        self.tiles, self.patches = tiles, patches
        sizes = [
            ("disp", 2 * nodes.half), ("vel", 2 * nodes.half), ("step", nodes.half),
            ("points", 8 * tiles), ("matrix", LANES * patches),
            ("misc", 8 * -(-(7 * patches + 4) // 8)), ("elements", local), ("grad", 2 * local),
        ]
        self.at, row = {}, 0
        for name, size in sizes:
            self.at[name] = slice(row, row + size)
            row += size
        self.rows = row
        first = self.at["misc"].start
        counts = [
            ("nodes", patches), ("quad", 1), ("modulus", 1), ("blend", 2 * patches), ("left", 1),
            ("right", 1), ("tile", 2 * patches),
        ]
        for name, size in counts:
            self.at[name] = slice(first, first + size)
            first += size


def pack_kernel(nodes, parcel, count, *refs):
    given, out, held, sem = refs[:count], refs[count], refs[count + 1 : -1], refs[-1]
    copies = [pltpu.make_async_copy(a, b, sem.at[k]) for k, (a, b) in enumerate(zip(given, held))]
    for copy in copies:
        copy.start()
    for copy in copies:
        copy.wait()
    (
        matrix, ids, disp, x, u, v, k, step, vel, mass_step, left, right, elements, grad, quad,
        modulus, blend, patch_tile,
    ) = held
    pad = jnp.zeros((nodes.half - nodes.rows_dev, LANES), f32)
    for name, flat in (("disp", disp), ("vel", vel)):
        rows = []
        for c in range(2):
            rows += [flat[c : c + 1, i * LANES : (i + 1) * LANES] for i in range(nodes.rows_dev)]
            rows.append(pad)
        out[parcel.at[name], :] = jnp.concatenate(rows, axis=0)
    out[parcel.at["step"], :] = jnp.concatenate([mass_step[...], pad], axis=0)
    rows = []
    for t in range(parcel.tiles):
        rows += [x[t], u[t], v[t], k[t : t + 1, :], step[t : t + 1, :]]
    out[parcel.at["points"], :] = jnp.concatenate(rows, axis=0)
    for p in range(parcel.patches):
        first = parcel.at["matrix"].start + p * LANES
        out[first : first + LANES, :] = matrix[p]
    out[parcel.at["misc"], :] = jnp.full((parcel.at["misc"].stop - parcel.at["misc"].start, LANES), -1.0, f32)
    for name, ref in (
        ("nodes", ids), ("quad", quad), ("modulus", modulus), ("blend", blend), ("left", left), ("right", right),
    ):
        out[parcel.at[name], : ref.shape[1]] = ref[...].astype(f32)
    for p in range(2 * parcel.patches):
        row = parcel.at["tile"].start + p
        out[row : row + 1, :] = jnp.full((1, LANES), patch_tile[p], jnp.int32).astype(f32)
    out[parcel.at["elements"], :] = elements[...].astype(f32)
    out[parcel.at["grad"], : grad.shape[1]] = grad[...]


def start_kernel(
    nodes, parcel, own, partner, table, vel, step, pack, matrices, ids, shared, patch_rows, elements,
    grad, quad, modulus,
):
    rank = lax.axis_index("blk")
    half, tiles, patches = nodes.half, parcel.tiles, parcel.patches
    for order, (side, ref) in enumerate(((rank, own), (1 - rank, partner))):
        for name, out in (("disp", table), ("vel", vel)):
            for c in range(2):
                at = pl.multiple_of(c * nodes.rows + side * half, 8)
                first = parcel.at[name].start + c * half
                out[pl.ds(at, half), :] = ref[first : first + half, :]
        step[pl.ds(pl.multiple_of(side * half, 8), half), :] = ref[parcel.at["step"], :]
        for t in range(tiles):
            first = parcel.at["points"].start + 8 * t
            pack[side * tiles + t] = ref[first : first + 8, :]
        for p in range(patches):
            k = order * patches + p
            first = parcel.at["matrix"].start + p * LANES
            matrices[k] = ref[first : first + LANES, :]
            row = parcel.at["nodes"].start + p
            ids[:, k * LANES : (k + 1) * LANES] = ref[row : row + 1, :].astype(jnp.int32)
            for n, name in enumerate(("blend", "tile")):
                row = parcel.at[name].start + side * patches + p
                patch_rows[2 * patches * n + k : 2 * patches * n + k + 1, :] = own[pl.ds(row, 1), :]
    for n, name in enumerate(("left", "right")):
        shared[:, n * LANES : (n + 1) * LANES] = own[parcel.at[name], :].astype(jnp.int32)
    elements[...] = own[parcel.at["elements"], :].astype(jnp.int32)
    grad[...] = own[parcel.at["grad"], : grad.shape[1]]
    quad[...] = own[parcel.at["quad"], : quad.shape[1]]
    modulus[...] = own[parcel.at["modulus"], :]
    picked = nodes.pick(table[...], ids[...])
    blend_tiles(picked, patch_rows, matrices, pack)


BLOCK = 4


def block_ids(ids, step):
    return jnp.concatenate([ids[pl.ds(step * BLOCK + k, 1), :] for k in range(BLOCK)], axis=1)


def stress_kernel(nodes, table, ids, modulus, quad, grad, force, cat, disp):
    local, elems = ids.shape
    n = nodes.rows
    pieces = split(table[...], 2)
    cat[:, :LANES] = pieces[0]
    cat[:, LANES:] = pieces[1]

    def gather(step, carry):
        nid = block_ids(ids, step)
        onehot = nodes.lane_onehot(nid)
        rows = dot(cat[...], jnp.concatenate([onehot, onehot], axis=0), NN)
        mask = nodes.row_mask(nodes.rows_of(nid))
        for c in range(2):
            got = jnp.sum(jnp.where(mask, rows[c * n : (c + 1) * n], 0.0), axis=0, keepdims=True)
            for k in range(BLOCK):
                disp[pl.ds(c * local + step * BLOCK + k, 1), :] = got[:, k * elems : (k + 1) * elems]
        return carry

    lax.fori_loop(0, local // BLOCK, gather, 0)
    g = grad[...]
    half = g.shape[0] // 2
    gx = dot(g, disp[:local], NN, HIGHEST)
    gy = dot(g, disp[local:], NN, HIGHEST)
    exx = gx[:half]
    eyy = gy[half:]
    exy = 0.5 * (gx[half:] + gy[:half])
    stiffen = 1.0 + exx * exx + eyy * eyy + 2.0 * exy * exy
    weights = jnp.broadcast_to(quad[...], (half, half))
    eye = lax.broadcasted_iota(jnp.int32, (half, half), 0) == lax.broadcasted_iota(
        jnp.int32, (half, half), 1
    )
    column = jnp.sum(jnp.where(eye, weights, 0.0), axis=1, keepdims=True)
    scaled = modulus[...] * column * stiffen
    trace = exx + eyy
    s_xx = scaled * (trace + 2.0 * exx)
    s_yy = scaled * (trace + 2.0 * eyy)
    s_xy = scaled * 2.0 * exy
    gt = g.T
    fx = dot(gt, jnp.concatenate([s_xx, s_xy], axis=0), NN, HIGHEST)
    fy = dot(gt, jnp.concatenate([s_xy, s_yy], axis=0), NN, HIGHEST)
    both = jnp.concatenate([fx, fy], axis=0)
    high = both.astype(bf16).astype(f32)
    force[0] = high
    force[1] = both - high


def assembly_kernel(nodes, ids, force, out):
    local, _ = ids.shape
    out[...] = jnp.zeros_like(out)

    def scatter(step, carry):
        nid = block_ids(ids, step)
        mask = nodes.row_mask(nodes.rows_of(nid))
        onehot = nodes.lane_onehot(nid)
        parts = []
        for part in range(2):
            comps = []
            for c in range(2):
                rows = [
                    force[part, pl.ds(c * local + step * BLOCK + k, 1), :] for k in range(BLOCK)
                ]
                comps.append(jnp.where(mask, jnp.concatenate(rows, axis=1), 0.0))
            parts.append(jnp.concatenate(comps, axis=0).astype(bf16))
        out[...] += dot(
            jnp.concatenate(parts, axis=1), jnp.concatenate([onehot, onehot], axis=1), NT
        )
        return carry

    lax.fori_loop(0, local // BLOCK, scatter, 0)


def gather_tiles(own, left, right, ext):
    tiles = own.shape[0]
    for k, ref in enumerate((left, own, right)):
        for t in range(tiles):
            tile = ref[t]
            ext[k * tiles + t] = jnp.concatenate(
                [tile[0:2], tile[0:2] + tile[2:4], tile[4:8]], axis=0
            )


CHUNK = 16


def pair_terms(x0, x1, y0, y1, far):
    o0 = far[0:1] - x0
    o1 = far[1:2] - x1
    d0 = far[2:3] - y0
    d1 = far[3:4] - y1
    rest_sq = o0 * o0 + o1 * o1
    rest_core = rest_sq + core_sq
    rest_len = rest_core * lax.rsqrt(rest_core)
    length_sq = (d0 * d0 + d1 * d1) + core_sq
    length = length_sq * lax.rsqrt(length_sq)
    stretch = length - rest_len
    bell = jnp.exp(rest_sq * (-1.0 / horizon_sq))
    soft = 1.0 + stretch * stretch * (1.0 / stretch_scale**2)
    return d0, d1, rest_core, rest_len, length, stretch, bell, soft


def dilatation_kernel(fam_own, fam_par, live, own, left, right, out, ext, cols, sums):
    rank = lax.axis_index("blk")
    tiles = own.shape[0]
    dev, slots = fam_own.shape
    gather_tiles(own, left, right, ext)
    ones = jnp.ones((8, LANES), f32)
    out[...] = jnp.zeros_like(out)
    for t in range(tiles):
        side, index = divmod(t, dev)
        tile = (rank if side == 0 else 1 - rank) * dev + index
        fam = fam_own if side == 0 else fam_par

        @pl.when(tile < live[0])
        def _():
            me = ext[tiles + tile]
            turned = me.T
            for q in range(4):
                cols[q] = jnp.broadcast_to(turned[:, q : q + 1], (LANES, LANES))
            fars = [ext[fam[index, s]] for s in range(slots)]

            def chunk(i, carry):
                at = pl.multiple_of(i * CHUNK, CHUNK)
                x0, x1, u0, u1 = [cols[q, pl.ds(at, CHUNK), :] for q in range(4)]
                vol = jnp.zeros((CHUNK, LANES), f32)
                dil = jnp.zeros((CHUNK, LANES), f32)
                for far in fars:
                    _, _, rest_core, rest_len, _, stretch, bell, soft = pair_terms(x0, x1, u0, u1, far)
                    influence = bell * pl.reciprocal(soft)
                    vol = vol + influence * rest_core
                    dil = dil + influence * rest_len * stretch
                sums[pl.ds(at, CHUNK), :] = vol
                sums[pl.ds(LANES + at, CHUNK), :] = dil
                return carry

            lax.fori_loop(0, LANES // CHUNK, chunk, 0)
            total = dot(ones, sums[...], NT, HIGHEST)
            volume = total[:1, :LANES]
            theta = 2.0 * total[:1, LANES:] / volume
            k = me[6:7]
            scale = 4.0 * k / volume
            out[pl.ds(tile, 1), :] = 2.0 * k * theta / volume - scale * (0.5 * theta)
            out[pl.ds(tiles + tile, 1), :] = scale


def bond_kernel(fam_own, fam_par, live, own, left, right, bonds, own_sums, ext, cols, sums):
    rank = lax.axis_index("blk")
    tiles = own.shape[0]
    dev, slots = fam_own.shape
    gather_tiles(own, left, right, ext)
    ones = jnp.ones((8, LANES), f32)
    for t in range(tiles):
        side, index = divmod(t, dev)
        tile = (rank if side == 0 else 1 - rank) * dev + index
        fam = fam_own if side == 0 else fam_par

        @pl.when(tile < live[0])
        def _():
            turned = ext[tiles + tile].T
            for q in range(4):
                cols[q] = jnp.broadcast_to(turned[:, q : q + 1], (LANES, LANES))
            fars = [ext[fam[index, s]] for s in range(slots)]

            def chunk(i, carry):
                at = pl.multiple_of(i * CHUNK, CHUNK)
                x0, x1, u0, u1 = [cols[q, pl.ds(at, CHUNK), :] for q in range(4)]
                acc = [jnp.zeros((CHUNK, LANES), f32)] * 4
                for s, far in enumerate(fars):
                    d0, d1, _, rest_len, length, stretch, bell, soft = pair_terms(x0, x1, u0, u1, far)
                    over = bell * pl.reciprocal(soft * length)
                    by_rest = over * rest_len
                    by_stretch = over * stretch
                    terms = [by_rest * d0, by_rest * d1, by_stretch * d0, by_stretch * d1]
                    for q, term in enumerate(terms):
                        bonds[tile, s, q, pl.ds(at, CHUNK), :] = term
                    acc = [a + term for a, term in zip(acc, terms)]
                for q in range(4):
                    sums[pl.ds(q * LANES + at, CHUNK), :] = acc[q]
                return carry

            lax.fori_loop(0, LANES // CHUNK, chunk, 0)
            total = dot(ones, sums[...], NT, HIGHEST)
            for q in range(4):
                own_sums[tile, q : q + 1, :] = total[:1, q * LANES : (q + 1) * LANES]


def force_kernel(
    nodes, last, fam_own, fam_par, live, pack, ac, ac_left, ac_right, bonds, own_sums,
    el_own, el_par, ids, matrices, patch_rows, shared, *refs,
):
    if last:
        nodal, low, high, disp_out, vel_out, ext, sums, held = refs
    else:
        nodal, low, high, state, ext, sums, held = refs
    rank = lax.axis_index("blk")
    tiles = pack.shape[0]
    dev, slots = fam_own.shape
    for k, ref in enumerate((ac_left, ac, ac_right)):
        for t in range(tiles):
            ext[k * tiles + t, 0:1, :] = ref[t : t + 1, :]
            ext[k * tiles + t, 1:2, :] = ref[tiles + t : tiles + t + 1, :]
    ones = jnp.ones((8, LANES), f32)
    held[...] = jnp.zeros_like(held)
    for t in range(tiles):
        side, index = divmod(t, dev)
        tile = (rank if side == 0 else 1 - rank) * dev + index
        fam = fam_own if side == 0 else fam_par

        @pl.when(tile < live[0])
        def _():
            me = pack[tile]
            mine = ext[tiles + tile]
            fars = [ext[fam[index, s]] for s in range(slots)]

            def chunk(i, carry):
                at = pl.multiple_of(i * CHUNK, CHUNK)
                f = [jnp.zeros((CHUNK, LANES), f32)] * 2
                for s, far in enumerate(fars):
                    w = [bonds[tile, s, q, pl.ds(at, CHUNK), :] for q in range(4)]
                    f = [f[c] + (w[c] * far[0:1] + w[2 + c] * far[1:2]) for c in range(2)]
                for c in range(2):
                    sums[pl.ds(c * LANES + at, CHUNK), :] = f[c]
                return carry

            lax.fori_loop(0, LANES // CHUNK, chunk, 0)
            total = dot(ones, sums[...], NT, HIGHEST)
            far_part = jnp.concatenate([total[:1, :LANES], total[:1, LANES:]], axis=0)
            near = own_sums[tile]
            force = (near[0:2] * mine[0:1] + near[2:4] * mine[1:2]) + far_part
            vel = me[4:6] + me[7:8] * force
            disp = me[2:4] + time_step * vel
            held[tile, 0:2, :] = force
            held[tile, 2:4, :] = disp
            held[tile, 4:6, :] = vel

    if last:
        for t in range(dev):
            disp_out[t] = held[rank * dev + t, 2:4, :]
            vel_out[t] = held[rank * dev + t, 4:6, :]
    else:
        for t in range(tiles):
            mine = pack[t]
            now = held[t]
            state[t] = jnp.concatenate([mine[0:2], now[2:6], mine[6:8]], axis=0)
    patches = matrices.shape[0]
    reactions = []
    for k in range(patches):
        chosen = patch_rows[patches + k : patches + k + 1, :]
        force = jnp.zeros((2, LANES), f32)
        for t in range(tiles):
            force = force + jnp.where(chosen == float(t), held[t, 0:2, :], 0.0)
        weighted = force * patch_rows[k : k + 1, :]
        rows = jnp.concatenate([weighted, jnp.zeros((6, LANES), f32)], axis=0)
        reactions.append(dot(rows, matrices[k], NN, HIGHEST))
    react = jnp.concatenate(reactions, axis=1)
    total = nodes.spread([react[0:1], react[1:2]], ids[...]) - (el_own[...] + el_par[...])
    nodal[...] = total
    picked = nodes.pick(total, shared[...])
    for ref, at in ((low, 0), (high, LANES)):
        ref[...] = jnp.concatenate(
            [picked[0][:, at : at + LANES], picked[1][:, at : at + LANES], jnp.zeros((6, LANES), f32)],
            axis=0,
        )


def add_border(nodes, total, shared, from_low, from_high):
    dom = lax.axis_index("dom")
    ends = lax.axis_size("dom") - 1
    low = jnp.where(dom > 0, from_low[...], 0.0)
    high = jnp.where(dom < ends, from_high[...], 0.0)
    rows = jnp.concatenate([low, high], axis=1)
    return total + nodes.spread([rows[0:1], rows[1:2]], shared)


def update_kernel(
    nodes, nodal, table, vel, step, from_low, from_high, shared, ids, matrices, patch_rows, state,
    table_out, vel_out, pack,
):
    force = add_border(nodes, nodal[...], shared[...], from_low, from_high)
    steps = step[...]
    now = vel[...] + jnp.concatenate([steps, steps], axis=0) * force
    vel_out[...] = now
    disp = table[...] + time_step * now
    table_out[...] = disp
    pack[...] = state[...]
    picked = nodes.pick(disp, ids[...])
    blend_tiles(picked, patch_rows, matrices, pack)


def final_kernel(
    nodes, nodal, table, vel, step, from_low, from_high, shared, disp_out, vel_out, f_s, v_s,
):
    rank = lax.axis_index("blk")
    force = add_border(nodes, nodal[...], shared[...], from_low, from_high)
    steps = step[...]
    now = vel[...] + jnp.concatenate([steps, steps], axis=0) * force
    v_s[...] = now
    f_s[...] = table[...] + time_step * now
    for out, held in ((disp_out, f_s), (vel_out, v_s)):
        for c in range(2):
            at = pl.multiple_of(c * nodes.rows + rank * nodes.half, 8)
            rows = held[pl.ds(at, nodes.half), :]
            for i in range(nodes.rows_dev):
                out[c : c + 1, i * LANES : (i + 1) * LANES] = rows[i : i + 1]


def call(kernel, outs, scalars, arrays, scratch=(), flops=0, vmem=4, spec=VM):
    size = sum(a.size * 4 for a in arrays) + sum(o.size * 4 for o in outs)
    return pl.pallas_call(
        kernel,
        out_shape=list(outs),
        in_specs=[SM] * len(scalars) + [spec] * len(arrays),
        out_specs=[VM] * len(outs),
        scratch_shapes=list(scratch),
        cost_estimate=pl.CostEstimate(flops=flops, bytes_accessed=size, transcendentals=0),
        compiler_params=pltpu.CompilerParams(vmem_limit_bytes=int(vmem * 2**20)),
    )(*scalars, *arrays)


def shape(*dims, dtype=f32):
    return jax.ShapeDtypeStruct(dims, dtype)


def shards(
    pd_disp, pd_vel, pd_coord, pd_modulus, pd_step, family_tile_lists, live_tiles, patch_tile,
    patch_blend, patch_nodes, patch_matrix, fe_disp, fe_vel, fe_step, fe_modulus, element_nodes,
    shape_grad, quad_weight, shared_left, shared_right,
):
    doms = lax.axis_size("dom")
    dev = pd_disp.shape[0]
    tiles = 2 * dev
    patches = patch_matrix.shape[0]
    slots = family_tile_lists.shape[1]
    nodes = Nodes(fe_disp.shape[1])
    n2 = 2 * nodes.rows
    local, elems = element_nodes.shape

    def swap(x):
        return lax.ppermute(x, "blk", [(0, 1), (1, 0)])

    def up(x):
        return lax.ppermute(x, "dom", [(i, (i + 1) % doms) for i in range(doms)])

    def down(x):
        return lax.ppermute(x, "dom", [((i + 1) % doms, i) for i in range(doms)])

    given = [
        patch_matrix, patch_nodes, fe_disp, pd_coord, pd_disp, pd_vel, pd_modulus, pd_step, fe_vel,
        fe_step.reshape(-1, LANES), shared_left, shared_right, element_nodes,
        shape_grad.reshape(-1, local), quad_weight[None, :], fe_modulus[None, :], patch_blend,
        patch_tile,
    ]
    spaces = [pltpu.VMEM] * (len(given) - 1) + [pltpu.SMEM]
    parcel = Parcel(nodes, dev, patches, local)
    (own,) = call(
        functools.partial(pack_kernel, nodes, parcel, len(given)),
        [shape(parcel.rows, LANES)],
        [], given,
        [space(x.shape, x.dtype) for space, x in zip(spaces, given)]
        + [pltpu.SemaphoreType.DMA((len(given),))],
        spec=HBM,
        vmem=63,
    )
    partner = swap(own)
    fam_par = swap(family_tile_lists)
    lists = [family_tile_lists, fam_par, live_tiles]
    int32 = jnp.int32
    table, vel, step, pack, matrices, ids, shared, patch_rows, elements, grad, quad, modulus = call(
        functools.partial(start_kernel, nodes, parcel),
        [
            shape(n2, LANES), shape(n2, LANES), shape(nodes.rows, LANES), shape(tiles, 8, LANES),
            shape(2 * patches, LANES, LANES), shape(1, 2 * patches * LANES, dtype=int32),
            shape(1, 2 * LANES, dtype=int32), shape(4 * patches, LANES),
            shape(local, elems, dtype=int32), shape(2 * local, local), shape(1, local), shape(1, elems),
        ],
        [],
        [own, partner],
    )
    for section in range(2):
        last = section == 1
        packs = [pack, up(pack), down(pack)]
        (force_el,) = call(
            functools.partial(stress_kernel, nodes),
            [shape(2, 2 * local, elems)],
            [],
            [table, elements, modulus, quad, grad],
            [pltpu.VMEM((n2, 2 * LANES), bf16), pltpu.VMEM((2 * local, elems), f32)],
            flops=10**9, vmem=8,
        )
        (ac,) = call(
            dilatation_kernel,
            [shape(2 * tiles, LANES)],
            lists,
            packs,
            [
                pltpu.VMEM((3 * tiles, 8, LANES), f32),
                pltpu.VMEM((4, LANES, LANES), f32),
                pltpu.VMEM((2 * LANES, LANES), f32),
            ],
        )
        acs = [ac, up(ac), down(ac)]
        (el_own,) = call(
            functools.partial(assembly_kernel, nodes),
            [shape(n2, LANES)],
            [],
            [elements, force_el],
            flops=10**9, vmem=8,
        )
        el_par = swap(el_own)
        bonds, own_sums = call(
            bond_kernel,
            [shape(tiles, slots, 4, LANES, LANES), shape(tiles, 8, LANES)],
            lists,
            packs,
            [
                pltpu.VMEM((3 * tiles, 8, LANES), f32),
                pltpu.VMEM((4, LANES, LANES), f32),
                pltpu.VMEM((4 * LANES, LANES), f32),
            ],
            vmem=8,
        )
        outs = [shape(n2, LANES), shape(8, LANES), shape(8, LANES)]
        if last:
            outs += [shape(dev, 2, LANES)] * 2
        else:
            outs += [shape(tiles, 8, LANES)]
        nodal, low, high, *rest = call(
            functools.partial(force_kernel, nodes, last),
            outs,
            lists,
            [
                pack, *acs, bonds, own_sums, el_own, el_par, ids, matrices, patch_rows,
                shared,
            ],
            [
                pltpu.VMEM((3 * tiles, 8, LANES), f32),
                pltpu.VMEM((2 * LANES, LANES), f32),
                pltpu.VMEM((tiles, 8, LANES), f32),
            ],
            vmem=8,
        )
        from_low, from_high = up(high), down(low)
        if not last:
            table, vel, pack = call(
                functools.partial(update_kernel, nodes),
                [shape(n2, LANES), shape(n2, LANES), shape(tiles, 8, LANES)],
                [],
                [
                    nodal, table, vel, step, from_low, from_high, shared, ids, matrices,
                    patch_rows, rest[0],
                ],
            )
        else:
            pd_disp, pd_vel = rest
            fe_disp, fe_vel = call(
                functools.partial(final_kernel, nodes),
                [shape(*fe_disp.shape)] * 2,
                [],
                [nodal, table, vel, step, from_low, from_high, shared],
                [pltpu.VMEM((n2, LANES), f32)] * 2,
            )
    return (pd_disp, pd_vel, fe_disp, fe_vel)


def solution(mesh):
    return jax.shard_map(
        shards,
        mesh=mesh,
        in_specs=(
            P(("dom", "blk"), None, None),
            P(("dom", "blk"), None, None),
            P(("dom", "blk"), None, None),
            P(("dom", "blk"), None),
            P(("dom", "blk"), None),
            P(("dom", "blk"), None),
            P("dom"),
            P("dom"),
            P("dom", None),
            P(("dom", "blk"), None),
            P(("dom", "blk"), None, None),
            P(None, ("dom", "blk")),
            P(None, ("dom", "blk")),
            P(("dom", "blk")),
            P(("dom", "blk")),
            P(None, ("dom", "blk")),
            P(),
            P(),
            P("dom", None),
            P("dom", None),
        ),
        out_specs=(
            P(("dom", "blk"), None, None),
            P(("dom", "blk"), None, None),
            P(None, ("dom", "blk")),
            P(None, ("dom", "blk")),
        ),
        check_vma=False,
    )
```

time: 123 us -> 97.1 us (0.79)
  local copies, waits for them, and re-layouts: 11.8 us -> 0.98 us
  Pallas kernels: 51.2 us -> 45.1 us
  starting transfers between devices: 32.9 us -> 28.8 us
  waiting for transfers between devices: 23.1 us -> 20.6 us
    unnamed x70 -> x4, local copies, waits for them, and re-layouts: 7.77 us -> 0.98 us
    pallas_call x9 -> x14, Pallas kernels: 51.2 us -> 45.1 us  [call(): pl.pallas_call(kernel, out_shape=list(outs), in_specs=[SM] * len(scalars)...]
    ppermute x6, starting transfers between devices: 28 us -> 23.6 us  [down(): return lax.ppermute(x, 'dom', [((i + 1) % doms, i) for i in range(doms)])]
    reshape x9 -> x0, local copies, waits for them, and re-layouts: 2.54 us -> none  [the longest x5 1.57 us: flat(): return x.reshape(-1, 2, LANES).transpose(1, 0, 2).reshape(2, -1)]
    ppermute x6, waiting for transfers between devices: 4.17 us -> 1.73 us  [down(): return lax.ppermute(x, 'dom', [((i + 1) % doms, i) for i in range(doms)])]
    ppermute x6, starting transfers between devices: 2.09 us -> 4.11 us  [up(): return lax.ppermute(x, 'dom', [(i, (i + 1) % doms) for i in range(doms)])]
    ppermute x6, waiting for transfers between devices: 18.9 us -> 17 us  [up(): return lax.ppermute(x, 'dom', [(i, (i + 1) % doms) for i in range(doms)])]
    ppermute x9 -> x4, waiting for transfers between devices: 0.02 us -> 1.89 us  [swap(): return lax.ppermute(x, 'blk', [(0, 1), (1, 0)])]
  transfers between devices with their start and end apart: 21 -> 16, of which waited for: 8 -> 10; matrix products, arithmetic and copies ran while one was open for 3% -> 0% of each run, Pallas kernels for 22% -> 17%
where the time goes in v2:
time: 97.1 us; the launch traced here: 96.9 us
  Pallas kernels  45.1 us (46%)
  starting transfers between devices  28.8 us (30%)
  waiting for transfers between devices  20.6 us (21%)
  between operations  1.4 us (1%)
  local copies, waits for them, and re-layouts  0.98 us (1%)
    pallas_call x14, Pallas kernels, call(): pl.pallas_call(kernel, out_shape=list(outs), in_specs=[SM] * len(scalars)...  45.1 us
    ppermute x6, starting transfers between devices, down(): return lax.ppermute(x, 'dom', [((i + 1) % doms, i) for i in range(doms)])  23.6 us
    ppermute x6, waiting for transfers between devices, up(): return lax.ppermute(x, 'dom', [(i, (i + 1) % doms) for i in range(doms)])  17 us
    ppermute x6, starting transfers between devices, up(): return lax.ppermute(x, 'dom', [(i, (i + 1) % doms) for i in range(doms)])  4.11 us
  transfers between devices with their start and end apart: 16, of which 10 were waited for; matrix products, arithmetic and copies ran while one was open for 0% of the time, Pallas kernels for 17%

profile of v2, /device:TPU:0, one launch (start us, length us, event | category | flops | bytes accessed | tf_op | source)
XLA Modules:
  0.0 96.9 jit_solution(6252547855547058476)
XLA Ops:
  0.6 2.0 %shard_map.219.own = f32[632,128]{1,0:T(8,128)} custom-call(f32[1,128,128]{2,1,0:T(8,128)} %refs_0_.1, s32[1,128]{1,0:T(1,128)} %refs_1_.1, f32[2,6400]{1,0:T(2,128)} %refs_2_.1, f32[2,2,128]{2,1,0:T(2,128)} %refs_3_.1, f32[2,2,128]{2,1,0:T(2,128)} %refs_4_.1, f32[2,2,128]{2,1,0:T(2,128)} %refs_5_.1, f32[2,128]{1,0:T(2,128)} %refs_6_.1, f32[2,128]{1,0:T(2,128)} %refs_7_.1, ...), custom_call_target="tpu_custom_call" | custom-call | bytes 594064 | tf_op jit(solution)/shard_map/pallas_call | solution.py:505
  2.7 0.6 collective-permute-start.1
  3.2 1.5 %collective-permute-done.1.partner = f32[632,128]{1,0:T(8,128)S(1)} collective-permute-done((f32[632,128]{1,0:T(8,128)}, f32[632,128]{1,0:T(8,128)S(1)}, u32[]{:S(2)}, u32[]{:S(2)}) %collective-permute-start.1) | collective-permute-done | bytes 323616 | tf_op jit(solution)/shard_map/ppermute | solution.py:535
  4.7 1.0 %copy-done = f32[632,128]{1,0:T(8,128)S(1)} copy-done((f32[632,128]{1,0:T(8,128)S(1)}, f32[632,128]{1,0:T(8,128)}, u32[]{:S(2)}) %copy-start) | copy-done | bytes 323608
  5.7 0.5 shard_map.220
  6.2 4.5 %shard_map.223.force = f32[2,128,128]{2,1,0:T(8,128)S(1)} custom-call(f32[224,128]{1,0:T(8,128)S(1)} %get-tuple-element.38.table, s32[64,128]{1,0:T(8,128)S(1)} %get-tuple-element.37.ids, f32[1,128]{1,0:T(1,128)S(1)} %get-tuple-element.39.modulus, f32[1,64]{1,0:T(1,128)S(1)} %get-tuple-element.40.quad, f32[128,64]{1,0:T(8,128)S(1)} %get-tuple-element.41.grad), custom_call_target="tpu_custom_call" | custom-call | flops 1000000000 | bytes 312064 | tf_op jit(solution)/shard_map/pallas_call | solution.py:505
  10.8 5.0 %shard_map.224.el_own = f32[224,128]{1,0:T(8,128)S(1)} custom-call(s32[64,128]{1,0:T(8,128)S(1)} %get-tuple-element.37.ids, f32[2,128,128]{2,1,0:T(8,128)S(1)} %shard_map.223.force), custom_call_target="tpu_custom_call" | custom-call | flops 1000000000 | bytes 278528 | tf_op jit(solution)/shard_map/pallas_call | solution.py:505
  15.8 0.4 collective-permute-start.6
  16.2 6.6 %collective-permute-start.3 = (f32[4,8,128]{2,1,0:T(8,128)S(1)}, f32[4,8,128]{2,1,0:T(8,128)S(1)}, u32[]{:S(2)}, u32[]{:S(2)}) collective-permute-start(f32[4,8,128]{2,1,0:T(8,128)S(1)} %get-tuple-element.34.own.pack), channel_id=1, source_target_pairs={{2,0},{4,2},{6,4},{8,6},{10,8},{12,10},{14,12},{16,14},{18,16},{20... | collective-permute-start | bytes 49160 | tf_op jit(solution)/shard_map/ppermute | solution.py:541
  23.6 0.4 collective-permute-done.fam_par
  24.3 5.9 %collective-permute-done.2.left = f32[4,8,128]{2,1,0:T(8,128)S(1)} collective-permute-done((f32[4,8,128]{2,1,0:T(8,128)S(1)}, f32[4,8,128]{2,1,0:T(8,128)S(1)}, u32[]{:S(2)}, u32[]{:S(2)}) %collective-permute-start.2) | collective-permute-done | bytes 16416 | tf_op jit(solution)/shard_map/ppermute | solution.py:538
  30.2 3.8 %shard_map.221.ac = f32[8,128]{1,0:T(8,128)S(1)} custom-call(s32[2,3]{1,0:T(2,128)S(1)} %copy-done.1, s32[2,3]{1,0:T(2,128)S(1)} %collective-permute-done.fam_par, s32[1]{0:T(128)S(6)} %copy.24.live, f32[4,8,128]{2,1,0:T(8,128)S(1)} %get-tuple-element.34.own.pack, f32[4,8,128]{2,1,0:T(8,128)S(1)} %collective-permute-done.2.left, ...), custom_call_target="tpu_custom_call" | custom-call | bytes 53248 | tf_op jit(solution)/shard_map/pallas_call | solution.py:505
  34.0 2.0 %collective-permute-start.4 = (f32[8,128]{1,0:T(8,128)S(1)}, f32[8,128]{1,0:T(8,128)S(1)}, u32[]{:S(2)}, u32[]{:S(2)}) collective-permute-start(f32[8,128]{1,0:T(8,128)S(1)} %shard_map.221.ac), channel_id=1, source_target_pairs={{0,2},{2,4},{4,6},{6,8},{8,10},{10,12},{12,14},{14,16},{16,18},{18... | collective-permute-start | bytes 12296 | tf_op jit(solution)/shard_map/ppermute | solution.py:538
  36.0 4.2 %shard_map.222 = (f32[4,3,4,128,128]{4,3,2,1,0:T(8,128)S(1)}, f32[4,8,128]{2,1,0:T(8,128)S(1)}) custom-call(s32[2,3]{1,0:T(2,128)S(1)} %copy-done.1, s32[2,3]{1,0:T(2,128)S(1)} %collective-permute-done.fam_par, s32[1]{0:T(128)S(6)} %copy.24.live, f32[4,8,128]{2,1,0:T(8,128)S(1)} %get-tuple-element.34.own.pack, f32[4,8,128]{2,1,0:T(8,128)S(1)} %collective-permute-done.2.left, ...), custom_call_target="tpu_custom_call" | custom-call | bytes 3211264 | tf_op jit(solution)/shard_map/pallas_call | solution.py:505
  40.2 1.0 %collective-permute-done.4.ac_left = f32[8,128]{1,0:T(8,128)S(1)} collective-permute-done((f32[8,128]{1,0:T(8,128)S(1)}, f32[8,128]{1,0:T(8,128)S(1)}, u32[]{:S(2)}, u32[]{:S(2)}) %collective-permute-start.4) | collective-permute-done | bytes 4128 | tf_op jit(solution)/shard_map/ppermute | solution.py:538
  41.3 2.6 %shard_map.225 = (f32[224,128]{1,0:T(8,128)S(1)}, f32[8,128]{1,0:T(8,128)S(1)}, f32[8,128]{1,0:T(8,128)S(1)}, f32[4,8,128]{2,1,0:T(8,128)S(1)}) custom-call(s32[2,3]{1,0:T(2,128)S(1)} %copy-done.1, s32[2,3]{1,0:T(2,128)S(1)} %collective-permute-done.fam_par, s32[1]{0:T(128)S(6)} %copy.24.live, f32[4,8,128]{2,1,0:T(8,128)S(1)} %get-tuple-element.34.own.pack, ...), custom_call_target="tpu_custom_call" | custom-call | bytes 3694592 | tf_op jit(solution)/shard_map/pallas_call | solution.py:505
  43.9 5.6 %collective-permute-start.8 = (f32[8,128]{1,0:T(8,128)S(1)}, f32[8,128]{1,0:T(8,128)S(1)}, u32[]{:S(2)}, u32[]{:S(2)}) collective-permute-start(f32[8,128]{1,0:T(8,128)S(1)} %get-tuple-element.50), channel_id=1, source_target_pairs={{2,0},{4,2},{6,4},{8,6},{10,8},{12,10},{14,12},{16,14},{18,16},{20... | collective-permute-start | bytes 12296 | tf_op jit(solution)/shard_map/ppermute | solution.py:541
  49.5 1.6 %collective-permute-done.7.from_low = f32[8,128]{1,0:T(8,128)S(1)} collective-permute-done((f32[8,128]{1,0:T(8,128)S(1)}, f32[8,128]{1,0:T(8,128)S(1)}, u32[]{:S(2)}, u32[]{:S(2)}) %collective-permute-start.7) | collective-permute-done | bytes 4128 | tf_op jit(solution)/shard_map/ppermute | solution.py:538
  51.1 0.8 shard_map.226
  51.9 4.5 %shard_map.229.force = f32[2,128,128]{2,1,0:T(8,128)S(1)} custom-call(f32[224,128]{1,0:T(8,128)S(1)} %get-tuple-element.55.table, s32[64,128]{1,0:T(8,128)S(1)} %get-tuple-element.37.ids, f32[1,128]{1,0:T(1,128)S(1)} %get-tuple-element.39.modulus, f32[1,64]{1,0:T(1,128)S(1)} %get-tuple-element.40.quad, f32[128,64]{1,0:T(8,128)S(1)} %get-tuple-element.41.grad), custom_call_target="tpu_custom_call" | custom-call | flops 1000000000 | bytes 312064 | tf_op jit(solution)/shard_map/pallas_call | solution.py:505
  56.5 5.0 %shard_map.230.el_own = f32[224,128]{1,0:T(8,128)S(1)} custom-call(s32[64,128]{1,0:T(8,128)S(1)} %get-tuple-element.37.ids, f32[2,128,128]{2,1,0:T(8,128)S(1)} %shard_map.229.force), custom_call_target="tpu_custom_call" | custom-call | flops 1000000000 | bytes 278528 | tf_op jit(solution)/shard_map/pallas_call | solution.py:505
  61.6 5.7 %collective-permute-start.10 = (f32[4,8,128]{2,1,0:T(8,128)S(1)}, f32[4,8,128]{2,1,0:T(8,128)S(1)}, u32[]{:S(2)}, u32[]{:S(2)}) collective-permute-start(f32[4,8,128]{2,1,0:T(8,128)S(1)} %get-tuple-element.52.own.pack), channel_id=1, source_target_pairs={{2,0},{4,2},{6,4},{8,6},{10,8},{12,10},{14,12},{16,14},{18,16},{20... | collective-permute-start | bytes 49160 | tf_op jit(solution)/shard_map/ppermute | solution.py:541
  67.3 1.4 %collective-permute-done.10.right = f32[4,8,128]{2,1,0:T(8,128)S(1)} collective-permute-done((f32[4,8,128]{2,1,0:T(8,128)S(1)}, f32[4,8,128]{2,1,0:T(8,128)S(1)}, u32[]{:S(2)}, u32[]{:S(2)}) %collective-permute-start.10) | collective-permute-done | bytes 16416 | tf_op jit(solution)/shard_map/ppermute | solution.py:541
  68.7 5.9 %collective-permute-done.9.left = f32[4,8,128]{2,1,0:T(8,128)S(1)} collective-permute-done((f32[4,8,128]{2,1,0:T(8,128)S(1)}, f32[4,8,128]{2,1,0:T(8,128)S(1)}, u32[]{:S(2)}, u32[]{:S(2)}) %collective-permute-start.9) | collective-permute-done | bytes 16416 | tf_op jit(solution)/shard_map/ppermute | solution.py:538
  74.6 3.8 %shard_map.227.ac = f32[8,128]{1,0:T(8,128)S(1)} custom-call(s32[2,3]{1,0:T(2,128)S(1)} %copy-done.1, s32[2,3]{1,0:T(2,128)S(1)} %collective-permute-done.fam_par, s32[1]{0:T(128)S(6)} %copy.24.live, f32[4,8,128]{2,1,0:T(8,128)S(1)} %get-tuple-element.52.own.pack, f32[4,8,128]{2,1,0:T(8,128)S(1)} %collective-permute-done.9.left, ...), custom_call_target="tpu_custom_call" | custom-call | bytes 53248 | tf_op jit(solution)/shard_map/pallas_call | solution.py:505
  78.4 2.0 %collective-permute-start.11 = (f32[8,128]{1,0:T(8,128)S(1)}, f32[8,128]{1,0:T(8,128)S(1)}, u32[]{:S(2)}, u32[]{:S(2)}) collective-permute-start(f32[8,128]{1,0:T(8,128)S(1)} %shard_map.227.ac), channel_id=1, source_target_pairs={{0,2},{2,4},{4,6},{6,8},{8,10},{10,12},{12,14},{14,16},{16,18},{18... | collective-permute-start | bytes 12296 | tf_op jit(solution)/shard_map/ppermute | solution.py:538
  80.5 4.2 %shard_map.228 = (f32[4,3,4,128,128]{4,3,2,1,0:T(8,128)S(1)}, f32[4,8,128]{2,1,0:T(8,128)S(1)}) custom-call(s32[2,3]{1,0:T(2,128)S(1)} %copy-done.1, s32[2,3]{1,0:T(2,128)S(1)} %collective-permute-done.fam_par, s32[1]{0:T(128)S(6)} %copy.24.live, f32[4,8,128]{2,1,0:T(8,128)S(1)} %get-tuple-element.52.own.pack, f32[4,8,128]{2,1,0:T(8,128)S(1)} %collective-permute-done.9.left, ...), custom_call_target="tpu_custom_call" | custom-call | bytes 3211264 | tf_op jit(solution)/shard_map/pallas_call | solution.py:505
  84.7 1.0 %collective-permute-done.11.ac_left = f32[8,128]{1,0:T(8,128)S(1)} collective-permute-done((f32[8,128]{1,0:T(8,128)S(1)}, f32[8,128]{1,0:T(8,128)S(1)}, u32[]{:S(2)}, u32[]{:S(2)}) %collective-permute-start.11) | collective-permute-done | bytes 4128 | tf_op jit(solution)/shard_map/ppermute | solution.py:538
  85.7 3.0 %shard_map.231 = (f32[224,128]{1,0:T(8,128)S(1)}, f32[8,128]{1,0:T(8,128)S(1)}, f32[8,128]{1,0:T(8,128)S(1)}, f32[2,2,128]{2,1,0:T(2,128)}, f32[2,2,128]{2,1,0:T(2,128)}) custom-call(s32[2,3]{1,0:T(2,128)S(1)} %copy-done.1, s32[2,3]{1,0:T(2,128)S(1)} %collective-permute-done.fam_par, s32[1]{0:T(128)S(6)} %copy.24.live, ...), custom_call_target="tpu_custom_call" | custom-call | bytes 3682304 | tf_op jit(solution)/shard_map/pallas_call | solution.py:505
  88.7 5.6 %collective-permute-start.15 = (f32[8,128]{1,0:T(8,128)S(1)}, f32[8,128]{1,0:T(8,128)S(1)}, u32[]{:S(2)}, u32[]{:S(2)}) collective-permute-start(f32[8,128]{1,0:T(8,128)S(1)} %get-tuple-element.61), channel_id=1, source_target_pairs={{2,0},{4,2},{6,4},{8,6},{10,8},{12,10},{14,12},{16,14},{18,16},{20... | collective-permute-start | bytes 12296 | tf_op jit(solution)/shard_map/ppermute | solution.py:541
  94.3 1.6 %collective-permute-done.14.from_low = f32[8,128]{1,0:T(8,128)S(1)} collective-permute-done((f32[8,128]{1,0:T(8,128)S(1)}, f32[8,128]{1,0:T(8,128)S(1)}, u32[]{:S(2)}, u32[]{:S(2)}) %collective-permute-start.14) | collective-permute-done | bytes 4128 | tf_op jit(solution)/shard_map/ppermute | solution.py:538
  95.9 1.0 shard_map.232
  (18 shorter events, 0.6 us)
Async XLA Ops:
  2.7 2.0 %collective-permute-start.1 = (f32[632,128]{1,0:T(8,128)}, f32[632,128]{1,0:T(8,128)S(1)}, u32[]{:S(2)}, u32[]{:S(2)}) collective-permute-start(f32[632,128]{1,0:T(8,128)} %shard_map.219.own), channel_id=1, source_target_pairs={{0,1},{1,0},{2,3},{3,2},{4,5},{5,4},{6,7},{7,6},{8,9},{9,8},{10,11... | collective-permute-start | bytes 970760 | tf_op jit(solution)/shard_map/ppermute | solution.py:535
  4.7 1.0 %copy-start = (f32[632,128]{1,0:T(8,128)S(1)}, f32[632,128]{1,0:T(8,128)}, u32[]{:S(2)}) copy-start(f32[632,128]{1,0:T(8,128)} %shard_map.219.own) | copy-start | bytes 970756
  6.2 16.6 %copy-start.1 = (s32[2,3]{1,0:T(2,128)S(1)}, s32[2,3]{1,0:T(2,128)}, u32[]{:S(2)}) copy-start(s32[2,3]{1,0:T(2,128)} %fam_own.11) | copy-start | bytes 76
  15.8 25.5 %collective-permute-start.6 = (f32[224,128]{1,0:T(8,128)S(1)}, f32[224,128]{1,0:T(8,128)S(1)}, u32[]{:S(2)}, u32[]{:S(2)}) collective-permute-start(f32[224,128]{1,0:T(8,128)S(1)} %shard_map.224.el_own), channel_id=1, source_target_pairs={{0,1},{1,0},{2,3},{3,2},{4,5},{5,4},{6,7},{7,6},{8,9},{9,8},{10,11... | collective-permute-start | bytes 344072 | tf_op jit(solution)/shard_map/ppermute | solution.py:535
  16.2 8.0 %collective-permute-start.3 = (f32[4,8,128]{2,1,0:T(8,128)S(1)}, f32[4,8,128]{2,1,0:T(8,128)S(1)}, u32[]{:S(2)}, u32[]{:S(2)}) collective-permute-start(f32[4,8,128]{2,1,0:T(8,128)S(1)} %get-tuple-element.34.own.pack), channel_id=1, source_target_pairs={{2,0},{4,2},{6,4},{8,6},{10,8},{12,10},{14,12},{16,14},{18,16},{20... | collective-permute-start | bytes 49160 | tf_op jit(solution)/shard_map/ppermute | solution.py:541
  22.8 7.3 %collective-permute-start.2 = (f32[4,8,128]{2,1,0:T(8,128)S(1)}, f32[4,8,128]{2,1,0:T(8,128)S(1)}, u32[]{:S(2)}, u32[]{:S(2)}) collective-permute-start(f32[4,8,128]{2,1,0:T(8,128)S(1)} %get-tuple-element.34.own.pack), channel_id=1, source_target_pairs={{0,2},{2,4},{4,6},{6,8},{8,10},{10,12},{12,14},{14,16},{16,18},{18... | collective-permute-start | bytes 49160 | tf_op jit(solution)/shard_map/ppermute | solution.py:538
  22.8 1.2 %collective-permute-start = (s32[2,3]{1,0:T(2,128)S(1)}, s32[2,3]{1,0:T(2,128)S(1)}, u32[]{:S(2)}, u32[]{:S(2)}) collective-permute-start(s32[2,3]{1,0:T(2,128)S(1)} %copy-done.1), channel_id=1, source_target_pairs={{0,1},{1,0},{2,3},{3,2},{4,5},{5,4},{6,7},{7,6},{8,9},{9,8},{10,11... | collective-permute-start | bytes 80 | tf_op jit(solution)/shard_map/ppermute | solution.py:535
  34.0 6.3 %collective-permute-start.5 = (f32[8,128]{1,0:T(8,128)S(1)}, f32[8,128]{1,0:T(8,128)S(1)}, u32[]{:S(2)}, u32[]{:S(2)}) collective-permute-start(f32[8,128]{1,0:T(8,128)S(1)} %shard_map.221.ac), channel_id=1, source_target_pairs={{2,0},{4,2},{6,4},{8,6},{10,8},{12,10},{14,12},{16,14},{18,16},{20... | collective-permute-start | bytes 12296 | tf_op jit(solution)/shard_map/ppermute | solution.py:541
  34.0 7.3 %collective-permute-start.4 = (f32[8,128]{1,0:T(8,128)S(1)}, f32[8,128]{1,0:T(8,128)S(1)}, u32[]{:S(2)}, u32[]{:S(2)}) collective-permute-start(f32[8,128]{1,0:T(8,128)S(1)} %shard_map.221.ac), channel_id=1, source_target_pairs={{0,2},{2,4},{4,6},{6,8},{8,10},{10,12},{12,14},{14,16},{16,18},{18... | collective-permute-start | bytes 12296 | tf_op jit(solution)/shard_map/ppermute | solution.py:538
  43.9 7.3 %collective-permute-start.7 = (f32[8,128]{1,0:T(8,128)S(1)}, f32[8,128]{1,0:T(8,128)S(1)}, u32[]{:S(2)}, u32[]{:S(2)}) collective-permute-start(f32[8,128]{1,0:T(8,128)S(1)} %get-tuple-element.49), channel_id=1, source_target_pairs={{0,2},{2,4},{4,6},{6,8},{8,10},{10,12},{12,14},{14,16},{16,18},{18... | collective-permute-start | bytes 12296 | tf_op jit(solution)/shard_map/ppermute | solution.py:538
  43.9 7.2 %collective-permute-start.8 = (f32[8,128]{1,0:T(8,128)S(1)}, f32[8,128]{1,0:T(8,128)S(1)}, u32[]{:S(2)}, u32[]{:S(2)}) collective-permute-start(f32[8,128]{1,0:T(8,128)S(1)} %get-tuple-element.50), channel_id=1, source_target_pairs={{2,0},{4,2},{6,4},{8,6},{10,8},{12,10},{14,12},{16,14},{18,16},{20... | collective-permute-start | bytes 12296 | tf_op jit(solution)/shard_map/ppermute | solution.py:541
  61.5 24.2 %collective-permute-start.13 = (f32[224,128]{1,0:T(8,128)S(1)}, f32[224,128]{1,0:T(8,128)S(1)}, u32[]{:S(2)}, u32[]{:S(2)}) collective-permute-start(f32[224,128]{1,0:T(8,128)S(1)} %shard_map.230.el_own), channel_id=1, source_target_pairs={{0,1},{1,0},{2,3},{3,2},{4,5},{5,4},{6,7},{7,6},{8,9},{9,8},{10,11... | collective-permute-start | bytes 344072 | tf_op jit(solution)/shard_map/ppermute | solution.py:535
  61.6 7.1 %collective-permute-start.10 = (f32[4,8,128]{2,1,0:T(8,128)S(1)}, f32[4,8,128]{2,1,0:T(8,128)S(1)}, u32[]{:S(2)}, u32[]{:S(2)}) collective-permute-start(f32[4,8,128]{2,1,0:T(8,128)S(1)} %get-tuple-element.52.own.pack), channel_id=1, source_target_pairs={{2,0},{4,2},{6,4},{8,6},{10,8},{12,10},{14,12},{16,14},{18,16},{20... | collective-permute-start | bytes 49160 | tf_op jit(solution)/shard_map/ppermute | solution.py:541
  67.3 7.3 %collective-permute-start.9 = (f32[4,8,128]{2,1,0:T(8,128)S(1)}, f32[4,8,128]{2,1,0:T(8,128)S(1)}, u32[]{:S(2)}, u32[]{:S(2)}) collective-permute-start(f32[4,8,128]{2,1,0:T(8,128)S(1)} %get-tuple-element.52.own.pack), channel_id=1, source_target_pairs={{0,2},{2,4},{4,6},{6,8},{8,10},{10,12},{12,14},{14,16},{16,18},{18... | collective-permute-start | bytes 49160 | tf_op jit(solution)/shard_map/ppermute | solution.py:538
  78.4 6.3 %collective-permute-start.12 = (f32[8,128]{1,0:T(8,128)S(1)}, f32[8,128]{1,0:T(8,128)S(1)}, u32[]{:S(2)}, u32[]{:S(2)}) collective-permute-start(f32[8,128]{1,0:T(8,128)S(1)} %shard_map.227.ac), channel_id=1, source_target_pairs={{2,0},{4,2},{6,4},{8,6},{10,8},{12,10},{14,12},{16,14},{18,16},{20... | collective-permute-start | bytes 12296 | tf_op jit(solution)/shard_map/ppermute | solution.py:541
  78.4 7.3 %collective-permute-start.11 = (f32[8,128]{1,0:T(8,128)S(1)}, f32[8,128]{1,0:T(8,128)S(1)}, u32[]{:S(2)}, u32[]{:S(2)}) collective-permute-start(f32[8,128]{1,0:T(8,128)S(1)} %shard_map.227.ac), channel_id=1, source_target_pairs={{0,2},{2,4},{4,6},{6,8},{8,10},{10,12},{12,14},{14,16},{16,18},{18... | collective-permute-start | bytes 12296 | tf_op jit(solution)/shard_map/ppermute | solution.py:538
  88.7 7.2 %collective-permute-start.14 = (f32[8,128]{1,0:T(8,128)S(1)}, f32[8,128]{1,0:T(8,128)S(1)}, u32[]{:S(2)}, u32[]{:S(2)}) collective-permute-start(f32[8,128]{1,0:T(8,128)S(1)} %get-tuple-element.60), channel_id=1, source_target_pairs={{0,2},{2,4},{4,6},{6,8},{8,10},{10,12},{12,14},{14,16},{16,18},{18... | collective-permute-start | bytes 12296 | tf_op jit(solution)/shard_map/ppermute | solution.py:538
  88.7 7.2 %collective-permute-start.15 = (f32[8,128]{1,0:T(8,128)S(1)}, f32[8,128]{1,0:T(8,128)S(1)}, u32[]{:S(2)}, u32[]{:S(2)}) collective-permute-start(f32[8,128]{1,0:T(8,128)S(1)} %get-tuple-element.61), channel_id=1, source_target_pairs={{2,0},{4,2},{6,4},{8,6},{10,8},{12,10},{14,12},{16,14},{18,16},{20... | collective-permute-start | bytes 12296 | tf_op jit(solution)/shard_map/ppermute | solution.py:541

commit v3 on v2

--- a/solution.py
+++ b/solution.py
@@ -54,6 +54,18 @@
         lane = ids & (LANES - 1)
         hit = lax.broadcasted_iota(jnp.int32, (LANES, ids.shape[1]), 0) == lane
         return jnp.where(hit, 1.0, 0.0).astype(bf16)
+
+    def wide_rows(self, table):
+        half = [table[pl.ds(k, self.rows, stride=2), :] for k in range(2)]
+        return jnp.concatenate(half, axis=1)
+
+    def wide_masks(self, ids):
+        row = self.rows_of(ids)
+        lane = ((row & 1) << 7) | (ids & (LANES - 1))
+        count = ids.shape[1]
+        mask = lax.broadcasted_iota(jnp.int32, (self.rows // 2, count), 0) == row >> 1
+        hit = lax.broadcasted_iota(jnp.int32, (2 * LANES, count), 0) == lane
+        return mask, jnp.where(hit, 1.0, 0.0).astype(bf16)
 
     def pick(self, table, ids, parts=3):
         pieces = jnp.concatenate(split(table, parts), axis=1)
@@ -188,32 +200,32 @@
     blend_tiles(picked, patch_rows, matrices, pack)
 
 
-BLOCK = 4
-
-
-def block_ids(ids, step):
-    return jnp.concatenate([ids[pl.ds(step * BLOCK + k, 1), :] for k in range(BLOCK)], axis=1)
+GATHER_BLOCK = 16
+ASSEMBLY_BLOCK = 32
+
+
+def block_ids(ids, step, block):
+    return jnp.concatenate([ids[pl.ds(step * block + k, 1), :] for k in range(block)], axis=1)
 
 
 def stress_kernel(nodes, table, ids, modulus, quad, grad, force, cat, disp):
     local, elems = ids.shape
-    n = nodes.rows
-    pieces = split(table[...], 2)
-    cat[:, :LANES] = pieces[0]
-    cat[:, LANES:] = pieces[1]
+    n = nodes.rows // 2
+    n2 = nodes.rows
+    block = GATHER_BLOCK
+    cat[...] = jnp.concatenate(split(nodes.wide_rows(table), 2), axis=0)
 
     def gather(step, carry):
-        nid = block_ids(ids, step)
-        onehot = nodes.lane_onehot(nid)
-        rows = dot(cat[...], jnp.concatenate([onehot, onehot], axis=0), NN)
-        mask = nodes.row_mask(nodes.rows_of(nid))
+        mask, onehot = nodes.wide_masks(block_ids(ids, step, block))
+        both = dot(cat[...], onehot, NN)
+        rows = both[:n2] + both[n2:]
         for c in range(2):
             got = jnp.sum(jnp.where(mask, rows[c * n : (c + 1) * n], 0.0), axis=0, keepdims=True)
-            for k in range(BLOCK):
-                disp[pl.ds(c * local + step * BLOCK + k, 1), :] = got[:, k * elems : (k + 1) * elems]
+            for k in range(block):
+                disp[pl.ds(c * local + step * block + k, 1), :] = got[:, k * elems : (k + 1) * elems]
         return carry
 
-    lax.fori_loop(0, local // BLOCK, gather, 0)
+    lax.fori_loop(0, local // block, gather, 0)
     g = grad[...]
     half = g.shape[0] // 2
     gx = dot(g, disp[:local], NN, HIGHEST)
@@ -241,42 +253,46 @@
     force[1] = both - high
 
 
-def assembly_kernel(nodes, ids, force, out):
+def assembly_kernel(nodes, ids, force, out, acc):
     local, _ = ids.shape
-    out[...] = jnp.zeros_like(out)
+    n2 = nodes.rows
+    block = ASSEMBLY_BLOCK
+    acc[...] = jnp.zeros_like(acc)
 
     def scatter(step, carry):
-        nid = block_ids(ids, step)
-        mask = nodes.row_mask(nodes.rows_of(nid))
-        onehot = nodes.lane_onehot(nid)
-        parts = []
+        mask, onehot = nodes.wide_masks(block_ids(ids, step, block))
+        placed = []
         for part in range(2):
-            comps = []
             for c in range(2):
                 rows = [
-                    force[part, pl.ds(c * local + step * BLOCK + k, 1), :] for k in range(BLOCK)
+                    force[part, pl.ds(c * local + step * block + k, 1), :] for k in range(block)
                 ]
-                comps.append(jnp.where(mask, jnp.concatenate(rows, axis=1), 0.0))
-            parts.append(jnp.concatenate(comps, axis=0).astype(bf16))
-        out[...] += dot(
-            jnp.concatenate(parts, axis=1), jnp.concatenate([onehot, onehot], axis=1), NT
-        )
+                placed.append(jnp.where(mask, jnp.concatenate(rows, axis=1), 0.0))
+        both = dot(jnp.concatenate(placed, axis=0).astype(bf16), onehot, NT)
+        acc[...] += both[:n2] + both[n2:]
         return carry
 
-    lax.fori_loop(0, local // BLOCK, scatter, 0)
-
-
-def gather_tiles(own, left, right, ext):
+    lax.fori_loop(0, local // block, scatter, 0)
+    for k in range(2):
+        out[pl.ds(k, nodes.rows, stride=2), :] = acc[:, k * LANES : (k + 1) * LANES]
+
+
+def side_of(order):
+    odd = lax.rem(lax.axis_index("dom"), 2)
+    return 2 * (1 - odd) if order == 0 else 2 * odd
+
+
+def gather_tiles(own, even, odd, ext):
     tiles = own.shape[0]
-    for k, ref in enumerate((left, own, right)):
+    for place, ref in ((side_of(0), even), (1, own), (side_of(1), odd)):
         for t in range(tiles):
             tile = ref[t]
-            ext[k * tiles + t] = jnp.concatenate(
+            ext[place * tiles + t] = jnp.concatenate(
                 [tile[0:2], tile[0:2] + tile[2:4], tile[4:8]], axis=0
             )
 
 
-CHUNK = 16
+CHUNK = 64
 
 
 def pair_terms(x0, x1, y0, y1, far):
@@ -295,139 +311,143 @@
     return d0, d1, rest_core, rest_len, length, stretch, bell, soft
 
 
-def dilatation_kernel(fam_own, fam_par, live, own, left, right, out, ext, cols, sums):
+def own_columns(own, ext, cols):
+    tiles = own.shape[0]
+    turned = jnp.concatenate([ext[tiles + t] for t in range(tiles)], axis=0).T
+    for t in range(tiles):
+        for q in range(4):
+            at = 8 * t + q
+            cols[4 * t + q] = jnp.broadcast_to(turned[:, at : at + 1], (LANES, LANES))
+
+
+def each_live_tile(fam_own, fam_par, live, body):
     rank = lax.axis_index("blk")
+    dev, slots = fam_own.shape
+    for side, fam in ((rank, fam_own), (1 - rank, fam_par)):
+        for index in range(dev):
+            tile = side * dev + index
+            pl.when(tile < live[0])(
+                functools.partial(body, tile, [fam[index, s] for s in range(slots)])
+            )
+
+
+def dilatation_kernel(fam_own, fam_par, live, own, even, odd, out, ext, cols, sums):
     tiles = own.shape[0]
-    dev, slots = fam_own.shape
-    gather_tiles(own, left, right, ext)
-    ones = jnp.ones((8, LANES), f32)
-    out[...] = jnp.zeros_like(out)
+    gather_tiles(own, even, odd, ext)
+    own_columns(own, ext, cols)
+
+    def body(tile, names):
+        fars = [ext[name] for name in names]
+
+        def chunk(i, carry):
+            at = pl.multiple_of(i * CHUNK, CHUNK)
+            x0, x1, u0, u1 = [cols[4 * tile + q, pl.ds(at, CHUNK), :] for q in range(4)]
+            vol = jnp.zeros((CHUNK, LANES), f32)
+            dil = jnp.zeros((CHUNK, LANES), f32)
+            for far in fars:
+                _, _, rest_core, rest_len, _, stretch, bell, soft = pair_terms(x0, x1, u0, u1, far)
+                influence = bell * pl.reciprocal(soft)
+                vol = vol + influence * rest_core
+                dil = dil + influence * rest_len * stretch
+            sums[tile, 0, pl.ds(at, CHUNK), :] = vol
+            sums[tile, 1, pl.ds(at, CHUNK), :] = dil
+            return carry
+
+        lax.fori_loop(0, LANES // CHUNK, chunk, 0)
+
+    each_live_tile(fam_own, fam_par, live, body)
+    total = dot(jnp.ones((8, LANES), f32), sums[...].reshape(2 * tiles * LANES, LANES), NT, HIGHEST)
+    parts = [total[:1, n * LANES : (n + 1) * LANES] for n in range(2 * tiles)]
+    volume = jnp.concatenate(parts[0::2], axis=0)
+    theta = 2.0 * jnp.concatenate(parts[1::2], axis=0) / volume
+    k = jnp.concatenate([own[t, 6:7, :] for t in range(tiles)], axis=0)
+    scale = 4.0 * k / volume
+    alpha = 2.0 * k * theta / volume - scale * (0.5 * theta)
+    alive = lax.broadcasted_iota(jnp.int32, (tiles, LANES), 0) < live[0]
+    out[:tiles, :] = jnp.where(alive, alpha, 0.0)
+    out[tiles:, :] = jnp.where(alive, scale, 0.0)
+
+
+def bond_kernel(fam_own, fam_par, live, own, even, odd, bonds, own_sums, ext, cols, sums):
+    tiles = own.shape[0]
+    gather_tiles(own, even, odd, ext)
+    own_columns(own, ext, cols)
+
+    def body(tile, names):
+        fars = [ext[name] for name in names]
+
+        def chunk(i, carry):
+            at = pl.multiple_of(i * CHUNK, CHUNK)
+            x0, x1, u0, u1 = [cols[4 * tile + q, pl.ds(at, CHUNK), :] for q in range(4)]
+            acc = [jnp.zeros((CHUNK, LANES), f32)] * 4
+            for s, far in enumerate(fars):
+                d0, d1, _, rest_len, length, stretch, bell, soft = pair_terms(x0, x1, u0, u1, far)
+                over = bell * pl.reciprocal(soft * length)
+                by_rest = over * rest_len
+                by_stretch = over * stretch
+                terms = [by_rest * d0, by_rest * d1, by_stretch * d0, by_stretch * d1]
+                for q, term in enumerate(terms):
+                    bonds[tile, s, q, pl.ds(at, CHUNK), :] = term
+                acc = [a + term for a, term in zip(acc, terms)]
+            for q in range(4):
+                sums[tile, q, pl.ds(at, CHUNK), :] = acc[q]
+            return carry
+
+        lax.fori_loop(0, LANES // CHUNK, chunk, 0)
+
+    each_live_tile(fam_own, fam_par, live, body)
+    total = dot(jnp.ones((8, LANES), f32), sums[...].reshape(4 * tiles * LANES, LANES), NT, HIGHEST)
     for t in range(tiles):
-        side, index = divmod(t, dev)
-        tile = (rank if side == 0 else 1 - rank) * dev + index
-        fam = fam_own if side == 0 else fam_par
-
-        @pl.when(tile < live[0])
-        def _():
-            me = ext[tiles + tile]
-            turned = me.T
-            for q in range(4):
-                cols[q] = jnp.broadcast_to(turned[:, q : q + 1], (LANES, LANES))
-            fars = [ext[fam[index, s]] for s in range(slots)]
-
-            def chunk(i, carry):
-                at = pl.multiple_of(i * CHUNK, CHUNK)
-                x0, x1, u0, u1 = [cols[q, pl.ds(at, CHUNK), :] for q in range(4)]
-                vol = jnp.zeros((CHUNK, LANES), f32)
-                dil = jnp.zeros((CHUNK, LANES), f32)
-                for far in fars:
-                    _, _, rest_core, rest_len, _, stretch, bell, soft = pair_terms(x0, x1, u0, u1, far)
-                    influence = bell * pl.reciprocal(soft)
-                    vol = vol + influence * rest_core
-                    dil = dil + influence * rest_len * stretch
-                sums[pl.ds(at, CHUNK), :] = vol
-                sums[pl.ds(LANES + at, CHUNK), :] = dil
-                return carry
-
-            lax.fori_loop(0, LANES // CHUNK, chunk, 0)
-            total = dot(ones, sums[...], NT, HIGHEST)
-            volume = total[:1, :LANES]
-            theta = 2.0 * total[:1, LANES:] / volume
-            k = me[6:7]
-            scale = 4.0 * k / volume
-            out[pl.ds(tile, 1), :] = 2.0 * k * theta / volume - scale * (0.5 * theta)
-            out[pl.ds(tiles + tile, 1), :] = scale
-
-
-def bond_kernel(fam_own, fam_par, live, own, left, right, bonds, own_sums, ext, cols, sums):
-    rank = lax.axis_index("blk")
-    tiles = own.shape[0]
-    dev, slots = fam_own.shape
-    gather_tiles(own, left, right, ext)
-    ones = jnp.ones((8, LANES), f32)
-    for t in range(tiles):
-        side, index = divmod(t, dev)
-        tile = (rank if side == 0 else 1 - rank) * dev + index
-        fam = fam_own if side == 0 else fam_par
-
-        @pl.when(tile < live[0])
-        def _():
-            turned = ext[tiles + tile].T
-            for q in range(4):
-                cols[q] = jnp.broadcast_to(turned[:, q : q + 1], (LANES, LANES))
-            fars = [ext[fam[index, s]] for s in range(slots)]
-
-            def chunk(i, carry):
-                at = pl.multiple_of(i * CHUNK, CHUNK)
-                x0, x1, u0, u1 = [cols[q, pl.ds(at, CHUNK), :] for q in range(4)]
-                acc = [jnp.zeros((CHUNK, LANES), f32)] * 4
-                for s, far in enumerate(fars):
-                    d0, d1, _, rest_len, length, stretch, bell, soft = pair_terms(x0, x1, u0, u1, far)
-                    over = bell * pl.reciprocal(soft * length)
-                    by_rest = over * rest_len
-                    by_stretch = over * stretch
-                    terms = [by_rest * d0, by_rest * d1, by_stretch * d0, by_stretch * d1]
-                    for q, term in enumerate(terms):
-                        bonds[tile, s, q, pl.ds(at, CHUNK), :] = term
-                    acc = [a + term for a, term in zip(acc, terms)]
-                for q in range(4):
-                    sums[pl.ds(q * LANES + at, CHUNK), :] = acc[q]
-                return carry
-
-            lax.fori_loop(0, LANES // CHUNK, chunk, 0)
-            total = dot(ones, sums[...], NT, HIGHEST)
-            for q in range(4):
-                own_sums[tile, q : q + 1, :] = total[:1, q * LANES : (q + 1) * LANES]
+        for q in range(4):
+            at = (4 * t + q) * LANES
+            own_sums[t, q : q + 1, :] = total[:1, at : at + LANES]
 
 
 def force_kernel(
-    nodes, last, fam_own, fam_par, live, pack, ac, ac_left, ac_right, bonds, own_sums,
+    nodes, last, fam_own, fam_par, live, pack, ac, ac_even, ac_odd, bonds, own_sums,
     el_own, el_par, ids, matrices, patch_rows, shared, *refs,
 ):
     if last:
-        nodal, low, high, disp_out, vel_out, ext, sums, held = refs
+        nodal, for_even, for_odd, disp_out, vel_out, ext, sums, held = refs
     else:
-        nodal, low, high, state, ext, sums, held = refs
+        nodal, for_even, for_odd, state, ext, sums, held = refs
     rank = lax.axis_index("blk")
     tiles = pack.shape[0]
-    dev, slots = fam_own.shape
-    for k, ref in enumerate((ac_left, ac, ac_right)):
+    dev, _ = fam_own.shape
+    for place, ref in ((side_of(0), ac_even), (1, ac), (side_of(1), ac_odd)):
         for t in range(tiles):
-            ext[k * tiles + t, 0:1, :] = ref[t : t + 1, :]
-            ext[k * tiles + t, 1:2, :] = ref[tiles + t : tiles + t + 1, :]
-    ones = jnp.ones((8, LANES), f32)
-    held[...] = jnp.zeros_like(held)
+            ext[place * tiles + t, 0:1, :] = ref[t : t + 1, :]
+            ext[place * tiles + t, 1:2, :] = ref[tiles + t : tiles + t + 1, :]
+
+    def body(tile, names):
+        fars = [ext[name] for name in names]
+
+        def chunk(i, carry):
+            at = pl.multiple_of(i * CHUNK, CHUNK)
+            f = [jnp.zeros((CHUNK, LANES), f32)] * 2
+            for s, far in enumerate(fars):
+                w = [bonds[tile, s, q, pl.ds(at, CHUNK), :] for q in range(4)]
+                f = [f[c] + (w[c] * far[0:1] + w[2 + c] * far[1:2]) for c in range(2)]
+            for c in range(2):
+                sums[tile, c, pl.ds(at, CHUNK), :] = f[c]
+            return carry
+
+        lax.fori_loop(0, LANES // CHUNK, chunk, 0)
+
+    each_live_tile(fam_own, fam_par, live, body)
+    total = dot(jnp.ones((8, LANES), f32), sums[...].reshape(2 * tiles * LANES, LANES), NT, HIGHEST)
     for t in range(tiles):
-        side, index = divmod(t, dev)
-        tile = (rank if side == 0 else 1 - rank) * dev + index
-        fam = fam_own if side == 0 else fam_par
-
-        @pl.when(tile < live[0])
-        def _():
-            me = pack[tile]
-            mine = ext[tiles + tile]
-            fars = [ext[fam[index, s]] for s in range(slots)]
-
-            def chunk(i, carry):
-                at = pl.multiple_of(i * CHUNK, CHUNK)
-                f = [jnp.zeros((CHUNK, LANES), f32)] * 2
-                for s, far in enumerate(fars):
-                    w = [bonds[tile, s, q, pl.ds(at, CHUNK), :] for q in range(4)]
-                    f = [f[c] + (w[c] * far[0:1] + w[2 + c] * far[1:2]) for c in range(2)]
-                for c in range(2):
-                    sums[pl.ds(c * LANES + at, CHUNK), :] = f[c]
-                return carry
-
-            lax.fori_loop(0, LANES // CHUNK, chunk, 0)
-            total = dot(ones, sums[...], NT, HIGHEST)
-            far_part = jnp.concatenate([total[:1, :LANES], total[:1, LANES:]], axis=0)
-            near = own_sums[tile]
-            force = (near[0:2] * mine[0:1] + near[2:4] * mine[1:2]) + far_part
-            vel = me[4:6] + me[7:8] * force
-            disp = me[2:4] + time_step * vel
-            held[tile, 0:2, :] = force
-            held[tile, 2:4, :] = disp
-            held[tile, 4:6, :] = vel
+        far_part = jnp.concatenate(
+            [total[:1, (2 * t + c) * LANES : (2 * t + c + 1) * LANES] for c in range(2)], axis=0
+        )
+        near = own_sums[t]
+        mine = ext[tiles + t]
+        me = pack[t]
+        force = (near[0:2] * mine[0:1] + near[2:4] * mine[1:2]) + far_part
+        vel = me[4:6] + me[7:8] * force
+        disp = me[2:4] + time_step * vel
+        alive = lax.broadcasted_iota(jnp.int32, (6, LANES), 0) * 0 + t < live[0]
+        held[t, 0:6, :] = jnp.where(alive, jnp.concatenate([force, disp, vel], axis=0), 0.0)
 
     if last:
         for t in range(dev):
@@ -452,27 +472,33 @@
     total = nodes.spread([react[0:1], react[1:2]], ids[...]) - (el_own[...] + el_par[...])
     nodal[...] = total
     picked = nodes.pick(total, shared[...])
-    for ref, at in ((low, 0), (high, LANES)):
-        ref[...] = jnp.concatenate(
+    low, high = [
+        jnp.concatenate(
             [picked[0][:, at : at + LANES], picked[1][:, at : at + LANES], jnp.zeros((6, LANES), f32)],
             axis=0,
         )
-
-
-def add_border(nodes, total, shared, from_low, from_high):
+        for at in (0, LANES)
+    ]
+    even_is_high = side_of(0) == 2
+    for_even[...] = jnp.where(even_is_high, high, low)
+    for_odd[...] = jnp.where(even_is_high, low, high)
+
+
+def add_border(nodes, total, shared, even, odd):
     dom = lax.axis_index("dom")
     ends = lax.axis_size("dom") - 1
-    low = jnp.where(dom > 0, from_low[...], 0.0)
-    high = jnp.where(dom < ends, from_high[...], 0.0)
+    even_is_high = side_of(0) == 2
+    low = jnp.where(dom > 0, jnp.where(even_is_high, odd[...], even[...]), 0.0)
+    high = jnp.where(dom < ends, jnp.where(even_is_high, even[...], odd[...]), 0.0)
     rows = jnp.concatenate([low, high], axis=1)
     return total + nodes.spread([rows[0:1], rows[1:2]], shared)
 
 
 def update_kernel(
-    nodes, nodal, table, vel, step, from_low, from_high, shared, ids, matrices, patch_rows, state,
+    nodes, nodal, table, vel, step, from_even, from_odd, shared, ids, matrices, patch_rows, state,
     table_out, vel_out, pack,
 ):
-    force = add_border(nodes, nodal[...], shared[...], from_low, from_high)
+    force = add_border(nodes, nodal[...], shared[...], from_even, from_odd)
     steps = step[...]
     now = vel[...] + jnp.concatenate([steps, steps], axis=0) * force
     vel_out[...] = now
@@ -484,10 +510,10 @@
 
 
 def final_kernel(
-    nodes, nodal, table, vel, step, from_low, from_high, shared, disp_out, vel_out, f_s, v_s,
+    nodes, nodal, table, vel, step, from_even, from_odd, shared, disp_out, vel_out, f_s, v_s,
 ):
     rank = lax.axis_index("blk")
-    force = add_border(nodes, nodal[...], shared[...], from_low, from_high)
+    force = add_border(nodes, nodal[...], shared[...], from_even, from_odd)
     steps = step[...]
     now = vel[...] + jnp.concatenate([steps, steps], axis=0) * force
     v_s[...] = now
@@ -534,11 +560,21 @@
     def swap(x):
         return lax.ppermute(x, "blk", [(0, 1), (1, 0)])
 
-    def up(x):
-        return lax.ppermute(x, "dom", [(i, (i + 1) % doms) for i in range(doms)])
-
-    def down(x):
-        return lax.ppermute(x, "dom", [((i + 1) % doms, i) for i in range(doms)])
+    def place(dom, core):
+        return 2 * dom + core
+
+    even_pairs, odd_pairs = [], []
+    for dom in range(doms):
+        for core in range(2):
+            other = dom - 1 if dom % 2 == 0 else dom + 1
+            even_pairs.append((place(dom, core), place(dom ^ 1, core)))
+            inside = 0 <= other < doms
+            odd_pairs.append((place(dom, core), place(other, core) if inside else place(dom, 1 - core)))
+
+    def exchange(for_even, for_odd):
+        from_even = lax.ppermute(for_even, ("dom", "blk"), even_pairs)
+        from_odd = lax.ppermute(for_odd, ("dom", "blk"), odd_pairs)
+        return from_even, from_odd
 
     given = [
         patch_matrix, patch_nodes, fe_disp, pd_coord, pd_disp, pd_vel, pd_modulus, pd_step, fe_vel,
@@ -574,14 +610,14 @@
     )
     for section in range(2):
         last = section == 1
-        packs = [pack, up(pack), down(pack)]
+        packs = [pack, *exchange(pack, pack)]
         (force_el,) = call(
             functools.partial(stress_kernel, nodes),
             [shape(2, 2 * local, elems)],
             [],
             [table, elements, modulus, quad, grad],
             [pltpu.VMEM((n2, 2 * LANES), bf16), pltpu.VMEM((2 * local, elems), f32)],
-            flops=10**9, vmem=8,
+            flops=10**9, vmem=16,
         )
         (ac,) = call(
             dilatation_kernel,
@@ -590,17 +626,18 @@
             packs,
             [
                 pltpu.VMEM((3 * tiles, 8, LANES), f32),
-                pltpu.VMEM((4, LANES, LANES), f32),
-                pltpu.VMEM((2 * LANES, LANES), f32),
+                pltpu.VMEM((4 * tiles, LANES, LANES), f32),
+                pltpu.VMEM((tiles, 2, LANES, LANES), f32),
             ],
         )
-        acs = [ac, up(ac), down(ac)]
+        acs = [ac, *exchange(ac, ac)]
         (el_own,) = call(
             functools.partial(assembly_kernel, nodes),
             [shape(n2, LANES)],
             [],
             [elements, force_el],
-            flops=10**9, vmem=8,
+            [pltpu.VMEM((nodes.rows, 2 * LANES), f32)],
+            flops=10**9, vmem=16,
         )
         el_par = swap(el_own)
         bonds, own_sums = call(
@@ -610,8 +647,8 @@
             packs,
             [
                 pltpu.VMEM((3 * tiles, 8, LANES), f32),
-                pltpu.VMEM((4, LANES, LANES), f32),
-                pltpu.VMEM((4 * LANES, LANES), f32),
+                pltpu.VMEM((4 * tiles, LANES, LANES), f32),
+                pltpu.VMEM((tiles, 4, LANES, LANES), f32),
             ],
             vmem=8,
         )
@@ -620,7 +657,7 @@
             outs += [shape(dev, 2, LANES)] * 2
         else:
             outs += [shape(tiles, 8, LANES)]
-        nodal, low, high, *rest = call(
+        nodal, for_even, for_odd, *rest = call(
             functools.partial(force_kernel, nodes, last),
             outs,
             lists,
@@ -630,19 +667,19 @@
             ],
             [
                 pltpu.VMEM((3 * tiles, 8, LANES), f32),
-                pltpu.VMEM((2 * LANES, LANES), f32),
+                pltpu.VMEM((tiles, 2, LANES, LANES), f32),
                 pltpu.VMEM((tiles, 8, LANES), f32),
             ],
             vmem=8,
         )
-        from_low, from_high = up(high), down(low)
+        from_even, from_odd = exchange(for_even, for_odd)
         if not last:
             table, vel, pack = call(
                 functools.partial(update_kernel, nodes),
                 [shape(n2, LANES), shape(n2, LANES), shape(tiles, 8, LANES)],
                 [],
                 [
-                    nodal, table, vel, step, from_low, from_high, shared, ids, matrices,
+                    nodal, table, vel, step, from_even, from_odd, shared, ids, matrices,
                     patch_rows, rest[0],
                 ],
             )
@@ -652,7 +689,7 @@
                 functools.partial(final_kernel, nodes),
                 [shape(*fe_disp.shape)] * 2,
                 [],
-                [nodal, table, vel, step, from_low, from_high, shared],
+                [nodal, table, vel, step, from_even, from_odd, shared],
                 [pltpu.VMEM((n2, LANES), f32)] * 2,
             )
     return (pd_disp, pd_vel, fe_disp, fe_vel)

time: 97.1 us -> 62.9 us (0.65)
  the two profiles are of different devices: /device:TPU:0 before, /device:TPU:16 now
where the time goes in v3:
time: 62.9 us; the launch traced here: 62.7 us
  Pallas kernels  28.1 us (45%)
  starting transfers between devices  16.5 us (26%)
  waiting for transfers between devices  15.7 us (25%)
  between operations  1.38 us (2%)
  local copies, waits for them, and re-layouts  0.98 us (2%)
    pallas_call x14, Pallas kernels, call(): pl.pallas_call(kernel, out_shape=list(outs), in_specs=[SM] * len(scalars)...  28.1 us
    ppermute x6, waiting for transfers between devices, exchange(): from_odd = lax.ppermute(for_odd, ('dom', 'blk'), odd_pairs)  12.3 us
    ppermute x6, starting transfers between devices, exchange(): from_odd = lax.ppermute(for_odd, ('dom', 'blk'), odd_pairs)  12.2 us
    ppermute x6, starting transfers between devices, exchange(): from_even = lax.ppermute(for_even, ('dom', 'blk'), even_pairs)  3.91 us
    ppermute x4, waiting for transfers between devices, swap(): return lax.ppermute(x, 'blk', [(0, 1), (1, 0)])  2.33 us
  transfers between devices with their start and end apart: 16, of which 12 were waited for; matrix products, arithmetic and copies ran while one was open for 0% of the time, Pallas kernels for 17%

profile of v3, /device:TPU:16, one launch (start us, length us, event | category | flops | bytes accessed | tf_op | source)
XLA Modules:
  0.0 62.7 jit_solution(13935688532025973829)
XLA Ops:
  0.6 2.0 %shard_map.219.own = f32[632,128]{1,0:T(8,128)} custom-call(f32[1,128,128]{2,1,0:T(8,128)} %refs_0_.1, s32[1,128]{1,0:T(1,128)} %refs_1_.1, f32[2,6400]{1,0:T(2,128)} %refs_2_.1, f32[2,2,128]{2,1,0:T(2,128)} %refs_3_.1, f32[2,2,128]{2,1,0:T(2,128)} %refs_4_.1, f32[2,2,128]{2,1,0:T(2,128)} %refs_5_.1, f32[2,128]{1,0:T(2,128)} %refs_6_.1, f32[2,128]{1,0:T(2,128)} %refs_7_.1, ...), custom_call_target="tpu_custom_call" | custom-call | bytes 594064 | tf_op jit(solution)/shard_map/pallas_call | solution.py:531
  2.7 1.8 %collective-permute-done.1.partner = f32[632,128]{1,0:T(8,128)S(1)} collective-permute-done((f32[632,128]{1,0:T(8,128)}, f32[632,128]{1,0:T(8,128)S(1)}, u32[]{:S(2)}, u32[]{:S(2)}) %collective-permute-start.1) | collective-permute-done | bytes 323616 | tf_op jit(solution)/shard_map/ppermute | solution.py:561
  4.6 1.0 %copy-done = f32[632,128]{1,0:T(8,128)S(1)} copy-done((f32[632,128]{1,0:T(8,128)S(1)}, f32[632,128]{1,0:T(8,128)}, u32[]{:S(2)}) %copy-start) | copy-done | bytes 323608
  5.5 0.5 shard_map.220
  6.1 2.5 %shard_map.223.force = f32[2,128,128]{2,1,0:T(8,128)S(1)} custom-call(f32[224,128]{1,0:T(8,128)S(1)} %get-tuple-element.38.table, s32[64,128]{1,0:T(8,128)S(1)} %get-tuple-element.37.ids, f32[1,128]{1,0:T(1,128)S(1)} %get-tuple-element.39.modulus, f32[1,64]{1,0:T(1,128)S(1)} %get-tuple-element.40.quad, f32[128,64]{1,0:T(8,128)S(1)} %get-tuple-element.41.grad), custom_call_target="tpu_custom_call" | custom-call | flops 1000000000 | bytes 312064 | tf_op jit(solution)/shard_map/pallas_call | solution.py:531
  8.6 1.8 %shard_map.224.el_own = f32[224,128]{1,0:T(8,128)S(1)} custom-call(s32[64,128]{1,0:T(8,128)S(1)} %get-tuple-element.37.ids, f32[2,128,128]{2,1,0:T(8,128)S(1)} %shard_map.223.force), custom_call_target="tpu_custom_call" | custom-call | flops 1000000000 | bytes 278528 | tf_op jit(solution)/shard_map/pallas_call | solution.py:531
  10.5 2.3 %collective-permute-start.3 = (f32[4,8,128]{2,1,0:T(8,128)S(1)}, f32[4,8,128]{2,1,0:T(8,128)S(1)}, u32[]{:S(2)}, u32[]{:S(2)}) collective-permute-start(f32[4,8,128]{2,1,0:T(8,128)S(1)} %get-tuple-element.34.own.pack), channel_id=1, source_target_pairs={{0,1},{1,0},{2,4},{3,5},{4,2},{5,3},{6,8},{7,9},{8,6},{9,7},{10,12... | collective-permute-start | bytes 49160 | tf_op jit(solution)/shard_map/ppermute | solution.py:576
  12.8 0.7 %collective-permute-start.2 = (f32[4,8,128]{2,1,0:T(8,128)S(1)}, f32[4,8,128]{2,1,0:T(8,128)S(1)}, u32[]{:S(2)}, u32[]{:S(2)}) collective-permute-start(f32[4,8,128]{2,1,0:T(8,128)S(1)} %get-tuple-element.34.own.pack), channel_id=1, source_target_pairs={{0,2},{1,3},{2,0},{3,1},{4,6},{5,7},{6,4},{7,5},{8,10},{9,11},{10,... | collective-permute-start | bytes 49160 | tf_op jit(solution)/shard_map/ppermute | solution.py:575
  14.2 0.5 collective-permute-done.fam_par
  14.7 1.4 %collective-permute-done.3.odd = f32[4,8,128]{2,1,0:T(8,128)S(1)} collective-permute-done((f32[4,8,128]{2,1,0:T(8,128)S(1)}, f32[4,8,128]{2,1,0:T(8,128)S(1)}, u32[]{:S(2)}, u32[]{:S(2)}) %collective-permute-start.3) | collective-permute-done | bytes 16416 | tf_op jit(solution)/shard_map/ppermute | solution.py:576
  16.1 0.5 collective-permute-done.2.even
  16.6 2.5 %shard_map.221.ac = f32[8,128]{1,0:T(8,128)S(1)} custom-call(s32[2,3]{1,0:T(2,128)S(1)} %copy-done.1, s32[2,3]{1,0:T(2,128)S(1)} %collective-permute-done.fam_par, s32[1]{0:T(128)S(6)} %copy.24.live, f32[4,8,128]{2,1,0:T(8,128)S(1)} %get-tuple-element.34.own.pack, f32[4,8,128]{2,1,0:T(8,128)S(1)} %collective-permute-done.2.even, ...), custom_call_target="tpu_custom_call" | custom-call | bytes 53248 | tf_op jit(solution)/shard_map/pallas_call | solution.py:531
  19.0 1.9 %collective-permute-start.5 = (f32[8,128]{1,0:T(8,128)S(1)}, f32[8,128]{1,0:T(8,128)S(1)}, u32[]{:S(2)}, u32[]{:S(2)}) collective-permute-start(f32[8,128]{1,0:T(8,128)S(1)} %shard_map.221.ac), channel_id=1, source_target_pairs={{0,1},{1,0},{2,4},{3,5},{4,2},{5,3},{6,8},{7,9},{8,6},{9,7},{10,12... | collective-permute-start | bytes 12296 | tf_op jit(solution)/shard_map/ppermute | solution.py:576
  21.2 3.0 %shard_map.222 = (f32[4,3,4,128,128]{4,3,2,1,0:T(8,128)S(1)}, f32[4,8,128]{2,1,0:T(8,128)S(1)}) custom-call(s32[2,3]{1,0:T(2,128)S(1)} %copy-done.1, s32[2,3]{1,0:T(2,128)S(1)} %collective-permute-done.fam_par, s32[1]{0:T(128)S(6)} %copy.24.live, f32[4,8,128]{2,1,0:T(8,128)S(1)} %get-tuple-element.34.own.pack, f32[4,8,128]{2,1,0:T(8,128)S(1)} %collective-permute-done.2.even, ...), custom_call_target="tpu_custom_call" | custom-call | bytes 3211264 | tf_op jit(solution)/shard_map/pallas_call | solution.py:531
  24.5 2.1 %shard_map.225 = (f32[224,128]{1,0:T(8,128)S(1)}, f32[8,128]{1,0:T(8,128)S(1)}, f32[8,128]{1,0:T(8,128)S(1)}, f32[4,8,128]{2,1,0:T(8,128)S(1)}) custom-call(s32[2,3]{1,0:T(2,128)S(1)} %copy-done.1, s32[2,3]{1,0:T(2,128)S(1)} %collective-permute-done.fam_par, s32[1]{0:T(128)S(6)} %copy.24.live, f32[4,8,128]{2,1,0:T(8,128)S(1)} %get-tuple-element.34.own.pack, ...), custom_call_target="tpu_custom_call" | custom-call | bytes 3694592 | tf_op jit(solution)/shard_map/pallas_call | solution.py:531
  26.6 1.5 %collective-permute-start.7 = (f32[8,128]{1,0:T(8,128)S(1)}, f32[8,128]{1,0:T(8,128)S(1)}, u32[]{:S(2)}, u32[]{:S(2)}) collective-permute-start(f32[8,128]{1,0:T(8,128)S(1)} %get-tuple-element.49), channel_id=1, source_target_pairs={{0,2},{1,3},{2,0},{3,1},{4,6},{5,7},{6,4},{7,5},{8,10},{9,11},{10,... | collective-permute-start | bytes 12296 | tf_op jit(solution)/shard_map/ppermute | solution.py:575
  28.1 2.0 %collective-permute-start.8 = (f32[8,128]{1,0:T(8,128)S(1)}, f32[8,128]{1,0:T(8,128)S(1)}, u32[]{:S(2)}, u32[]{:S(2)}) collective-permute-start(f32[8,128]{1,0:T(8,128)S(1)} %get-tuple-element.50), channel_id=1, source_target_pairs={{0,1},{1,0},{2,4},{3,5},{4,2},{5,3},{6,8},{7,9},{8,6},{9,7},{10,12... | collective-permute-start | bytes 12296 | tf_op jit(solution)/shard_map/ppermute | solution.py:576
  30.3 3.2 %collective-permute-done.8.from_odd = f32[8,128]{1,0:T(8,128)S(1)} collective-permute-done((f32[8,128]{1,0:T(8,128)S(1)}, f32[8,128]{1,0:T(8,128)S(1)}, u32[]{:S(2)}, u32[]{:S(2)}) %collective-permute-start.8) | collective-permute-done | bytes 4128 | tf_op jit(solution)/shard_map/ppermute | solution.py:576
  33.5 0.8 %shard_map.226 = (f32[224,128]{1,0:T(8,128)S(1)}, f32[224,128]{1,0:T(8,128)S(1)}, f32[4,8,128]{2,1,0:T(8,128)S(1)}) custom-call(f32[224,128]{1,0:T(8,128)S(1)} %get-tuple-element.46.nodal, f32[224,128]{1,0:T(8,128)S(1)} %get-tuple-element.38.table, f32[224,128]{1,0:T(8,128)S(1)} %get-tuple-element.47.vel, f32[112,128]{1,0:T(8,128)S(1)} %get-tuple-element.48.step, ...), custom_call_target="tpu_custom_call" | custom-call | bytes 806912 | tf_op jit(solution)/shard_map/pallas_call | solution.py:531
  34.3 2.5 %shard_map.229.force = f32[2,128,128]{2,1,0:T(8,128)S(1)} custom-call(f32[224,128]{1,0:T(8,128)S(1)} %get-tuple-element.55.table, s32[64,128]{1,0:T(8,128)S(1)} %get-tuple-element.37.ids, f32[1,128]{1,0:T(1,128)S(1)} %get-tuple-element.39.modulus, f32[1,64]{1,0:T(1,128)S(1)} %get-tuple-element.40.quad, f32[128,64]{1,0:T(8,128)S(1)} %get-tuple-element.41.grad), custom_call_target="tpu_custom_call" | custom-call | flops 1000000000 | bytes 312064 | tf_op jit(solution)/shard_map/pallas_call | solution.py:531
  36.8 1.8 %shard_map.230.el_own = f32[224,128]{1,0:T(8,128)S(1)} custom-call(s32[64,128]{1,0:T(8,128)S(1)} %get-tuple-element.37.ids, f32[2,128,128]{2,1,0:T(8,128)S(1)} %shard_map.229.force), custom_call_target="tpu_custom_call" | custom-call | flops 1000000000 | bytes 278528 | tf_op jit(solution)/shard_map/pallas_call | solution.py:531
  38.6 2.1 %collective-permute-start.10 = (f32[4,8,128]{2,1,0:T(8,128)S(1)}, f32[4,8,128]{2,1,0:T(8,128)S(1)}, u32[]{:S(2)}, u32[]{:S(2)}) collective-permute-start(f32[4,8,128]{2,1,0:T(8,128)S(1)} %get-tuple-element.52.own.pack), channel_id=1, source_target_pairs={{0,1},{1,0},{2,4},{3,5},{4,2},{5,3},{6,8},{7,9},{8,6},{9,7},{10,12... | collective-permute-start | bytes 49160 | tf_op jit(solution)/shard_map/ppermute | solution.py:576
  40.7 3.5 %collective-permute-done.10.odd = f32[4,8,128]{2,1,0:T(8,128)S(1)} collective-permute-done((f32[4,8,128]{2,1,0:T(8,128)S(1)}, f32[4,8,128]{2,1,0:T(8,128)S(1)}, u32[]{:S(2)}, u32[]{:S(2)}) %collective-permute-start.10) | collective-permute-done | bytes 16416 | tf_op jit(solution)/shard_map/ppermute | solution.py:576
  44.5 2.5 %shard_map.227.ac = f32[8,128]{1,0:T(8,128)S(1)} custom-call(s32[2,3]{1,0:T(2,128)S(1)} %copy-done.1, s32[2,3]{1,0:T(2,128)S(1)} %collective-permute-done.fam_par, s32[1]{0:T(128)S(6)} %copy.24.live, f32[4,8,128]{2,1,0:T(8,128)S(1)} %get-tuple-element.52.own.pack, f32[4,8,128]{2,1,0:T(8,128)S(1)} %collective-permute-done.9.even, ...), custom_call_target="tpu_custom_call" | custom-call | bytes 53248 | tf_op jit(solution)/shard_map/pallas_call | solution.py:531
  46.9 1.9 %collective-permute-start.12 = (f32[8,128]{1,0:T(8,128)S(1)}, f32[8,128]{1,0:T(8,128)S(1)}, u32[]{:S(2)}, u32[]{:S(2)}) collective-permute-start(f32[8,128]{1,0:T(8,128)S(1)} %shard_map.227.ac), channel_id=1, source_target_pairs={{0,1},{1,0},{2,4},{3,5},{4,2},{5,3},{6,8},{7,9},{8,6},{9,7},{10,12... | collective-permute-start | bytes 12296 | tf_op jit(solution)/shard_map/ppermute | solution.py:576
  48.9 3.0 %shard_map.228 = (f32[4,3,4,128,128]{4,3,2,1,0:T(8,128)S(1)}, f32[4,8,128]{2,1,0:T(8,128)S(1)}) custom-call(s32[2,3]{1,0:T(2,128)S(1)} %copy-done.1, s32[2,3]{1,0:T(2,128)S(1)} %collective-permute-done.fam_par, s32[1]{0:T(128)S(6)} %copy.24.live, f32[4,8,128]{2,1,0:T(8,128)S(1)} %get-tuple-element.52.own.pack, f32[4,8,128]{2,1,0:T(8,128)S(1)} %collective-permute-done.9.even, ...), custom_call_target="tpu_custom_call" | custom-call | bytes 3211264 | tf_op jit(solution)/shard_map/pallas_call | solution.py:531
  51.8 0.6 collective-permute-done.12.ac_odd
  52.4 2.5 %shard_map.231 = (f32[224,128]{1,0:T(8,128)S(1)}, f32[8,128]{1,0:T(8,128)S(1)}, f32[8,128]{1,0:T(8,128)S(1)}, f32[2,2,128]{2,1,0:T(2,128)}, f32[2,2,128]{2,1,0:T(2,128)}) custom-call(s32[2,3]{1,0:T(2,128)S(1)} %copy-done.1, s32[2,3]{1,0:T(2,128)S(1)} %collective-permute-done.fam_par, s32[1]{0:T(128)S(6)} %copy.24.live, ...), custom_call_target="tpu_custom_call" | custom-call | bytes 3682304 | tf_op jit(solution)/shard_map/pallas_call | solution.py:531
  54.9 1.4 %collective-permute-start.14 = (f32[8,128]{1,0:T(8,128)S(1)}, f32[8,128]{1,0:T(8,128)S(1)}, u32[]{:S(2)}, u32[]{:S(2)}) collective-permute-start(f32[8,128]{1,0:T(8,128)S(1)} %get-tuple-element.60), channel_id=1, source_target_pairs={{0,2},{1,3},{2,0},{3,1},{4,6},{5,7},{6,4},{7,5},{8,10},{9,11},{10,... | collective-permute-start | bytes 12296 | tf_op jit(solution)/shard_map/ppermute | solution.py:575
  56.3 2.0 %collective-permute-start.15 = (f32[8,128]{1,0:T(8,128)S(1)}, f32[8,128]{1,0:T(8,128)S(1)}, u32[]{:S(2)}, u32[]{:S(2)}) collective-permute-start(f32[8,128]{1,0:T(8,128)S(1)} %get-tuple-element.61), channel_id=1, source_target_pairs={{0,1},{1,0},{2,4},{3,5},{4,2},{5,3},{6,8},{7,9},{8,6},{9,7},{10,12... | collective-permute-start | bytes 12296 | tf_op jit(solution)/shard_map/ppermute | solution.py:576
  58.5 3.2 %collective-permute-done.15.from_odd = f32[8,128]{1,0:T(8,128)S(1)} collective-permute-done((f32[8,128]{1,0:T(8,128)S(1)}, f32[8,128]{1,0:T(8,128)S(1)}, u32[]{:S(2)}, u32[]{:S(2)}) %collective-permute-start.15) | collective-permute-done | bytes 4128 | tf_op jit(solution)/shard_map/ppermute | solution.py:576
  61.7 1.0 %shard_map.232 = (f32[2,6400]{1,0:T(2,128)}, f32[2,6400]{1,0:T(2,128)}) custom-call(f32[224,128]{1,0:T(8,128)S(1)} %get-tuple-element.58.nodal, f32[224,128]{1,0:T(8,128)S(1)} %get-tuple-element.55.table, f32[224,128]{1,0:T(8,128)S(1)} %get-tuple-element.59.vel, f32[112,128]{1,0:T(8,128)S(1)} %get-tuple-element.48.step, ...), custom_call_target="tpu_custom_call" | custom-call | bytes 513024 | tf_op jit(solution)/shard_map/pallas_call | solution.py:531
  (18 shorter events, 1.7 us)
Async XLA Ops:
  2.7 1.9 %collective-permute-start.1 = (f32[632,128]{1,0:T(8,128)}, f32[632,128]{1,0:T(8,128)S(1)}, u32[]{:S(2)}, u32[]{:S(2)}) collective-permute-start(f32[632,128]{1,0:T(8,128)} %shard_map.219.own), channel_id=1, source_target_pairs={{0,1},{1,0},{2,3},{3,2},{4,5},{5,4},{6,7},{7,6},{8,9},{9,8},{10,11... | collective-permute-start | bytes 970760 | tf_op jit(solution)/shard_map/ppermute | solution.py:561
  4.6 1.0 %copy-start = (f32[632,128]{1,0:T(8,128)S(1)}, f32[632,128]{1,0:T(8,128)}, u32[]{:S(2)}) copy-start(f32[632,128]{1,0:T(8,128)} %shard_map.219.own) | copy-start | bytes 970756
  6.1 7.4 %copy-start.1 = (s32[2,3]{1,0:T(2,128)S(1)}, s32[2,3]{1,0:T(2,128)}, u32[]{:S(2)}) copy-start(s32[2,3]{1,0:T(2,128)} %fam_own.11) | copy-start | bytes 76
  10.3 14.2 %collective-permute-start.6 = (f32[224,128]{1,0:T(8,128)S(1)}, f32[224,128]{1,0:T(8,128)S(1)}, u32[]{:S(2)}, u32[]{:S(2)}) collective-permute-start(f32[224,128]{1,0:T(8,128)S(1)} %shard_map.224.el_own), channel_id=1, source_target_pairs={{0,1},{1,0},{2,3},{3,2},{4,5},{5,4},{6,7},{7,6},{8,9},{9,8},{10,11... | collective-permute-start | bytes 344072 | tf_op jit(solution)/shard_map/ppermute | solution.py:561
  10.5 5.5 %collective-permute-start.3 = (f32[4,8,128]{2,1,0:T(8,128)S(1)}, f32[4,8,128]{2,1,0:T(8,128)S(1)}, u32[]{:S(2)}, u32[]{:S(2)}) collective-permute-start(f32[4,8,128]{2,1,0:T(8,128)S(1)} %get-tuple-element.34.own.pack), channel_id=1, source_target_pairs={{0,1},{1,0},{2,4},{3,5},{4,2},{5,3},{6,8},{7,9},{8,6},{9,7},{10,12... | collective-permute-start | bytes 49160 | tf_op jit(solution)/shard_map/ppermute | solution.py:576
  12.8 3.7 %collective-permute-start.2 = (f32[4,8,128]{2,1,0:T(8,128)S(1)}, f32[4,8,128]{2,1,0:T(8,128)S(1)}, u32[]{:S(2)}, u32[]{:S(2)}) collective-permute-start(f32[4,8,128]{2,1,0:T(8,128)S(1)} %get-tuple-element.34.own.pack), channel_id=1, source_target_pairs={{0,2},{1,3},{2,0},{3,1},{4,6},{5,7},{6,4},{7,5},{8,10},{9,11},{10,... | collective-permute-start | bytes 49160 | tf_op jit(solution)/shard_map/ppermute | solution.py:575
  13.5 1.2 %collective-permute-start = (s32[2,3]{1,0:T(2,128)S(1)}, s32[2,3]{1,0:T(2,128)S(1)}, u32[]{:S(2)}, u32[]{:S(2)}) collective-permute-start(s32[2,3]{1,0:T(2,128)S(1)} %copy-done.1), channel_id=1, source_target_pairs={{0,1},{1,0},{2,3},{3,2},{4,5},{5,4},{6,7},{7,6},{8,9},{9,8},{10,11... | collective-permute-start | bytes 80 | tf_op jit(solution)/shard_map/ppermute | solution.py:561
  19.0 5.5 %collective-permute-start.5 = (f32[8,128]{1,0:T(8,128)S(1)}, f32[8,128]{1,0:T(8,128)S(1)}, u32[]{:S(2)}, u32[]{:S(2)}) collective-permute-start(f32[8,128]{1,0:T(8,128)S(1)} %shard_map.221.ac), channel_id=1, source_target_pairs={{0,1},{1,0},{2,4},{3,5},{4,2},{5,3},{6,8},{7,9},{8,6},{9,7},{10,12... | collective-permute-start | bytes 12296 | tf_op jit(solution)/shard_map/ppermute | solution.py:576
  20.9 3.6 %collective-permute-start.4 = (f32[8,128]{1,0:T(8,128)S(1)}, f32[8,128]{1,0:T(8,128)S(1)}, u32[]{:S(2)}, u32[]{:S(2)}) collective-permute-start(f32[8,128]{1,0:T(8,128)S(1)} %shard_map.221.ac), channel_id=1, source_target_pairs={{0,2},{1,3},{2,0},{3,1},{4,6},{5,7},{6,4},{7,5},{8,10},{9,11},{10,... | collective-permute-start | bytes 12296 | tf_op jit(solution)/shard_map/ppermute | solution.py:575
  26.6 3.7 %collective-permute-start.7 = (f32[8,128]{1,0:T(8,128)S(1)}, f32[8,128]{1,0:T(8,128)S(1)}, u32[]{:S(2)}, u32[]{:S(2)}) collective-permute-start(f32[8,128]{1,0:T(8,128)S(1)} %get-tuple-element.49), channel_id=1, source_target_pairs={{0,2},{1,3},{2,0},{3,1},{4,6},{5,7},{6,4},{7,5},{8,10},{9,11},{10,... | collective-permute-start | bytes 12296 | tf_op jit(solution)/shard_map/ppermute | solution.py:575
  28.1 5.4 %collective-permute-start.8 = (f32[8,128]{1,0:T(8,128)S(1)}, f32[8,128]{1,0:T(8,128)S(1)}, u32[]{:S(2)}, u32[]{:S(2)}) collective-permute-start(f32[8,128]{1,0:T(8,128)S(1)} %get-tuple-element.50), channel_id=1, source_target_pairs={{0,1},{1,0},{2,4},{3,5},{4,2},{5,3},{6,8},{7,9},{8,6},{9,7},{10,12... | collective-permute-start | bytes 12296 | tf_op jit(solution)/shard_map/ppermute | solution.py:576
  38.6 13.8 %collective-permute-start.13 = (f32[224,128]{1,0:T(8,128)S(1)}, f32[224,128]{1,0:T(8,128)S(1)}, u32[]{:S(2)}, u32[]{:S(2)}) collective-permute-start(f32[224,128]{1,0:T(8,128)S(1)} %shard_map.230.el_own), channel_id=1, source_target_pairs={{0,1},{1,0},{2,3},{3,2},{4,5},{5,4},{6,7},{7,6},{8,9},{9,8},{10,11... | collective-permute-start | bytes 344072 | tf_op jit(solution)/shard_map/ppermute | solution.py:561
  38.6 5.6 %collective-permute-start.10 = (f32[4,8,128]{2,1,0:T(8,128)S(1)}, f32[4,8,128]{2,1,0:T(8,128)S(1)}, u32[]{:S(2)}, u32[]{:S(2)}) collective-permute-start(f32[4,8,128]{2,1,0:T(8,128)S(1)} %get-tuple-element.52.own.pack), channel_id=1, source_target_pairs={{0,1},{1,0},{2,4},{3,5},{4,2},{5,3},{6,8},{7,9},{8,6},{9,7},{10,12... | collective-permute-start | bytes 49160 | tf_op jit(solution)/shard_map/ppermute | solution.py:576
  40.7 3.7 %collective-permute-start.9 = (f32[4,8,128]{2,1,0:T(8,128)S(1)}, f32[4,8,128]{2,1,0:T(8,128)S(1)}, u32[]{:S(2)}, u32[]{:S(2)}) collective-permute-start(f32[4,8,128]{2,1,0:T(8,128)S(1)} %get-tuple-element.52.own.pack), channel_id=1, source_target_pairs={{0,2},{1,3},{2,0},{3,1},{4,6},{5,7},{6,4},{7,5},{8,10},{9,11},{10,... | collective-permute-start | bytes 49160 | tf_op jit(solution)/shard_map/ppermute | solution.py:575
  46.9 5.5 %collective-permute-start.12 = (f32[8,128]{1,0:T(8,128)S(1)}, f32[8,128]{1,0:T(8,128)S(1)}, u32[]{:S(2)}, u32[]{:S(2)}) collective-permute-start(f32[8,128]{1,0:T(8,128)S(1)} %shard_map.227.ac), channel_id=1, source_target_pairs={{0,1},{1,0},{2,4},{3,5},{4,2},{5,3},{6,8},{7,9},{8,6},{9,7},{10,12... | collective-permute-start | bytes 12296 | tf_op jit(solution)/shard_map/ppermute | solution.py:576
  48.8 3.6 %collective-permute-start.11 = (f32[8,128]{1,0:T(8,128)S(1)}, f32[8,128]{1,0:T(8,128)S(1)}, u32[]{:S(2)}, u32[]{:S(2)}) collective-permute-start(f32[8,128]{1,0:T(8,128)S(1)} %shard_map.227.ac), channel_id=1, source_target_pairs={{0,2},{1,3},{2,0},{3,1},{4,6},{5,7},{6,4},{7,5},{8,10},{9,11},{10,... | collective-permute-start | bytes 12296 | tf_op jit(solution)/shard_map/ppermute | solution.py:575
  54.9 3.6 %collective-permute-start.14 = (f32[8,128]{1,0:T(8,128)S(1)}, f32[8,128]{1,0:T(8,128)S(1)}, u32[]{:S(2)}, u32[]{:S(2)}) collective-permute-start(f32[8,128]{1,0:T(8,128)S(1)} %get-tuple-element.60), channel_id=1, source_target_pairs={{0,2},{1,3},{2,0},{3,1},{4,6},{5,7},{6,4},{7,5},{8,10},{9,11},{10,... | collective-permute-start | bytes 12296 | tf_op jit(solution)/shard_map/ppermute | solution.py:575
  56.3 5.4 %collective-permute-start.15 = (f32[8,128]{1,0:T(8,128)S(1)}, f32[8,128]{1,0:T(8,128)S(1)}, u32[]{:S(2)}, u32[]{:S(2)}) collective-permute-start(f32[8,128]{1,0:T(8,128)S(1)} %get-tuple-element.61), channel_id=1, source_target_pairs={{0,1},{1,0},{2,4},{3,5},{4,2},{5,3},{6,8},{7,9},{8,6},{9,7},{10,12... | collective-permute-start | bytes 12296 | tf_op jit(solution)/shard_map/ppermute | solution.py:576
